TPU v7x, 32 devices: a whole 2x2x4 slice. The times are simulated.
32 devices in a mesh: cfg: 2 (over x), ta: 2 (over core), sa: 8 (over z, y).
Axes of the slice: x: 2, y: 2, z: 4, core: 2. Of those that a mesh axis runs over, the one named last changes fastest.
Arguments:
- links: float32 [4, 3, 2, 3, 3, 32, 1024], P(None, None, None, None, None, 'sa', 'ta'), may hold values from -2.5 to 2.5
- vectors: float32 [4, 16, 2, 3, 32, 1024], P('ta', None, None, None, 'sa'), may hold values from -6 to 6
Outputs:
- filtered: float32 [8, 16, 2, 3, 32, 1024], P(('cfg', 'ta'), None, None, None, 'sa'), parts along dimension 0
- grams: float32 [8, 2, 2, 16, 16], P(('cfg', 'ta')), parts along dimension 0
There are 2 independent parts, one for each index of `cfg`. A program takes and returns all parts, laid end to end along the dimension named above; an argument that names none is the same for every part. Nothing has to cross between parts.
All inputs are finite; a program needn't handle non-finite values.
Results may differ from a plain program's by a relative error of at most 0.00011.
Values sent between devices are 32-bit elements; how exact they have to be, the bound alone decides.
No kernel may reach another device: no remote copies, remote signals or barrier semaphores. Data moves between devices by JAX's collectives and lax.ppermute only.
A program may use at most 256 MiB of HBM per device.

v0:
```python
import functools

import jax
import jax.numpy as jnp
from jax import lax
from jax.experimental import pallas as pl
from jax.experimental.pallas import tpu as pltpu
from jax.sharding import PartitionSpec as P


LX = 32
LANES = 128
SCALE = 5.5
F32 = jnp.float32
BF16 = jnp.bfloat16
VMEM = pl.BlockSpec(memory_space=pltpu.VMEM)
GRANT = 16 * 2**20


def shape_of(*dims, dtype=F32):
    return jax.ShapeDtypeStruct(dims, dtype)


def call(kernel, outs, *args, ops=1e6, scratch=(), pick=None, whole=None, grid=1):
    size = sum(a.size * 4 for a in args) + sum(4 * o.size for o in jax.tree.leaves(outs))
    several = isinstance(outs, (list, tuple))
    params = dict(
        out_shape=outs,
        compiler_params=pltpu.CompilerParams(vmem_limit_bytes=GRANT),
        cost_estimate=pl.CostEstimate(flops=int(ops), bytes_accessed=int(size), transcendentals=0),
    )
    if pick is None:
        specs = [VMEM] * len(outs) if several else VMEM
        return pl.pallas_call(
            kernel, in_specs=[VMEM] * len(args), out_specs=specs, scratch_shapes=scratch, **params
        )(*args)
    specs = [pl.BlockSpec(*whole[k]) if k in whole else VMEM for k in range(len(args) + len(outs))]
    spec = pltpu.PrefetchScalarGridSpec(
        num_scalar_prefetch=1, grid=(grid,), in_specs=specs[: len(args)], out_specs=specs[len(args) :],
        scratch_shapes=scratch,
    )
    return pl.pallas_call(kernel, grid_spec=spec, **params)(pick, *args)


def to_rows(x):
    depth, plane = x.shape[-2:]
    x = x.reshape(-1, depth, plane // LANES, LANES)
    return jnp.swapaxes(x, 1, 2).reshape(-1, LANES)


def from_rows(x, shape):
    depth, plane = shape[-2:]
    x = x.reshape(-1, plane // LANES, depth, LANES)
    return jnp.swapaxes(x, 1, 2).reshape(shape)


def pieces_of(depth):
    if depth == 1:
        return [[0]]
    if depth == 2:
        return [[0], [1]]
    return [[0], list(range(1, depth - 1)), [depth - 1]]


def plane_refs(refs, pieces):
    return {z: ref.at[k] for ref, planes in zip(refs, pieces) for k, z in enumerate(planes)}


def lane_index(shape):
    return lax.broadcasted_iota(jnp.int32, shape, len(shape) - 1)


def ahead_x(v, lane):
    wrap = (lane % LX) == LX - 1
    return jnp.where(wrap, pltpu.roll(v, LX - 1, v.ndim - 1), pltpu.roll(v, LANES - 1, v.ndim - 1))


def behind_x(v, lane):
    wrap = (lane % LX) == 0
    return jnp.where(wrap, pltpu.roll(v, LANES - LX + 1, v.ndim - 1), pltpu.roll(v, 1, v.ndim - 1))


def ahead_y(here, after, lane):
    ax = here.ndim - 1
    return jnp.where(lane < LANES - LX, pltpu.roll(here, LANES - LX, ax), pltpu.roll(after, LANES - LX, ax))


def behind_y(here, before, lane):
    ax = here.ndim - 1
    return jnp.where(lane < LX, pltpu.roll(before, LX, ax), pltpu.roll(here, LX, ax))


def split_kernel(depth, rows, vecs, pieces, _, v_ref, *out_refs):
    out = plane_refs(out_refs[: len(pieces)], pieces)
    stride = 6 * rows * depth

    def body(c, _):
        for z in out:
            for q in range(6):
                out[z][c, q] = v_ref[pl.ds(q * rows * depth + c * depth + z, vecs, stride=stride), :]
        return 0

    lax.fori_loop(0, rows, body, 0)
    if len(out_refs) > len(pieces):
        out_refs[-1][...] = v_ref[0:8, :]


def link_kernel(depth, half, pick_ref, kept_ref, came_ref, out_ref, top_ref):
    rows = 2 * half
    core = pick_ref[1]

    def body(c, _):
        for ref, first in ((kept_ref, core * half), (came_ref, (1 - core) * half)):
            for z in range(depth):
                out_ref[z, first + c, 0:54, :] = ref[pl.ds(c * depth + z, 54, stride=half * depth), :]
        return 0

    lax.fori_loop(0, half, body, 0)
    lane = lane_index((18, LANES))

    def shift(c, _):
        before = lax.rem(c + rows - 1, rows)
        for z in range(depth):
            out_ref[z, c, 54:72, :] = behind_x(out_ref[z, c, 0:18, :], lane)
            out_ref[z, c, 72:90, :] = behind_y(out_ref[z, c, 18:36, :], out_ref[z, before, 18:36, :], lane)
        top_ref[c, 0:18, :] = out_ref[depth - 1, c, 36:54, :]
        return 0

    lax.fori_loop(0, rows, shift, 0)


def multiply_into(total, field, link, adjoint):
    for col in range(3):
        re, im = field(col), field(3 + col)
        for row in range(3):
            entry = col * 3 + row if adjoint else row * 3 + col
            a, b = link(entry), link(9 + entry)
            if adjoint:
                total[row] = total[row] + a * re + b * im
                total[3 + row] = total[3 + row] + a * im - b * re
            else:
                total[row] = total[row] + a * re - b * im
                total[3 + row] = total[3 + row] + a * im + b * re


def link_rows(ref, c, first, vecs):
    def link(k):
        return jnp.broadcast_to(ref[c, first + k : first + k + 1, :], (vecs, LANES))

    return link


def forward_hops(total, cur, up, links, c, rows, lane):
    vecs = lane.shape[0]
    after = lax.rem(c + 1, rows)
    multiply_into(total, lambda q: ahead_x(cur[c, q], lane), link_rows(links, c, 0, vecs), False)
    multiply_into(total, lambda q: ahead_y(cur[c, q], cur[after, q], lane), link_rows(links, c, 18, vecs), False)
    if up is not None:
        multiply_into(total, lambda q: up[c, q], link_rows(links, c, 36, vecs), False)


def backward_hops(total, cur, down, links, down_links, c, rows, lane):
    vecs = lane.shape[0]
    before = lax.rem(c + rows - 1, rows)
    multiply_into(total, lambda q: behind_x(cur[c, q], lane), link_rows(links, c, 54, vecs), True)
    multiply_into(total, lambda q: behind_y(cur[c, q], cur[before, q], lane), link_rows(links, c, 72, vecs), True)
    if down is not None:
        multiply_into(total, lambda q: down[c, q], link_rows(down_links, c, 36, vecs), True)


def part_kernel(pieces, todo, factor, first, links_ref, *refs):
    refs = list(refs)
    cur = plane_refs([refs.pop(0) for _ in pieces], pieces)
    done = [pieces[k] for k in todo]
    old = None if first else plane_refs([refs.pop(0) for _ in todo], done)
    out = plane_refs(refs, done)
    rows, _, vecs, _ = cur[0].shape
    lane = lane_index((vecs, LANES))
    for z in out:

        def body(c, _, z=z):
            total = [cur[z][c, q] for q in range(6)]
            links = links_ref.at[z]
            forward_hops(total, cur[z], cur.get(z + 1), links, c, rows, lane)
            below = links_ref.at[z - 1] if z else None
            backward_hops(total, cur[z], cur.get(z - 1), links, below, c, rows, lane)
            for q in range(6):
                value = total[q] * factor
                out[z][c, q] = value if first else value - old[z][c, q]
            return 0

        lax.fori_loop(0, rows, body, 0)


def close_kernel(factor, behind, *refs):
    part_ref, out_ref = refs[-2].at[0], refs[-1].at[0]
    rows, _, vecs, _ = out_ref.shape

    def body(c, _):
        total = [jnp.zeros((vecs, LANES), F32) for _ in range(6)]
        for k, back in enumerate(behind):
            links_ref, halo_ref = refs[2 * k : 2 * k + 2]
            multiply_into(total, lambda q: halo_ref[0, c, q], link_rows(links_ref, c, 0, vecs), back)
        for q in range(6):
            out_ref[c, q] = part_ref[c, q] + total[q] * factor
        return 0

    lax.fori_loop(0, rows, body, 0)


def halves(x):
    high = x.astype(BF16)
    return high, (x - high.astype(F32)).astype(BF16)


def high_low(tiles):
    pairs = [halves(jnp.concatenate(tiles[k : k + 3], axis=1)) for k in (0, 3)]
    return [pairs[0][0], pairs[1][0], pairs[0][1], pairs[1][1]]


def products(acc_ref, rows, own, sides):
    def body(pair, _):
        stacks = [[], []]
        for c in (2 * pair, 2 * pair + 1):
            for stack, tiles in zip(stacks, sides(c)):
                stack.append(jnp.concatenate(high_low(tiles), axis=0))
        left, right = [jnp.concatenate(s, axis=1) for s in stacks]
        right = jnp.concatenate([left if own else jnp.zeros_like(left), right], axis=0)
        acc_ref[...] += lax.dot_general(left, right, (((1,), (1,)), ((), ())), preferred_element_type=F32)
        return 0

    lax.fori_loop(0, rows // 2, body, 0)


def packed_product(acc, n):
    acc = acc[0 : 2 * n] + acc[2 * n : 4 * n]
    acc = acc + pltpu.roll(acc, LANES - 2 * n, 1)
    re, im = acc[0:n], acc[n : 2 * n]
    real = re + pltpu.roll(im, LANES - n, 1)
    imag = re - pltpu.roll(im, n, 1)
    return jnp.where(lane_index((n, LANES)) % (2 * n) < n, real, imag)


def gram_kernel(pieces, tasks, more, links_ref, *refs):
    refs = list(refs)
    acc_ref, out_ref = refs.pop(), refs.pop()
    sofar_ref = refs.pop() if more else None
    cur = plane_refs(refs, pieces)
    rows, _, vecs, _ = out_shape_of(cur)
    lane = lane_index((vecs, LANES))
    acc_ref[...] = jnp.zeros_like(acc_ref)
    for z, own, depth_hop in tasks:

        def sides(c, z=z, own=own, depth_hop=depth_hop):
            total = [jnp.zeros((vecs, LANES), F32) for _ in range(6)]
            links = links_ref.at[z]
            if own:
                forward_hops(total, cur[z], cur[z + 1] if depth_hop else None, links, c, rows, lane)
            else:
                multiply_into(total, lambda q: cur[z + 1][c, q], link_rows(links, c, 36, vecs), False)
            return [cur[z][c, q] for q in range(6)], total

        products(acc_ref, rows, own, sides)
    part = packed_product(acc_ref[...], vecs)
    out_ref[...] = part + sofar_ref[...] if more else part


def out_shape_of(planes):
    return next(iter(planes.values())).shape


def last_hop_kernel(links_ref, top_ref, above_ref, sofar_ref, out_ref, acc_ref):
    rows, _, vecs, _ = top_ref.shape[1:]
    acc_ref[...] = jnp.zeros_like(acc_ref)

    def sides(c):
        total = [jnp.zeros((vecs, LANES), F32) for _ in range(6)]
        multiply_into(total, lambda q: above_ref[0, c, q], link_rows(links_ref, c, 0, vecs), False)
        return [top_ref[0, c, q] for q in range(6)], total

    products(acc_ref, rows, False, sides)
    out_ref[...] = packed_product(acc_ref[...], vecs) + sofar_ref[...]


def norms_of(packed):
    n = packed.shape[0]
    diag = lane_index((n, LANES)) == lax.broadcasted_iota(jnp.int32, (n, LANES), 0)
    return jnp.where(diag, packed, 0.0)


def scatter_kernel(depth, pieces, *refs):
    out_ref = refs[-1]
    planes = plane_refs(refs[:-1], pieces)
    rows, _, vecs, _ = planes[0].shape
    stride = 6 * rows * depth

    def body(c, _):
        for z in range(depth):
            for q in range(6):
                start = q * rows * depth + c * depth + z
                out_ref[pl.ds(start, vecs, stride=stride), :] = planes[z][c, q]
        return 0

    lax.fori_loop(0, rows, body, 0)


def final_kernel(slot_ref, *refs):
    out_ref, grams_ref, scale_ref = refs[-3:]
    for k in range(2):
        term0, term1, field_ref = refs[3 * k : 3 * k + 3]
        n = term0.shape[0]

        @pl.when(pl.program_id(0) == k)
        def _(k=k, term0=term0, term1=term1, field_ref=field_ref):
            slot = slot_ref[0] if k == 0 else 1 - slot_ref[0]
            packed = term0[...] + term1[...]
            norm = norms_of(packed)
            down = lax.rsqrt(jnp.sum(norm, axis=1, keepdims=True))
            across = lax.rsqrt(jnp.sum(norm, axis=0, keepdims=True)[:, 0:n])
            scale = down * across
            over_re, over_im = packed[:, 0:n], packed[:, n : 2 * n]
            hop_re, hop_im = packed[:, 4 * n : 5 * n], packed[:, 5 * n : 6 * n]
            grams_ref[slot, 0, 0] = over_re * scale
            grams_ref[slot, 0, 1] = over_im * scale
            grams_ref[slot, 1, 0] = (6.0 * over_re - (hop_re + hop_re.T)) * scale
            grams_ref[slot, 1, 1] = (6.0 * over_im - (hop_im - hop_im.T)) * scale
            scale_ref[...] = jnp.broadcast_to(down, (n, LANES))
            size = out_ref.shape[0] // n

            def body(i, _):
                block = pl.ds(pl.multiple_of(i * size, 8), size)
                out_ref[block, :] = field_ref[block, :] * scale_ref[pl.ds(i, 1), :]
                return 0

            lax.fori_loop(0, n, body, 0)


def shifted(x, axis, by):
    n = lax.axis_size(axis)
    return lax.ppermute(x, axis, [(i, (i + by) % n) for i in range(n)])


def flipped(x, axis, bit):
    return lax.ppermute(x, axis, [(i, i ^ bit) for i in range(lax.axis_size(axis))])


def summed(x):
    size = lax.axis_size("sa")
    count = size.bit_length() - 1
    assert size == 1 << count

    def across(x, cfg, bits):
        pairs = range(lax.axis_size("cfg") * size)
        return lax.ppermute(x, ("cfg", "sa"), [(i, i ^ (cfg * size + bits)) for i in pairs])

    bit = 1
    for _ in range((count - 1) // 2):
        x = x + flipped(x, "sa", bit) + flipped(x, "sa", 2 * bit) + flipped(x, "sa", 3 * bit)
        bit *= 4
    if count % 2 == 0:
        x = x + flipped(x, "sa", bit)
        bit *= 2
    return (x, flipped(x, "sa", bit)), (across(x, 1, 0), across(x, 1, bit))


def on_device(links, vectors):
    slices, vecs, _, _, depth, plane = vectors.shape
    rows = plane // LANES
    assert slices == 2 and lax.axis_size("cfg") % 2 == 0 and lax.axis_size("ta") == 2
    pieces = pieces_of(depth)
    ends = [0] if len(pieces) == 1 else [0, len(pieces) - 1]
    inner = [k for k in range(len(pieces)) if k not in ends]
    core = lax.axis_index("ta")
    mine = lax.axis_index("cfg") % 2
    pick = jnp.stack([mine, core, 2 * core + mine]).astype(jnp.int32)
    field = [shape_of(len(p), rows, 6, vecs, LANES) for p in pieces]
    work = 1000 * LANES * vecs * rows
    many = vecs * 6 * rows * depth
    mine_block = ((many, LANES), lambda step, pick: (pick[0], 0))

    view = to_rows(vectors)

    def split(todo, token):
        return call(
            functools.partial(split_kernel, depth, rows, vecs, [pieces[k] for k in todo]),
            [field[k] for k in todo] + token, view, pick=pick, whole={0: mine_block}, ops=1e5,
        )

    start = [None] * len(pieces)
    *got, token = split(ends, [shape_of(8, LANES)])
    for k, x in zip(ends, got):
        start[k] = x
    links, view, _ = lax.optimization_barrier((links, view, token))

    flat = links.reshape((links.shape[0], 54) + links.shape[-2:])
    given = lax.dynamic_index_in_dim(flat, 2 * (1 - core) + mine, 0, keepdims=False)
    came = flipped(given, "ta", 1)
    if inner:
        for k, x in zip(inner, split(inner, [])):
            start[k] = x
    block = ((54 * (rows // 2) * depth, LANES), lambda step, pick: (pick[2], 0))
    table, top_links = call(
        functools.partial(link_kernel, depth, rows // 2),
        [shape_of(depth, rows, 90, LANES), shape_of(rows, 18, LANES)],
        to_rows(links), to_rows(came), pick=pick, whole={0: block}, ops=1e6,
    )
    prior = shifted(top_links, "sa", 1)

    def advance(cur, old):
        factor = -(1.0 if old is None else 2.0) / SCALE
        low = shifted(cur[-1], "sa", 1)
        high = shifted(cur[0], "sa", -1)
        new = [None] * len(pieces)
        for todo in (inner, ends):
            if todo:
                got = call(
                    functools.partial(part_kernel, pieces, todo, factor, old is None),
                    [field[k] for k in todo], table, *cur, *([] if old is None else [old[k] for k in todo]),
                    ops=work * sum(len(pieces[k]) for k in todo),
                )
                for k, x in zip(todo, got):
                    new[k] = x
        sides = [(0, True, prior, low), (len(pieces) - 1, False, top_links, high)]
        for k in ends:
            used = [side for side in sides if side[0] == k]
            operands = [x for side in used for x in side[2:]]
            (new[k],) = call(
                functools.partial(close_kernel, factor, [side[1] for side in used]),
                [field[k]], *operands, new[k], ops=work / 6,
            )
        return new

    packed = shape_of(vecs, LANES)
    acc = [pltpu.VMEM((4 * vecs, 8 * vecs), F32)]

    def swapped(x):
        return flipped(x, "cfg", 1)

    def grams_of(planes, tasks, sofar):
        return call(
            functools.partial(gram_kernel, [pieces[k] for k in planes], tasks, sofar is not None),
            packed, table, *[three[k] for k in planes], *([] if sofar is None else [sofar]),
            scratch=acc, ops=work * len(tasks) / 2,
        )

    one = advance(start, None)
    two = advance(one, start)
    three = advance(two, one)

    sofar = None
    if inner:
        middle = pieces[1]
        sofar = grams_of(inner, [(z, True, z + 1 in middle) for z in middle], None)
    above = shifted(three[0], "sa", -1)
    tasks = [(z, True, z + 1 < depth) for z in sorted({0, depth - 1})]
    if inner:
        tasks.append((depth - 2, False, True))
    sofar = grams_of(range(len(pieces)), tasks, sofar)
    sofar = call(
        last_hop_kernel, packed, top_links, three[-1], above, sofar,
        scratch=acc, ops=work / 4,
    )
    sum_mine, sum_other = summed(sofar)
    other = [swapped(x) for x in three]

    def scattered(planes):
        return call(functools.partial(scatter_kernel, depth, pieces), shape_of(many, LANES), *planes, ops=1e6)

    place = ((many, LANES), lambda step, pick: (jnp.where(step == 0, pick[0], 1 - pick[0]), 0))
    given = [*sum_mine, scattered(three), *sum_other, scattered(other)]
    out, grams = call(
        final_kernel, [shape_of(2 * many, LANES), shape_of(2, 2, 2, vecs, vecs)], *given,
        pick=pick, whole={len(given): place}, grid=2, ops=1e6, scratch=[pltpu.VMEM((vecs, LANES), F32)],
    )
    return from_rows(out, vectors.shape), grams


def solution(mesh):
    in_specs = (P(None, None, None, None, None, "sa", "ta"), P("ta", None, None, None, "sa", None))
    out_specs = (
        P(("cfg", "ta"), None, None, None, "sa", None),
        P(("cfg", "ta"), None, None, None, None),
    )
    return jax.shard_map(on_device, mesh=mesh, in_specs=in_specs, out_specs=out_specs, check_vma=False)
```

profile of v0, /device:TPU:0, one launch (start us, length us, event | category | flops | bytes accessed | tf_op | source)
XLA Modules:
  0.0 99.8 jit_solution(1129054599883595490)
XLA Ops:
  0.6 1.0 %dynamic-slice_bitcast_fusion = f32[54,4,512]{2,1,0:T(4,128)S(1)} fusion(f32[4,54,4,512]{3,2,1,0:T(4,128)} %bitcast.28, s32[]{:T(128)S(6)} %select_n.12), kind=kLoop, calls=%fused_computation | loop fusion | bytes 884740 | tf_op jit(solution)/shard_map/jit(dynamic_index_in_dim)/squeeze | solution.py:396
  2.3 1.9 %copy-done = f32[2,16,2,3,4,1024]{5,4,3,2,1,0:T(4,128)S(1)} copy-done((f32[2,16,2,3,4,1024]{5,4,3,2,1,0:T(4,128)S(1)}, f32[2,16,2,3,4,1024]{5,4,3,2,1,0:T(4,128)}, u32[]{:S(2)}) %copy-start) | copy-done | bytes 3145752
  4.2 1.8 %shard_map.42 = (f32[1,8,6,16,128]{4,3,2,1,0:T(8,128)S(1)}, f32[1,8,6,16,128]{4,3,2,1,0:T(8,128)S(1)}, f32[8,128]{1,0:T(8,128)}) custom-call(s32[3]{0:T(128)S(1)} %pad_add_fusion.pick_ref._.slot_ref, f32[6144,128]{1,0:T(8,128)S(1)} %bitcast.26), custom_call_target="tpu_custom_call" | custom-call | flops 100000 | bytes 3936256 | tf_op jit(solution)/shard_map/pallas_call | solution.py:42
  6.1 2.5 %collective-permute-start.4 = (f32[1,8,6,16,128]{4,3,2,1,0:T(8,128)S(1)}, f32[1,8,6,16,128]{4,3,2,1,0:T(8,128)S(1)}, u32[]{:S(2)}, u32[]{:S(2)}) collective-permute-start(f32[1,8,6,16,128]{4,3,2,1,0:T(8,128)S(1)} %get-tuple-element.21.refs_2_.refs_4_), channel_id=1, source_target_pairs={{0,1},{1,2},{2,3},{3,4},{4,5},{5,6},{6,7},{7,0},{8,9},{9,10},{10,1... | collective-permute-start | bytes 1179656 | tf_op jit(solution)/shard_map/ppermute | solution.py:340
  8.6 3.0 %collective-permute-start.2 = (f32[1,8,6,16,128]{4,3,2,1,0:T(8,128)S(1)}, f32[1,8,6,16,128]{4,3,2,1,0:T(8,128)S(1)}, u32[]{:S(2)}, u32[]{:S(2)}) collective-permute-start(f32[1,8,6,16,128]{4,3,2,1,0:T(8,128)S(1)} %get-tuple-element.18.refs_0_.refs_3_), channel_id=1, source_target_pairs={{0,7},{1,0},{2,1},{3,2},{4,3},{5,4},{6,5},{7,6},{8,15},{9,8},{10,9... | collective-permute-start | bytes 1179656 | tf_op jit(solution)/shard_map/ppermute | solution.py:340
  11.6 1.5 %copy-done.2 = f32[4,3,2,3,3,4,512]{6,5,4,3,2,1,0:T(4,128)S(1)} copy-done((f32[4,3,2,3,3,4,512]{6,5,4,3,2,1,0:T(4,128)S(1)}, f32[4,3,2,3,3,4,512]{6,5,4,3,2,1,0:T(4,128)}, u32[]{:S(2)}) %copy-start.2) | copy-done | bytes 1769496
  13.1 3.8 %shard_map.41 = (f32[4,8,90,128]{3,2,1,0:T(8,128)S(1)}, f32[8,18,128]{2,1,0:T(8,128)S(1)}) custom-call(s32[3]{0:T(128)S(1)} %pad_add_fusion.pick_ref._.slot_ref, f32[3456,128]{1,0:T(8,128)S(1)} %bitcast.29, f32[864,128]{1,0:T(8,128)S(1)} %bitcast.30), custom_call_target="tpu_custom_call" | custom-call | flops 1000000 | bytes 3760128 | tf_op jit(solution)/shard_map/pallas_call | solution.py:42
  17.0 1.3 %shard_map.43.refs_1_.refs_3_ = f32[2,8,6,16,128]{4,3,2,1,0:T(8,128)S(1)} custom-call(s32[3]{0:T(128)S(1)} %pad_add_fusion.pick_ref._.slot_ref, f32[6144,128]{1,0:T(8,128)S(1)} %bitcast.27), custom_call_target="tpu_custom_call" | custom-call | flops 100000 | bytes 3932160 | tf_op jit(solution)/shard_map/pallas_call | solution.py:42
  18.2 3.0 %shard_map.44 = (f32[1,8,6,16,128]{4,3,2,1,0:T(8,128)S(1)}, f32[1,8,6,16,128]{4,3,2,1,0:T(8,128)S(1)}) custom-call(f32[4,8,90,128]{3,2,1,0:T(8,128)S(1)} %get-tuple-element.19.links_ref, f32[1,8,6,16,128]{4,3,2,1,0:T(8,128)S(1)} %get-tuple-element.18.refs_0_.refs_3_, f32[2,8,6,16,128]{4,3,2,1,0:T(8,128)S(1)} %shard_map.43.refs_1_.refs_3_, ...), custom_call_target="tpu_custom_call" | custom-call | flops 32768000 | bytes 3833856 | tf_op jit(solution)/shard_map/pallas_call | solution.py:34
  21.2 5.3 %collective-permute-done.4.refs_1_ = f32[1,8,6,16,128]{4,3,2,1,0:T(8,128)S(1)} collective-permute-done((f32[1,8,6,16,128]{4,3,2,1,0:T(8,128)S(1)}, f32[1,8,6,16,128]{4,3,2,1,0:T(8,128)S(1)}, u32[]{:S(2)}, u32[]{:S(2)}) %collective-permute-start.4) | collective-permute-done | bytes 393248 | tf_op jit(solution)/shard_map/ppermute | solution.py:340
  26.5 1.6 %collective-permute-done.1.refs_0_ = f32[8,18,128]{2,1,0:T(8,128)S(1)} collective-permute-done((f32[8,18,128]{2,1,0:T(8,128)S(1)}, f32[8,18,128]{2,1,0:T(8,128)S(1)}, u32[]{:S(2)}, u32[]{:S(2)}) %collective-permute-start.1) | collective-permute-done | bytes 73760 | tf_op jit(solution)/shard_map/ppermute | solution.py:340
  28.4 5.6 %collective-permute-start.6 = (f32[1,8,6,16,128]{4,3,2,1,0:T(8,128)S(1)}, f32[1,8,6,16,128]{4,3,2,1,0:T(8,128)S(1)}, u32[]{:S(2)}, u32[]{:S(2)}) collective-permute-start(f32[1,8,6,16,128]{4,3,2,1,0:T(8,128)S(1)} %shard_map.46.refs_0_.refs_3_), channel_id=1, source_target_pairs={{0,7},{1,0},{2,1},{3,2},{4,3},{5,4},{6,5},{7,6},{8,15},{9,8},{10,9... | collective-permute-start | bytes 1179656 | tf_op jit(solution)/shard_map/ppermute | solution.py:340
  34.3 3.2 %shard_map.47.refs_1_.refs_3_ = f32[2,8,6,16,128]{4,3,2,1,0:T(8,128)S(1)} custom-call(f32[4,8,90,128]{3,2,1,0:T(8,128)S(1)} %get-tuple-element.19.links_ref, f32[1,8,6,16,128]{4,3,2,1,0:T(8,128)S(1)} %get-tuple-element.18.refs_0_.refs_3_, f32[2,8,6,16,128]{4,3,2,1,0:T(8,128)S(1)} %shard_map.43.refs_1_.refs_3_, ...), custom_call_target="tpu_custom_call" | custom-call | flops 32768000 | bytes 3833856 | tf_op jit(solution)/shard_map/pallas_call | solution.py:34
  37.4 3.0 %shard_map.48 = (f32[1,8,6,16,128]{4,3,2,1,0:T(8,128)S(1)}, f32[1,8,6,16,128]{4,3,2,1,0:T(8,128)S(1)}) custom-call(f32[4,8,90,128]{3,2,1,0:T(8,128)S(1)} %get-tuple-element.19.links_ref, f32[1,8,6,16,128]{4,3,2,1,0:T(8,128)S(1)} %shard_map.46.refs_0_.refs_3_, f32[2,8,6,16,128]{4,3,2,1,0:T(8,128)S(1)} %shard_map.47.refs_1_.refs_3_, ...), custom_call_target="tpu_custom_call" | custom-call | flops 32768000 | bytes 4620288 | tf_op jit(solution)/shard_map/pallas_call | solution.py:34
  40.4 7.8 %collective-permute-done.6.refs_1_ = f32[1,8,6,16,128]{4,3,2,1,0:T(8,128)S(1)} collective-permute-done((f32[1,8,6,16,128]{4,3,2,1,0:T(8,128)S(1)}, f32[1,8,6,16,128]{4,3,2,1,0:T(8,128)S(1)}, u32[]{:S(2)}, u32[]{:S(2)}) %collective-permute-start.6) | collective-permute-done | bytes 393248 | tf_op jit(solution)/shard_map/ppermute | solution.py:340
  48.8 4.8 %collective-permute-start.5 = (f32[1,8,6,16,128]{4,3,2,1,0:T(8,128)S(1)}, f32[1,8,6,16,128]{4,3,2,1,0:T(8,128)S(1)}, u32[]{:S(2)}, u32[]{:S(2)}) collective-permute-start(f32[1,8,6,16,128]{4,3,2,1,0:T(8,128)S(1)} %shard_map.49.refs_0_), channel_id=1, source_target_pairs={{0,7},{1,0},{2,1},{3,2},{4,3},{5,4},{6,5},{7,6},{8,15},{9,8},{10,9... | collective-permute-start | bytes 1179656 | tf_op jit(solution)/shard_map/ppermute | solution.py:340
  53.6 3.2 %shard_map.50.refs_1_ = f32[2,8,6,16,128]{4,3,2,1,0:T(8,128)S(1)} custom-call(f32[4,8,90,128]{3,2,1,0:T(8,128)S(1)} %get-tuple-element.19.links_ref, f32[1,8,6,16,128]{4,3,2,1,0:T(8,128)S(1)} %shard_map.46.refs_0_.refs_3_, f32[2,8,6,16,128]{4,3,2,1,0:T(8,128)S(1)} %shard_map.47.refs_1_.refs_3_, f32[1,8,6,16,128]{4,3,2,1,0:T(8,128)S(1)} %shard_map.45.refs_2_.refs_4_, ...), custom_call_target="tpu_custom_call" | custom-call | flops 32768000 | bytes 4620288 | tf_op jit(solution)/shard_map/pallas_call | solution.py:34
  56.8 3.2 %shard_map.55.refs_0_.refs_1_ = f32[2,8,6,16,128]{4,3,2,1,0:T(8,128)S(1)} custom-call(f32[4,8,90,128]{3,2,1,0:T(8,128)S(1)} %get-tuple-element.19.links_ref, f32[1,8,6,16,128]{4,3,2,1,0:T(8,128)S(1)} %shard_map.49.refs_0_, f32[2,8,6,16,128]{4,3,2,1,0:T(8,128)S(1)} %shard_map.50.refs_1_, f32[1,8,6,16,128]{4,3,2,1,0:T(8,128)S(1)} %shard_map.51.refs_2_, ...), custom_call_target="tpu_custom_call" | custom-call | flops 32768000 | bytes 4620288 | tf_op jit(solution)/shard_map/pallas_call | solution.py:34
  60.0 1.6 %collective-permute-start.16 = (f32[2,8,6,16,128]{4,3,2,1,0:T(8,128)S(1)}, f32[2,8,6,16,128]{4,3,2,1,0:T(8,128)S(1)}, u32[]{:S(2)}, u32[]{:S(2)}) collective-permute-start(f32[2,8,6,16,128]{4,3,2,1,0:T(8,128)S(1)} %shard_map.55.refs_0_.refs_1_), channel_id=1, source_target_pairs={{0,16},{16,0},{1,17},{17,1},{2,18},{18,2},{3,19},{19,3},{4,20},{20... | collective-permute-start | bytes 2359304 | tf_op jit(solution)/shard_map/ppermute | solution.py:344
  61.6 3.0 %shard_map.52 = (f32[1,8,6,16,128]{4,3,2,1,0:T(8,128)S(1)}, f32[1,8,6,16,128]{4,3,2,1,0:T(8,128)S(1)}) custom-call(f32[4,8,90,128]{3,2,1,0:T(8,128)S(1)} %get-tuple-element.19.links_ref, f32[1,8,6,16,128]{4,3,2,1,0:T(8,128)S(1)} %shard_map.49.refs_0_, f32[2,8,6,16,128]{4,3,2,1,0:T(8,128)S(1)} %shard_map.50.refs_1_, ...), custom_call_target="tpu_custom_call" | custom-call | flops 32768000 | bytes 4620288 | tf_op jit(solution)/shard_map/pallas_call | solution.py:34
  65.5 5.2 %collective-permute-start.8 = (f32[1,8,6,16,128]{4,3,2,1,0:T(8,128)S(1)}, f32[1,8,6,16,128]{4,3,2,1,0:T(8,128)S(1)}, u32[]{:S(2)}, u32[]{:S(2)}) collective-permute-start(f32[1,8,6,16,128]{4,3,2,1,0:T(8,128)S(1)} %shard_map.54.refs_0_), channel_id=1, source_target_pairs={{0,7},{1,0},{2,1},{3,2},{4,3},{5,4},{6,5},{7,6},{8,15},{9,8},{10,9... | collective-permute-start | bytes 1179656 | tf_op jit(solution)/shard_map/ppermute | solution.py:340
  70.9 1.6 %collective-permute-start.17 = (f32[1,8,6,16,128]{4,3,2,1,0:T(8,128)S(1)}, f32[1,8,6,16,128]{4,3,2,1,0:T(8,128)S(1)}, u32[]{:S(2)}, u32[]{:S(2)}) collective-permute-start(f32[1,8,6,16,128]{4,3,2,1,0:T(8,128)S(1)} %shard_map.53.refs_2_.top_ref), channel_id=1, source_target_pairs={{0,16},{16,0},{1,17},{17,1},{2,18},{18,2},{3,19},{19,3},{4,20},{20... | collective-permute-start | bytes 1179656 | tf_op jit(solution)/shard_map/ppermute | solution.py:344
  73.0 3.1 %shard_map.56.refs_3_ = f32[16,128]{1,0:T(8,128)S(1)} custom-call(f32[4,8,90,128]{3,2,1,0:T(8,128)S(1)} %get-tuple-element.19.links_ref, f32[2,8,6,16,128]{4,3,2,1,0:T(8,128)S(1)} %shard_map.55.refs_0_.refs_1_), custom_call_target="tpu_custom_call" | custom-call | flops 16384000 | bytes 2269184 | tf_op jit(solution)/shard_map/pallas_call | solution.py:34
  76.1 4.0 %shard_map.57.sofar_ref = f32[16,128]{1,0:T(8,128)S(1)} custom-call(f32[4,8,90,128]{3,2,1,0:T(8,128)S(1)} %get-tuple-element.19.links_ref, f32[1,8,6,16,128]{4,3,2,1,0:T(8,128)S(1)} %shard_map.54.refs_0_, f32[2,8,6,16,128]{4,3,2,1,0:T(8,128)S(1)} %shard_map.55.refs_0_.refs_1_, f32[1,8,6,16,128]{4,3,2,1,0:T(8,128)S(1)} %shard_map.53.refs_2_.top_ref, ...), custom_call_target="tpu_custom_call" | custom-call | flops 24576000 | bytes 3063808 | tf_op jit(solution)/shard_map/pallas_call | solution.py:34
  80.1 1.0 %shard_map.58 = f32[16,128]{1,0:T(8,128)S(1)} custom-call(f32[8,18,128]{2,1,0:T(8,128)S(1)} %get-tuple-element.17.refs_0_.links_ref, f32[1,8,6,16,128]{4,3,2,1,0:T(8,128)S(1)} %shard_map.53.refs_2_.top_ref, f32[1,8,6,16,128]{4,3,2,1,0:T(8,128)S(1)} %collective-permute-done.8.above_ref, f32[16,128]{1,0:T(8,128)S(1)} %shard_map.57.sofar_ref), custom_call_target="tpu_custom_call" | custom-call | flops 4096000 | bytes 876544 | tf_op jit(solution)/shard_map/pallas_call | solution.py:34
  81.3 4.3 %collective-permute-done.11 = f32[16,128]{1,0:T(8,128)S(1)} collective-permute-done((f32[16,128]{1,0:T(8,128)S(1)}, f32[16,128]{1,0:T(8,128)S(1)}, u32[]{:S(2)}, u32[]{:S(2)}) %collective-permute-start.11) | collective-permute-done | bytes 8224 | tf_op jit(solution)/shard_map/ppermute | solution.py:344
  85.7 3.6 %collective-permute-done.9 = f32[16,128]{1,0:T(8,128)S(1)} collective-permute-done((f32[16,128]{1,0:T(8,128)S(1)}, f32[16,128]{1,0:T(8,128)S(1)}, u32[]{:S(2)}, u32[]{:S(2)}) %collective-permute-start.9) | collective-permute-done | bytes 8224 | tf_op jit(solution)/shard_map/ppermute | solution.py:344
  89.3 1.3 %collective-permute-start.14 = (f32[16,128]{1,0:T(8,128)S(1)}, f32[16,128]{1,0:T(8,128)S(1)}, u32[]{:S(2)}, u32[]{:S(2)}) collective-permute-start(f32[16,128]{1,0:T(8,128)S(1)} %add_add_fusion.refs_0_), channel_id=1, source_target_pairs={{0,20},{1,21},{2,22},{3,23},{4,16},{5,17},{6,18},{7,19},{16,4},{17... | collective-permute-start | bytes 24584 | tf_op jit(solution)/shard_map/ppermute | solution.py:354
  91.2 2.5 %collective-permute-start.12 = (f32[16,128]{1,0:T(8,128)S(1)}, f32[16,128]{1,0:T(8,128)S(1)}, u32[]{:S(2)}, u32[]{:S(2)}) collective-permute-start(f32[16,128]{1,0:T(8,128)S(1)} %add_add_fusion.refs_0_), channel_id=1, source_target_pairs={{0,4},{1,5},{2,6},{3,7},{4,0},{5,1},{6,2},{7,3},{8,12},{9,13},{10,... | collective-permute-start | bytes 24584 | tf_op jit(solution)/shard_map/ppermute | solution.py:344
  93.7 1.6 %shard_map.59.refs_2_ = f32[3072,128]{1,0:T(8,128)S(1)} custom-call(f32[1,8,6,16,128]{4,3,2,1,0:T(8,128)S(1)} %shard_map.54.refs_0_, f32[2,8,6,16,128]{4,3,2,1,0:T(8,128)S(1)} %shard_map.55.refs_0_.refs_1_, f32[1,8,6,16,128]{4,3,2,1,0:T(8,128)S(1)} %shard_map.53.refs_2_.top_ref), custom_call_target="tpu_custom_call" | custom-call | flops 1000000 | bytes 3145728 | tf_op jit(solution)/shard_map/pallas_call | solution.py:34
  95.3 1.6 %shard_map.60.refs_5_ = f32[3072,128]{1,0:T(8,128)S(1)} custom-call(f32[1,8,6,16,128]{4,3,2,1,0:T(8,128)S(1)} %collective-permute-done.15.refs_0_, f32[2,8,6,16,128]{4,3,2,1,0:T(8,128)S(1)} %collective-permute-done.16.refs_1_, f32[1,8,6,16,128]{4,3,2,1,0:T(8,128)S(1)} %collective-permute-done.17.refs_2_), custom_call_target="tpu_custom_call" | custom-call | flops 1000000 | bytes 3145728 | tf_op jit(solution)/shard_map/pallas_call | solution.py:34
  97.0 2.8 %shard_map.61 = (f32[6144,128]{1,0:T(8,128)}, f32[2,2,2,16,16]{4,3,2,1,0:T(8,128)}) custom-call(s32[3]{0:T(128)S(1)} %pad_add_fusion.pick_ref._.slot_ref, f32[16,128]{1,0:T(8,128)S(1)} %add_add_fusion.refs_0_, f32[16,128]{1,0:T(8,128)S(1)} %collective-permute-done.12.refs_1_, f32[3072,128]{1,0:T(8,128)S(1)} %shard_map.59.refs_2_, ...), custom_call_target="tpu_custom_call" | custom-call | flops 1000000 | bytes 6332416 | tf_op jit(solution)/shard_map/pallas_call | solution.py:42
  (34 shorter events, 4.2 us)
Async XLA Ops:
  1.7 9.9 %collective-permute-start = (f32[54,4,512]{2,1,0:T(4,128)S(1)}, f32[54,4,512]{2,1,0:T(4,128)S(1)}, u32[]{:S(2)}, u32[]{:S(2)}) collective-permute-start(f32[54,4,512]{2,1,0:T(4,128)S(1)} %dynamic-slice_bitcast_fusion), channel_id=1, source_target_pairs={{0,8},{8,0},{1,9},{9,1},{2,10},{10,2},{3,11},{11,3},{4,12},{12,4},... | collective-permute-start | bytes 1327112 | tf_op jit(solution)/shard_map/ppermute | solution.py:344
  2.3 1.9 %copy-start = (f32[2,16,2,3,4,1024]{5,4,3,2,1,0:T(4,128)S(1)}, f32[2,16,2,3,4,1024]{5,4,3,2,1,0:T(4,128)}, u32[]{:S(2)}) copy-start(f32[2,16,2,3,4,1024]{5,4,3,2,1,0:T(4,128)} %param.3) | copy-start | bytes 9437188
  4.2 12.8 %copy-start.1 = (f32[2,16,2,3,4,1024]{5,4,3,2,1,0:T(4,128)S(1)}, f32[2,16,2,3,4,1024]{5,4,3,2,1,0:T(4,128)}, u32[]{:S(2)}) copy-start(f32[2,16,2,3,4,1024]{5,4,3,2,1,0:T(4,128)} %param.3) | copy-start | bytes 9437188
  6.1 20.5 %collective-permute-start.4 = (f32[1,8,6,16,128]{4,3,2,1,0:T(8,128)S(1)}, f32[1,8,6,16,128]{4,3,2,1,0:T(8,128)S(1)}, u32[]{:S(2)}, u32[]{:S(2)}) collective-permute-start(f32[1,8,6,16,128]{4,3,2,1,0:T(8,128)S(1)} %get-tuple-element.21.refs_2_.refs_4_), channel_id=1, source_target_pairs={{0,1},{1,2},{2,3},{3,4},{4,5},{5,6},{6,7},{7,0},{8,9},{9,10},{10,1... | collective-permute-start | bytes 1179656 | tf_op jit(solution)/shard_map/ppermute | solution.py:340
  8.6 25.4 %collective-permute-start.2 = (f32[1,8,6,16,128]{4,3,2,1,0:T(8,128)S(1)}, f32[1,8,6,16,128]{4,3,2,1,0:T(8,128)S(1)}, u32[]{:S(2)}, u32[]{:S(2)}) collective-permute-start(f32[1,8,6,16,128]{4,3,2,1,0:T(8,128)S(1)} %get-tuple-element.18.refs_0_.refs_3_), channel_id=1, source_target_pairs={{0,7},{1,0},{2,1},{3,2},{4,3},{5,4},{6,5},{7,6},{8,15},{9,8},{10,9... | collective-permute-start | bytes 1179656 | tf_op jit(solution)/shard_map/ppermute | solution.py:340
  11.6 1.5 %copy-start.2 = (f32[4,3,2,3,3,4,512]{6,5,4,3,2,1,0:T(4,128)S(1)}, f32[4,3,2,3,3,4,512]{6,5,4,3,2,1,0:T(4,128)}, u32[]{:S(2)}) copy-start(f32[4,3,2,3,3,4,512]{6,5,4,3,2,1,0:T(4,128)} %param.2) | copy-start | bytes 5308420
  17.0 11.2 %collective-permute-start.1 = (f32[8,18,128]{2,1,0:T(8,128)S(1)}, f32[8,18,128]{2,1,0:T(8,128)S(1)}, u32[]{:S(2)}, u32[]{:S(2)}) collective-permute-start(f32[8,18,128]{2,1,0:T(8,128)S(1)} %get-tuple-element.17.refs_0_.links_ref), channel_id=1, source_target_pairs={{0,1},{1,2},{2,3},{3,4},{4,5},{5,6},{6,7},{7,0},{8,9},{9,10},{10,1... | collective-permute-start | bytes 221192 | tf_op jit(solution)/shard_map/ppermute | solution.py:340
  28.4 19.9 %collective-permute-start.6 = (f32[1,8,6,16,128]{4,3,2,1,0:T(8,128)S(1)}, f32[1,8,6,16,128]{4,3,2,1,0:T(8,128)S(1)}, u32[]{:S(2)}, u32[]{:S(2)}) collective-permute-start(f32[1,8,6,16,128]{4,3,2,1,0:T(8,128)S(1)} %shard_map.46.refs_0_.refs_3_), channel_id=1, source_target_pairs={{0,7},{1,0},{2,1},{3,2},{4,3},{5,4},{6,5},{7,6},{8,15},{9,8},{10,9... | collective-permute-start | bytes 1179656 | tf_op jit(solution)/shard_map/ppermute | solution.py:340
  34.2 14.4 %collective-permute-start.3 = (f32[1,8,6,16,128]{4,3,2,1,0:T(8,128)S(1)}, f32[1,8,6,16,128]{4,3,2,1,0:T(8,128)S(1)}, u32[]{:S(2)}, u32[]{:S(2)}) collective-permute-start(f32[1,8,6,16,128]{4,3,2,1,0:T(8,128)S(1)} %shard_map.45.refs_2_.refs_4_), channel_id=1, source_target_pairs={{0,1},{1,2},{2,3},{3,4},{4,5},{5,6},{6,7},{7,0},{8,9},{9,10},{10,1... | collective-permute-start | bytes 1179656 | tf_op jit(solution)/shard_map/ppermute | solution.py:340
  48.5 16.8 %collective-permute-start.7 = (f32[1,8,6,16,128]{4,3,2,1,0:T(8,128)S(1)}, f32[1,8,6,16,128]{4,3,2,1,0:T(8,128)S(1)}, u32[]{:S(2)}, u32[]{:S(2)}) collective-permute-start(f32[1,8,6,16,128]{4,3,2,1,0:T(8,128)S(1)} %shard_map.51.refs_2_), channel_id=1, source_target_pairs={{0,1},{1,2},{2,3},{3,4},{4,5},{5,6},{6,7},{7,0},{8,9},{9,10},{10,1... | collective-permute-start | bytes 1179656 | tf_op jit(solution)/shard_map/ppermute | solution.py:340
  48.8 21.9 %collective-permute-start.5 = (f32[1,8,6,16,128]{4,3,2,1,0:T(8,128)S(1)}, f32[1,8,6,16,128]{4,3,2,1,0:T(8,128)S(1)}, u32[]{:S(2)}, u32[]{:S(2)}) collective-permute-start(f32[1,8,6,16,128]{4,3,2,1,0:T(8,128)S(1)} %shard_map.49.refs_0_), channel_id=1, source_target_pairs={{0,7},{1,0},{2,1},{3,2},{4,3},{5,4},{6,5},{7,6},{8,15},{9,8},{10,9... | collective-permute-start | bytes 1179656 | tf_op jit(solution)/shard_map/ppermute | solution.py:340
  60.0 35.3 %collective-permute-start.16 = (f32[2,8,6,16,128]{4,3,2,1,0:T(8,128)S(1)}, f32[2,8,6,16,128]{4,3,2,1,0:T(8,128)S(1)}, u32[]{:S(2)}, u32[]{:S(2)}) collective-permute-start(f32[2,8,6,16,128]{4,3,2,1,0:T(8,128)S(1)} %shard_map.55.refs_0_.refs_1_), channel_id=1, source_target_pairs={{0,16},{16,0},{1,17},{17,1},{2,18},{18,2},{3,19},{19,3},{4,20},{20... | collective-permute-start | bytes 2359304 | tf_op jit(solution)/shard_map/ppermute | solution.py:344
  65.5 14.6 %collective-permute-start.8 = (f32[1,8,6,16,128]{4,3,2,1,0:T(8,128)S(1)}, f32[1,8,6,16,128]{4,3,2,1,0:T(8,128)S(1)}, u32[]{:S(2)}, u32[]{:S(2)}) collective-permute-start(f32[1,8,6,16,128]{4,3,2,1,0:T(8,128)S(1)} %shard_map.54.refs_0_), channel_id=1, source_target_pairs={{0,7},{1,0},{2,1},{3,2},{4,3},{5,4},{6,5},{7,6},{8,15},{9,8},{10,9... | collective-permute-start | bytes 1179656 | tf_op jit(solution)/shard_map/ppermute | solution.py:340
  70.9 20.3 %collective-permute-start.17 = (f32[1,8,6,16,128]{4,3,2,1,0:T(8,128)S(1)}, f32[1,8,6,16,128]{4,3,2,1,0:T(8,128)S(1)}, u32[]{:S(2)}, u32[]{:S(2)}) collective-permute-start(f32[1,8,6,16,128]{4,3,2,1,0:T(8,128)S(1)} %shard_map.53.refs_2_.top_ref), channel_id=1, source_target_pairs={{0,16},{16,0},{1,17},{17,1},{2,18},{18,2},{3,19},{19,3},{4,20},{20... | collective-permute-start | bytes 1179656 | tf_op jit(solution)/shard_map/ppermute | solution.py:344
  72.4 22.9 %collective-permute-start.15 = (f32[1,8,6,16,128]{4,3,2,1,0:T(8,128)S(1)}, f32[1,8,6,16,128]{4,3,2,1,0:T(8,128)S(1)}, u32[]{:S(2)}, u32[]{:S(2)}) collective-permute-start(f32[1,8,6,16,128]{4,3,2,1,0:T(8,128)S(1)} %shard_map.54.refs_0_), channel_id=1, source_target_pairs={{0,16},{16,0},{1,17},{17,1},{2,18},{18,2},{3,19},{19,3},{4,20},{20... | collective-permute-start | bytes 1179656 | tf_op jit(solution)/shard_map/ppermute | solution.py:344
  81.1 4.6 %collective-permute-start.11 = (f32[16,128]{1,0:T(8,128)S(1)}, f32[16,128]{1,0:T(8,128)S(1)}, u32[]{:S(2)}, u32[]{:S(2)}) collective-permute-start(f32[16,128]{1,0:T(8,128)S(1)} %shard_map.58), channel_id=1, source_target_pairs={{0,3},{1,2},{2,1},{3,0},{4,7},{5,6},{6,5},{7,4},{8,11},{9,10},{10,... | collective-permute-start | bytes 24584 | tf_op jit(solution)/shard_map/ppermute | solution.py:344
  81.1 4.5 %collective-permute-start.10 = (f32[16,128]{1,0:T(8,128)S(1)}, f32[16,128]{1,0:T(8,128)S(1)}, u32[]{:S(2)}, u32[]{:S(2)}) collective-permute-start(f32[16,128]{1,0:T(8,128)S(1)} %shard_map.58), channel_id=1, source_target_pairs={{0,2},{1,3},{2,0},{3,1},{4,6},{5,7},{6,4},{7,5},{8,10},{9,11},{10,... | collective-permute-start | bytes 24584 | tf_op jit(solution)/shard_map/ppermute | solution.py:344
  85.7 3.7 %collective-permute-start.9 = (f32[16,128]{1,0:T(8,128)S(1)}, f32[16,128]{1,0:T(8,128)S(1)}, u32[]{:S(2)}, u32[]{:S(2)}) collective-permute-start(f32[16,128]{1,0:T(8,128)S(1)} %shard_map.58), channel_id=1, source_target_pairs={{0,1},{1,0},{2,3},{3,2},{4,5},{5,4},{6,7},{7,6},{8,9},{9,8},{10,11... | collective-permute-start | bytes 24584 | tf_op jit(solution)/shard_map/ppermute | solution.py:344
  89.3 7.6 %collective-permute-start.14 = (f32[16,128]{1,0:T(8,128)S(1)}, f32[16,128]{1,0:T(8,128)S(1)}, u32[]{:S(2)}, u32[]{:S(2)}) collective-permute-start(f32[16,128]{1,0:T(8,128)S(1)} %add_add_fusion.refs_0_), channel_id=1, source_target_pairs={{0,20},{1,21},{2,22},{3,23},{4,16},{5,17},{6,18},{7,19},{16,4},{17... | collective-permute-start | bytes 24584 | tf_op jit(solution)/shard_map/ppermute | solution.py:354
  90.6 6.3 %collective-permute-start.13 = (f32[16,128]{1,0:T(8,128)S(1)}, f32[16,128]{1,0:T(8,128)S(1)}, u32[]{:S(2)}, u32[]{:S(2)}) collective-permute-start(f32[16,128]{1,0:T(8,128)S(1)} %add_add_fusion.refs_0_), channel_id=1, source_target_pairs={{0,16},{1,17},{2,18},{3,19},{4,20},{5,21},{6,22},{7,23},{16,0},{17... | collective-permute-start | bytes 24584 | tf_op jit(solution)/shard_map/ppermute | solution.py:354
  91.2 5.8 %collective-permute-start.12 = (f32[16,128]{1,0:T(8,128)S(1)}, f32[16,128]{1,0:T(8,128)S(1)}, u32[]{:S(2)}, u32[]{:S(2)}) collective-permute-start(f32[16,128]{1,0:T(8,128)S(1)} %add_add_fusion.refs_0_), channel_id=1, source_target_pairs={{0,4},{1,5},{2,6},{3,7},{4,0},{5,1},{6,2},{7,3},{8,12},{9,13},{10,... | collective-permute-start | bytes 24584 | tf_op jit(solution)/shard_map/ppermute | solution.py:344
where the time goes:
time: 100 us; the launch traced here: 99.8 us
  Pallas kernels  40.9 us (41%)
  starting transfers between devices  30.1 us (30%)
  waiting for transfers between devices  23.5 us (24%)
  local copies, waits for them, and re-layouts  4.42 us (4%)
    pallas_call x17, Pallas kernels, call(): pl.pallas_call(kernel, in_specs=[VMEM] * len(args), out_specs=specs, scra...  31.1 us
    ppermute x8, starting transfers between devices, shifted(): return lax.ppermute(x, axis, [(i, (i + by) % n) for i in range(n)])  21.3 us
    ppermute x8, waiting for transfers between devices, shifted(): return lax.ppermute(x, axis, [(i, (i + by) % n) for i in range(n)])  15.5 us
    pallas_call x4, Pallas kernels, call(): return pl.pallas_call(kernel, grid_spec=spec, **params)(pick, *args)  9.75 us
    ppermute x8, waiting for transfers between devices, flipped(): lax.ppermute(x, axis, [(i, i ^ bit) for i in range(lax.axis_size(axis))])  7.98 us
    ppermute x8, starting transfers between devices, flipped(): lax.ppermute(x, axis, [(i, i ^ bit) for i in range(lax.axis_size(axis))])  6.95 us
    unnamed x6, local copies, waits for them, and re-layouts  3.37 us
  transfers between devices with their start and end apart: 18, of which 6 were waited for; matrix products, arithmetic and copies ran while one was open for 0% of the time, Pallas kernels for 38%

commit v1 on v0

--- a/solution.py
+++ b/solution.py
@@ -14,6 +14,7 @@
 F32 = jnp.float32
 BF16 = jnp.bfloat16
 VMEM = pl.BlockSpec(memory_space=pltpu.VMEM)
+FAR = pl.BlockSpec(memory_space=pltpu.HBM)
 GRANT = 16 * 2**20
 
 
@@ -21,23 +22,25 @@
     return jax.ShapeDtypeStruct(dims, dtype)
 
 
-def call(kernel, outs, *args, ops=1e6, scratch=(), pick=None, whole=None, grid=1):
+def call(kernel, outs, *args, ops=1e6, scratch=(), pick=None, far=(), place=None, grid=1, alias=None):
     size = sum(a.size * 4 for a in args) + sum(4 * o.size for o in jax.tree.leaves(outs))
     several = isinstance(outs, (list, tuple))
     params = dict(
         out_shape=outs,
         compiler_params=pltpu.CompilerParams(vmem_limit_bytes=GRANT),
         cost_estimate=pl.CostEstimate(flops=int(ops), bytes_accessed=int(size), transcendentals=0),
-    )
+        input_output_aliases=alias or {},
+    )
+    in_specs = [FAR if k in far else VMEM for k in range(len(args))]
+    out_specs = [VMEM] * len(outs) if several else VMEM
     if pick is None:
-        specs = [VMEM] * len(outs) if several else VMEM
         return pl.pallas_call(
-            kernel, in_specs=[VMEM] * len(args), out_specs=specs, scratch_shapes=scratch, **params
+            kernel, in_specs=in_specs, out_specs=out_specs, scratch_shapes=scratch, **params
         )(*args)
-    specs = [pl.BlockSpec(*whole[k]) if k in whole else VMEM for k in range(len(args) + len(outs))]
+    if place is not None:
+        out_specs = [pl.BlockSpec(*place)] + out_specs[1:]
     spec = pltpu.PrefetchScalarGridSpec(
-        num_scalar_prefetch=1, grid=(grid,), in_specs=specs[: len(args)], out_specs=specs[len(args) :],
-        scratch_shapes=scratch,
+        num_scalar_prefetch=1, grid=(grid,), in_specs=in_specs, out_specs=out_specs, scratch_shapes=scratch
     )
     return pl.pallas_call(kernel, grid_spec=spec, **params)(pick, *args)
 
@@ -90,43 +93,65 @@
     return jnp.where(lane < LX, pltpu.roll(before, LX, ax), pltpu.roll(here, LX, ax))
 
 
-def split_kernel(depth, rows, vecs, pieces, _, v_ref, *out_refs):
-    out = plane_refs(out_refs[: len(pieces)], pieces)
+def take_planes(out, raw_ref, first, count, rows, depth):
     stride = 6 * rows * depth
 
     def body(c, _):
         for z in out:
             for q in range(6):
-                out[z][c, q] = v_ref[pl.ds(q * rows * depth + c * depth + z, vecs, stride=stride), :]
+                start = first * stride + q * rows * depth + c * depth + z
+                out[z][c, q, first : first + count, :] = raw_ref[pl.ds(start, count, stride=stride), :]
         return 0
 
     lax.fori_loop(0, rows, body, 0)
-    if len(out_refs) > len(pieces):
-        out_refs[-1][...] = v_ref[0:8, :]
-
-
-def link_kernel(depth, half, pick_ref, kept_ref, came_ref, out_ref, top_ref):
-    rows = 2 * half
+
+
+def ends_kernel(depth, pieces, pick_ref, far_ref, raw_ref, *refs):
+    *out_refs, sems = refs
+    out = plane_refs(out_refs, pieces)
+    rows, _, vecs, _ = out[0].shape
+    size = raw_ref.shape[0]
+    parts = 2
+    copies = []
+    for k in range(parts):
+        block = pl.ds(k * (size // parts), size // parts)
+        source = pl.ds(pick_ref[0] * size + k * (size // parts), size // parts)
+        copies.append(pltpu.make_async_copy(far_ref.at[source], raw_ref.at[block], sems.at[k]))
+        copies[-1].start()
+    for k in range(parts):
+        copies[k].wait()
+        take_planes(out, raw_ref, k * (vecs // parts), vecs // parts, rows, depth)
+
+
+def rest_kernel(depth, pieces, raw_ref, *out_refs):
+    out = plane_refs(out_refs, pieces)
+    rows, _, vecs, _ = out[pieces[0][0]].shape
+    take_planes(out, raw_ref, 0, vecs, rows, depth)
+
+
+def link_kernel(depth, half, pick_ref, far_ref, came_ref, table_ref, behind_ref, top_ref, sem):
     core = pick_ref[1]
-
-    def body(c, _):
-        for ref, first in ((kept_ref, core * half), (came_ref, (1 - core) * half)):
-            for z in range(depth):
-                out_ref[z, first + c, 0:54, :] = ref[pl.ds(c * depth + z, 54, stride=half * depth), :]
+    copy = pltpu.make_async_copy(far_ref.at[pick_ref[2]], table_ref.at[core], sem)
+    copy.start()
+    table_ref[1 - core] = came_ref[...]
+    copy.wait()
+    count = half * depth
+    lane = lane_index((count, LANES))
+
+    def shift(d, _):
+        for h in range(2):
+            behind_ref[h, d] = behind_x(table_ref[h, d], lane)
+        low, high = table_ref[0, 18 + d], table_ref[1, 18 + d]
+        for h, here, wrap in ((0, low, high), (1, high, low)):
+            before = wrap[count - depth :]
+            if half > 1:
+                before = jnp.concatenate([before, here[: count - depth]], axis=0)
+            behind_ref[h, 18 + d] = behind_y(here, before, lane)
+        for h in range(2):
+            top_ref[d, h * half : (h + 1) * half, :] = table_ref[h, 36 + d, pl.ds(depth - 1, half, stride=depth), :]
         return 0
 
-    lax.fori_loop(0, half, body, 0)
-    lane = lane_index((18, LANES))
-
-    def shift(c, _):
-        before = lax.rem(c + rows - 1, rows)
-        for z in range(depth):
-            out_ref[z, c, 54:72, :] = behind_x(out_ref[z, c, 0:18, :], lane)
-            out_ref[z, c, 72:90, :] = behind_y(out_ref[z, c, 18:36, :], out_ref[z, before, 18:36, :], lane)
-        top_ref[c, 0:18, :] = out_ref[depth - 1, c, 36:54, :]
-        return 0
-
-    lax.fori_loop(0, rows, shift, 0)
+    lax.fori_loop(0, 18, shift, 0)
 
 
 def multiply_into(total, field, link, adjoint):
@@ -143,32 +168,46 @@
                 total[3 + row] = total[3 + row] + a * im + b * re
 
 
-def link_rows(ref, c, first, vecs):
+def rows_of(ref, c, z, depth, first, vecs):
+    half = ref.shape[2] // depth
+    row = lax.rem(c, half) * depth + z
+
     def link(k):
-        return jnp.broadcast_to(ref[c, first + k : first + k + 1, :], (vecs, LANES))
+        return jnp.broadcast_to(ref[c // half, first + k, pl.ds(row, 1), :], (vecs, LANES))
 
     return link
 
 
-def forward_hops(total, cur, up, links, c, rows, lane):
-    vecs = lane.shape[0]
+def edge_rows(ref, c, vecs):
+    def link(k):
+        return jnp.broadcast_to(ref[k, pl.ds(c, 1), :], (vecs, LANES))
+
+    return link
+
+
+def forward_hops(total, cur, up, table, c, z, depth, lane):
+    rows, _, vecs, _ = cur.shape
     after = lax.rem(c + 1, rows)
-    multiply_into(total, lambda q: ahead_x(cur[c, q], lane), link_rows(links, c, 0, vecs), False)
-    multiply_into(total, lambda q: ahead_y(cur[c, q], cur[after, q], lane), link_rows(links, c, 18, vecs), False)
+    multiply_into(total, lambda q: ahead_x(cur[c, q], lane), rows_of(table, c, z, depth, 0, vecs), False)
+    multiply_into(
+        total, lambda q: ahead_y(cur[c, q], cur[after, q], lane), rows_of(table, c, z, depth, 18, vecs), False
+    )
     if up is not None:
-        multiply_into(total, lambda q: up[c, q], link_rows(links, c, 36, vecs), False)
-
-
-def backward_hops(total, cur, down, links, down_links, c, rows, lane):
-    vecs = lane.shape[0]
+        multiply_into(total, lambda q: up[c, q], rows_of(table, c, z, depth, 36, vecs), False)
+
+
+def backward_hops(total, cur, down, table, behind, c, z, depth, lane):
+    rows, _, vecs, _ = cur.shape
     before = lax.rem(c + rows - 1, rows)
-    multiply_into(total, lambda q: behind_x(cur[c, q], lane), link_rows(links, c, 54, vecs), True)
-    multiply_into(total, lambda q: behind_y(cur[c, q], cur[before, q], lane), link_rows(links, c, 72, vecs), True)
+    multiply_into(total, lambda q: behind_x(cur[c, q], lane), rows_of(behind, c, z, depth, 0, vecs), True)
+    multiply_into(
+        total, lambda q: behind_y(cur[c, q], cur[before, q], lane), rows_of(behind, c, z, depth, 18, vecs), True
+    )
     if down is not None:
-        multiply_into(total, lambda q: down[c, q], link_rows(down_links, c, 36, vecs), True)
-
-
-def part_kernel(pieces, todo, factor, first, links_ref, *refs):
+        multiply_into(total, lambda q: down[c, q], rows_of(table, c, z - 1, depth, 36, vecs), True)
+
+
+def part_kernel(depth, pieces, todo, factor, first, table_ref, behind_ref, *refs):
     refs = list(refs)
     cur = plane_refs([refs.pop(0) for _ in pieces], pieces)
     done = [pieces[k] for k in todo]
@@ -180,10 +219,8 @@
 
         def body(c, _, z=z):
             total = [cur[z][c, q] for q in range(6)]
-            links = links_ref.at[z]
-            forward_hops(total, cur[z], cur.get(z + 1), links, c, rows, lane)
-            below = links_ref.at[z - 1] if z else None
-            backward_hops(total, cur[z], cur.get(z - 1), links, below, c, rows, lane)
+            forward_hops(total, cur[z], cur.get(z + 1), table_ref, c, z, depth, lane)
+            backward_hops(total, cur[z], cur.get(z - 1), table_ref, behind_ref, c, z, depth, lane)
             for q in range(6):
                 value = total[q] * factor
                 out[z][c, q] = value if first else value - old[z][c, q]
@@ -200,7 +237,7 @@
         total = [jnp.zeros((vecs, LANES), F32) for _ in range(6)]
         for k, back in enumerate(behind):
             links_ref, halo_ref = refs[2 * k : 2 * k + 2]
-            multiply_into(total, lambda q: halo_ref[0, c, q], link_rows(links_ref, c, 0, vecs), back)
+            multiply_into(total, lambda q: halo_ref[0, c, q], edge_rows(links_ref, c, vecs), back)
         for q in range(6):
             out_ref[c, q] = part_ref[c, q] + total[q] * factor
         return 0
@@ -241,23 +278,23 @@
     return jnp.where(lane_index((n, LANES)) % (2 * n) < n, real, imag)
 
 
-def gram_kernel(pieces, tasks, more, links_ref, *refs):
+def gram_kernel(depth, pieces, tasks, more, table_ref, *refs):
     refs = list(refs)
     acc_ref, out_ref = refs.pop(), refs.pop()
     sofar_ref = refs.pop() if more else None
     cur = plane_refs(refs, pieces)
-    rows, _, vecs, _ = out_shape_of(cur)
+    rows, _, vecs, _ = cur[tasks[0][0]].shape
     lane = lane_index((vecs, LANES))
     acc_ref[...] = jnp.zeros_like(acc_ref)
     for z, own, depth_hop in tasks:
 
         def sides(c, z=z, own=own, depth_hop=depth_hop):
             total = [jnp.zeros((vecs, LANES), F32) for _ in range(6)]
-            links = links_ref.at[z]
             if own:
-                forward_hops(total, cur[z], cur[z + 1] if depth_hop else None, links, c, rows, lane)
+                forward_hops(total, cur[z], cur[z + 1] if depth_hop else None, table_ref, c, z, depth, lane)
             else:
-                multiply_into(total, lambda q: cur[z + 1][c, q], link_rows(links, c, 36, vecs), False)
+                up = cur[z + 1]
+                multiply_into(total, lambda q: up[c, q], rows_of(table_ref, c, z, depth, 36, vecs), False)
             return [cur[z][c, q] for q in range(6)], total
 
         products(acc_ref, rows, own, sides)
@@ -265,17 +302,13 @@
     out_ref[...] = part + sofar_ref[...] if more else part
 
 
-def out_shape_of(planes):
-    return next(iter(planes.values())).shape
-
-
 def last_hop_kernel(links_ref, top_ref, above_ref, sofar_ref, out_ref, acc_ref):
     rows, _, vecs, _ = top_ref.shape[1:]
     acc_ref[...] = jnp.zeros_like(acc_ref)
 
     def sides(c):
         total = [jnp.zeros((vecs, LANES), F32) for _ in range(6)]
-        multiply_into(total, lambda q: above_ref[0, c, q], link_rows(links_ref, c, 0, vecs), False)
+        multiply_into(total, lambda q: above_ref[0, c, q], edge_rows(links_ref, c, vecs), False)
         return [top_ref[0, c, q] for q in range(6)], total
 
     products(acc_ref, rows, False, sides)
@@ -288,34 +321,55 @@
     return jnp.where(diag, packed, 0.0)
 
 
-def scatter_kernel(depth, pieces, *refs):
+def scatter_kernel(depth, planes, piece_ref, *refs):
     out_ref = refs[-1]
-    planes = plane_refs(refs[:-1], pieces)
-    rows, _, vecs, _ = planes[0].shape
+    rows, _, vecs, _ = piece_ref.shape[1:]
     stride = 6 * rows * depth
 
     def body(c, _):
-        for z in range(depth):
+        for k, z in enumerate(planes):
             for q in range(6):
                 start = q * rows * depth + c * depth + z
-                out_ref[pl.ds(start, vecs, stride=stride), :] = planes[z][c, q]
+                out_ref[pl.ds(start, vecs, stride=stride), :] = piece_ref[k, c, q]
         return 0
 
     lax.fori_loop(0, rows, body, 0)
 
 
-def final_kernel(slot_ref, *refs):
+def final_kernel(steps, slot_ref, *refs):
     out_ref, grams_ref, scale_ref = refs[-3:]
+    step = pl.program_id(0)
     for k in range(2):
         term0, term1, field_ref = refs[3 * k : 3 * k + 3]
         n = term0.shape[0]
-
-        @pl.when(pl.program_id(0) == k)
-        def _(k=k, term0=term0, term1=term1, field_ref=field_ref):
-            slot = slot_ref[0] if k == 0 else 1 - slot_ref[0]
+        slot = slot_ref[0] if k == 0 else 1 - slot_ref[0]
+
+        def normalised(term0=term0, term1=term1):
             packed = term0[...] + term1[...]
             norm = norms_of(packed)
-            down = lax.rsqrt(jnp.sum(norm, axis=1, keepdims=True))
+            return packed, norm, lax.rsqrt(jnp.sum(norm, axis=1, keepdims=True))
+
+        @pl.when(step == k * steps)
+        def _(n=n, normalised=normalised):
+            scale_ref[...] = jnp.broadcast_to(normalised()[2], (n, LANES))
+
+        @pl.when((step >= k * steps) & (step < (k + 1) * steps))
+        def _(k=k, n=n, field_ref=field_ref):
+            size = field_ref.shape[0] // n
+            each = n // steps
+
+            def body(i, _):
+                vec = (step - k * steps) * each + i
+                source = pl.ds(pl.multiple_of(vec * size, 8), size)
+                target = pl.ds(pl.multiple_of(i * size, 8), size)
+                out_ref[target, :] = field_ref[source, :] * scale_ref[pl.ds(vec, 1), :]
+                return 0
+
+            lax.fori_loop(0, each, body, 0)
+
+        @pl.when(step == (k + 1) * steps - 2)
+        def _(n=n, slot=slot, normalised=normalised):
+            packed, norm, down = normalised()
             across = lax.rsqrt(jnp.sum(norm, axis=0, keepdims=True)[:, 0:n])
             scale = down * across
             over_re, over_im = packed[:, 0:n], packed[:, n : 2 * n]
@@ -324,15 +378,6 @@
             grams_ref[slot, 0, 1] = over_im * scale
             grams_ref[slot, 1, 0] = (6.0 * over_re - (hop_re + hop_re.T)) * scale
             grams_ref[slot, 1, 1] = (6.0 * over_im - (hop_im - hop_im.T)) * scale
-            scale_ref[...] = jnp.broadcast_to(down, (n, LANES))
-            size = out_ref.shape[0] // n
-
-            def body(i, _):
-                block = pl.ds(pl.multiple_of(i * size, 8), size)
-                out_ref[block, :] = field_ref[block, :] * scale_ref[pl.ds(i, 1), :]
-                return 0
-
-            lax.fori_loop(0, n, body, 0)
 
 
 def shifted(x, axis, by):
@@ -376,33 +421,33 @@
     field = [shape_of(len(p), rows, 6, vecs, LANES) for p in pieces]
     work = 1000 * LANES * vecs * rows
     many = vecs * 6 * rows * depth
-    mine_block = ((many, LANES), lambda step, pick: (pick[0], 0))
-
-    view = to_rows(vectors)
-
-    def split(todo, token):
-        return call(
-            functools.partial(split_kernel, depth, rows, vecs, [pieces[k] for k in todo]),
-            [field[k] for k in todo] + token, view, pick=pick, whole={0: mine_block}, ops=1e5,
-        )
-
+    half = rows // 2
+    sem = pltpu.SemaphoreType.DMA
+
+    raw, *got = call(
+        functools.partial(ends_kernel, depth, [pieces[k] for k in ends]),
+        [shape_of(many, LANES)] + [field[k] for k in ends],
+        to_rows(vectors), pick=pick, far=(0,), scratch=[sem((2,))], ops=1e5,
+    )
     start = [None] * len(pieces)
-    *got, token = split(ends, [shape_of(8, LANES)])
     for k, x in zip(ends, got):
         start[k] = x
-    links, view, _ = lax.optimization_barrier((links, view, token))
-
     flat = links.reshape((links.shape[0], 54) + links.shape[-2:])
     given = lax.dynamic_index_in_dim(flat, 2 * (1 - core) + mine, 0, keepdims=False)
     came = flipped(given, "ta", 1)
     if inner:
-        for k, x in zip(inner, split(inner, [])):
+        got = call(
+            functools.partial(rest_kernel, depth, [pieces[k] for k in inner]),
+            [field[k] for k in inner], raw, ops=1e5,
+        )
+        for k, x in zip(inner, got):
             start[k] = x
-    block = ((54 * (rows // 2) * depth, LANES), lambda step, pick: (pick[2], 0))
-    table, top_links = call(
-        functools.partial(link_kernel, depth, rows // 2),
-        [shape_of(depth, rows, 90, LANES), shape_of(rows, 18, LANES)],
-        to_rows(links), to_rows(came), pick=pick, whole={0: block}, ops=1e6,
+    table, behind, top_links = call(
+        functools.partial(link_kernel, depth, half),
+        [shape_of(2, 54, half * depth, LANES), shape_of(2, 36, half * depth, LANES), shape_of(18, rows, LANES)],
+        to_rows(links).reshape(-1, 54, half * depth, LANES),
+        to_rows(came).reshape(54, half * depth, LANES),
+        pick=pick, far=(0,), scratch=[sem], ops=1e6,
     )
     prior = shifted(top_links, "sa", 1)
 
@@ -414,8 +459,8 @@
         for todo in (inner, ends):
             if todo:
                 got = call(
-                    functools.partial(part_kernel, pieces, todo, factor, old is None),
-                    [field[k] for k in todo], table, *cur, *([] if old is None else [old[k] for k in todo]),
+                    functools.partial(part_kernel, depth, pieces, todo, factor, old is None),
+                    [field[k] for k in todo], table, behind, *cur, *([] if old is None else [old[k] for k in todo]),
                     ops=work * sum(len(pieces[k]) for k in todo),
                 )
                 for k, x in zip(todo, got):
@@ -438,7 +483,7 @@
 
     def grams_of(planes, tasks, sofar):
         return call(
-            functools.partial(gram_kernel, [pieces[k] for k in planes], tasks, sofar is not None),
+            functools.partial(gram_kernel, depth, [pieces[k] for k in planes], tasks, sofar is not None),
             packed, table, *[three[k] for k in planes], *([] if sofar is None else [sofar]),
             scratch=acc, ops=work * len(tasks) / 2,
         )
@@ -464,13 +509,26 @@
     other = [swapped(x) for x in three]
 
     def scattered(planes):
-        return call(functools.partial(scatter_kernel, depth, pieces), shape_of(many, LANES), *planes, ops=1e6)
-
-    place = ((many, LANES), lambda step, pick: (jnp.where(step == 0, pick[0], 1 - pick[0]), 0))
-    given = [*sum_mine, scattered(three), *sum_other, scattered(other)]
+        out = None
+        for k in inner + ends:
+            out = call(
+                functools.partial(scatter_kernel, depth, pieces[k]), shape_of(many, LANES),
+                planes[k], *([] if out is None else [out]), alias={} if out is None else {1: 0}, ops=1e5,
+            )
+        return out
+
+    steps = 4
+    assert vecs % steps == 0
+
+    def target(step, pick):
+        slot = jnp.where(step < steps, pick[0], 1 - pick[0])
+        return slot * steps + lax.rem(step, steps), 0
+
     out, grams = call(
-        final_kernel, [shape_of(2 * many, LANES), shape_of(2, 2, 2, vecs, vecs)], *given,
-        pick=pick, whole={len(given): place}, grid=2, ops=1e6, scratch=[pltpu.VMEM((vecs, LANES), F32)],
+        functools.partial(final_kernel, steps), [shape_of(2 * many, LANES), shape_of(2, 2, 2, vecs, vecs)],
+        *sum_mine, scattered(three), *sum_other, scattered(other),
+        pick=pick, place=((many // steps, LANES), target), grid=2 * steps, ops=1e6,
+        scratch=[pltpu.VMEM((vecs, LANES), F32)],
     )
     return from_rows(out, vectors.shape), grams
 

time: 100 us -> 101 us (1.010)
  waiting for transfers between devices: 23.5 us -> 25.4 us
  local copies, waits for them, and re-layouts: 4.42 us -> 2.94 us
    ppermute x8, waiting for transfers between devices: 15.5 us -> 21.6 us  [shifted(): return lax.ppermute(x, axis, [(i, (i + by) % n) for i in range(n)])]
    ppermute x8, starting transfers between devices: 21.3 us -> 16.5 us  [shifted(): return lax.ppermute(x, axis, [(i, (i + by) % n) for i in range(n)])]
    ppermute x8, waiting for transfers between devices: 7.98 us -> 3.8 us  [flipped(): lax.ppermute(x, axis, [(i, i ^ bit) for i in range(lax.axis_size(axis))])]
    ppermute x8, starting transfers between devices: 6.95 us -> 9.99 us  [flipped(): lax.ppermute(x, axis, [(i, i ^ bit) for i in range(lax.axis_size(axis))])]
    ppermute x2, starting transfers between devices: 1.87 us -> 3.94 us  [across(): lax.ppermute(x, ('cfg', 'sa'), [(i, i ^ cfg * size + bits) for i in pairs])]
    unnamed x6 -> x4, local copies, waits for them, and re-layouts: 3.37 us -> 1.89 us
    pallas_call x4 -> x3, Pallas kernels: 9.75 us -> 8.47 us  [call(): return pl.pallas_call(kernel, grid_spec=spec, **params)(pick, *args)]
    pallas_call x17 -> x22, Pallas kernels: 31.1 us -> 32.2 us  [call(): pl.pallas_call(kernel, in_specs=in_specs, out_specs=out_specs, scratch_sh...]
  transfers between devices with their start and end apart: 18 -> 18, of which waited for: 6 -> 8; matrix products, arithmetic and copies ran while one was open for 0% -> 0% of each run, Pallas kernels for 38% -> 36%
where the time goes in v1:
time: 101 us; the launch traced here: 100 us
  Pallas kernels  40.6 us (40%)
  starting transfers between devices  30.5 us (30%)
  waiting for transfers between devices  25.4 us (25%)
  local copies, waits for them, and re-layouts  2.94 us (3%)
    pallas_call x22, Pallas kernels, call(): pl.pallas_call(kernel, in_specs=in_specs, out_specs=out_specs, scratch_sh...  32.2 us
    ppermute x8, waiting for transfers between devices, shifted(): return lax.ppermute(x, axis, [(i, (i + by) % n) for i in range(n)])  21.6 us
    ppermute x8, starting transfers between devices, shifted(): return lax.ppermute(x, axis, [(i, (i + by) % n) for i in range(n)])  16.5 us
    ppermute x8, starting transfers between devices, flipped(): lax.ppermute(x, axis, [(i, i ^ bit) for i in range(lax.axis_size(axis))])  9.99 us
    pallas_call x3, Pallas kernels, call(): return pl.pallas_call(kernel, grid_spec=spec, **params)(pick, *args)  8.47 us
    ppermute x2, starting transfers between devices, across(): lax.ppermute(x, ('cfg', 'sa'), [(i, i ^ cfg * size + bits) for i in pairs])  3.94 us
    ppermute x8, waiting for transfers between devices, flipped(): lax.ppermute(x, axis, [(i, i ^ bit) for i in range(lax.axis_size(axis))])  3.8 us
  transfers between devices with their start and end apart: 18, of which 8 were waited for; matrix products, arithmetic and copies ran while one was open for 0% of the time, Pallas kernels for 36%

profile of v1, /device:TPU:0, one launch (start us, length us, event | category | flops | bytes accessed | tf_op | source)
XLA Modules:
  0.0 100.4 jit_solution(7875517724254582409)
XLA Ops:
  0.6 1.0 %dynamic-slice_bitcast_fusion = f32[54,4,512]{2,1,0:T(4,128)S(1)} fusion(f32[4,54,4,512]{3,2,1,0:T(4,128)} %bitcast.27, s32[]{:T(128)S(6)} %select_n.12), kind=kLoop, calls=%fused_computation | loop fusion | bytes 884740 | tf_op jit(solution)/shard_map/jit(dynamic_index_in_dim)/squeeze | solution.py:436
  2.3 1.9 %copy-done = f32[2,16,2,3,4,1024]{5,4,3,2,1,0:T(4,128)S(1)} copy-done((f32[2,16,2,3,4,1024]{5,4,3,2,1,0:T(4,128)S(1)}, f32[2,16,2,3,4,1024]{5,4,3,2,1,0:T(4,128)}, u32[]{:S(2)}) %copy-start) | copy-done | bytes 3145752
  4.2 1.3 %shard_map.42 = (f32[3072,128]{1,0:T(8,128)S(1)}, f32[1,8,6,16,128]{4,3,2,1,0:T(8,128)S(1)}, f32[1,8,6,16,128]{4,3,2,1,0:T(8,128)S(1)}) custom-call(s32[3]{0:T(128)S(1)} %pad_add_fusion.pick_ref.slot_ref, f32[6144,128]{1,0:T(8,128)S(1)} %bitcast.26), custom_call_target="tpu_custom_call" | custom-call | flops 100000 | bytes 5505024 | tf_op jit(solution)/shard_map/pallas_call | solution.py:45
  5.5 2.6 %collective-permute-start.4 = (f32[1,8,6,16,128]{4,3,2,1,0:T(8,128)S(1)}, f32[1,8,6,16,128]{4,3,2,1,0:T(8,128)S(1)}, u32[]{:S(2)}, u32[]{:S(2)}) collective-permute-start(f32[1,8,6,16,128]{4,3,2,1,0:T(8,128)S(1)} %get-tuple-element.21.refs_2_.refs_4_), channel_id=1, source_target_pairs={{0,1},{1,2},{2,3},{3,4},{4,5},{5,6},{6,7},{7,0},{8,9},{9,10},{10,1... | collective-permute-start | bytes 1179656 | tf_op jit(solution)/shard_map/ppermute | solution.py:385
  8.1 3.1 %collective-permute-start.2 = (f32[1,8,6,16,128]{4,3,2,1,0:T(8,128)S(1)}, f32[1,8,6,16,128]{4,3,2,1,0:T(8,128)S(1)}, u32[]{:S(2)}, u32[]{:S(2)}) collective-permute-start(f32[1,8,6,16,128]{4,3,2,1,0:T(8,128)S(1)} %get-tuple-element.17.refs_0_.refs_3_), channel_id=1, source_target_pairs={{0,7},{1,0},{2,1},{3,2},{4,3},{5,4},{6,5},{7,6},{8,15},{9,8},{10,9... | collective-permute-start | bytes 1179656 | tf_op jit(solution)/shard_map/ppermute | solution.py:385
  11.2 2.4 %shard_map.41 = (f32[2,54,16,128]{3,2,1,0:T(8,128)S(1)}, f32[2,36,16,128]{3,2,1,0:T(8,128)S(1)}, f32[18,8,128]{2,1,0:T(8,128)S(1)}) custom-call(s32[3]{0:T(128)S(1)} %pad_add_fusion.pick_ref.slot_ref, f32[4,54,16,128]{3,2,1,0:T(8,128)S(1)} %bitcast.28, f32[54,16,128]{2,1,0:T(8,128)S(1)} %bitcast.29), custom_call_target="tpu_custom_call" | custom-call | flops 1000000 | bytes 3760128 | tf_op jit(solution)/shard_map/pallas_call | solution.py:45
  13.6 0.7 shard_map.43.refs_1_.refs_3_
  14.4 3.0 %shard_map.44 = (f32[1,8,6,16,128]{4,3,2,1,0:T(8,128)S(1)}, f32[1,8,6,16,128]{4,3,2,1,0:T(8,128)S(1)}) custom-call(f32[2,54,16,128]{3,2,1,0:T(8,128)S(1)} %get-tuple-element.18.table_ref, f32[2,36,16,128]{3,2,1,0:T(8,128)S(1)} %get-tuple-element.19.behind_ref, f32[1,8,6,16,128]{4,3,2,1,0:T(8,128)S(1)} %get-tuple-element.17.refs_0_.refs_3_, ...), custom_call_target="tpu_custom_call" | custom-call | flops 32768000 | bytes 3833856 | tf_op jit(solution)/shard_map/pallas_call | solution.py:37
  17.4 8.7 %collective-permute-done.4.refs_1_ = f32[1,8,6,16,128]{4,3,2,1,0:T(8,128)S(1)} collective-permute-done((f32[1,8,6,16,128]{4,3,2,1,0:T(8,128)S(1)}, f32[1,8,6,16,128]{4,3,2,1,0:T(8,128)S(1)}, u32[]{:S(2)}, u32[]{:S(2)}) %collective-permute-start.4) | collective-permute-done | bytes 393248 | tf_op jit(solution)/shard_map/ppermute | solution.py:385
  26.0 1.1 %collective-permute-done.1.refs_0_ = f32[18,8,128]{2,1,0:T(8,128)S(1)} collective-permute-done((f32[18,8,128]{2,1,0:T(8,128)S(1)}, f32[18,8,128]{2,1,0:T(8,128)S(1)}, u32[]{:S(2)}, u32[]{:S(2)}) %collective-permute-start.1) | collective-permute-done | bytes 73760 | tf_op jit(solution)/shard_map/ppermute | solution.py:385
  27.4 5.6 %collective-permute-start.6 = (f32[1,8,6,16,128]{4,3,2,1,0:T(8,128)S(1)}, f32[1,8,6,16,128]{4,3,2,1,0:T(8,128)S(1)}, u32[]{:S(2)}, u32[]{:S(2)}) collective-permute-start(f32[1,8,6,16,128]{4,3,2,1,0:T(8,128)S(1)} %shard_map.46.refs_0_.refs_3_), channel_id=1, source_target_pairs={{0,7},{1,0},{2,1},{3,2},{4,3},{5,4},{6,5},{7,6},{8,15},{9,8},{10,9... | collective-permute-start | bytes 1179656 | tf_op jit(solution)/shard_map/ppermute | solution.py:385
  33.2 3.2 %shard_map.47.refs_1_.refs_3_ = f32[2,8,6,16,128]{4,3,2,1,0:T(8,128)S(1)} custom-call(f32[2,54,16,128]{3,2,1,0:T(8,128)S(1)} %get-tuple-element.18.table_ref, f32[2,36,16,128]{3,2,1,0:T(8,128)S(1)} %get-tuple-element.19.behind_ref, f32[1,8,6,16,128]{4,3,2,1,0:T(8,128)S(1)} %get-tuple-element.17.refs_0_.refs_3_, ...), custom_call_target="tpu_custom_call" | custom-call | flops 32768000 | bytes 3833856 | tf_op jit(solution)/shard_map/pallas_call | solution.py:37
  36.4 3.0 %shard_map.48 = (f32[1,8,6,16,128]{4,3,2,1,0:T(8,128)S(1)}, f32[1,8,6,16,128]{4,3,2,1,0:T(8,128)S(1)}) custom-call(f32[2,54,16,128]{3,2,1,0:T(8,128)S(1)} %get-tuple-element.18.table_ref, f32[2,36,16,128]{3,2,1,0:T(8,128)S(1)} %get-tuple-element.19.behind_ref, f32[1,8,6,16,128]{4,3,2,1,0:T(8,128)S(1)} %shard_map.46.refs_0_.refs_3_, ...), custom_call_target="tpu_custom_call" | custom-call | flops 32768000 | bytes 4620288 | tf_op jit(solution)/shard_map/pallas_call | solution.py:37
  39.5 7.8 %collective-permute-done.6.refs_1_ = f32[1,8,6,16,128]{4,3,2,1,0:T(8,128)S(1)} collective-permute-done((f32[1,8,6,16,128]{4,3,2,1,0:T(8,128)S(1)}, f32[1,8,6,16,128]{4,3,2,1,0:T(8,128)S(1)}, u32[]{:S(2)}, u32[]{:S(2)}) %collective-permute-start.6) | collective-permute-done | bytes 393248 | tf_op jit(solution)/shard_map/ppermute | solution.py:385
  47.5 3.2 %shard_map.50.refs_1_ = f32[2,8,6,16,128]{4,3,2,1,0:T(8,128)S(1)} custom-call(f32[2,54,16,128]{3,2,1,0:T(8,128)S(1)} %get-tuple-element.18.table_ref, f32[2,36,16,128]{3,2,1,0:T(8,128)S(1)} %get-tuple-element.19.behind_ref, f32[1,8,6,16,128]{4,3,2,1,0:T(8,128)S(1)} %shard_map.46.refs_0_.refs_3_, f32[2,8,6,16,128]{4,3,2,1,0:T(8,128)S(1)} %shard_map.47.refs_1_.refs_3_, ...), custom_call_target="tpu_custom_call" | custom-call | flops 32768000 | bytes 4620288 | tf_op jit(solution)/shard_map/pallas_call | solution.py:37
  51.0 3.2 %shard_map.55.refs_0_.refs_1_.piece_ref = f32[2,8,6,16,128]{4,3,2,1,0:T(8,128)S(1)} custom-call(f32[2,54,16,128]{3,2,1,0:T(8,128)S(1)} %get-tuple-element.18.table_ref, f32[2,36,16,128]{3,2,1,0:T(8,128)S(1)} %get-tuple-element.19.behind_ref, f32[1,8,6,16,128]{4,3,2,1,0:T(8,128)S(1)} %shard_map.49.refs_0_, f32[2,8,6,16,128]{4,3,2,1,0:T(8,128)S(1)} %shard_map.50.refs_1_, ...), custom_call_target="tpu_custom_call" | custom-call | flops 32768000 | bytes 4620288 | tf_op jit(solution)/shard_map/pallas_call | solution.py:37
  54.3 1.6 %collective-permute-start.17 = (f32[2,8,6,16,128]{4,3,2,1,0:T(8,128)S(1)}, f32[2,8,6,16,128]{4,3,2,1,0:T(8,128)S(1)}, u32[]{:S(2)}, u32[]{:S(2)}) collective-permute-start(f32[2,8,6,16,128]{4,3,2,1,0:T(8,128)S(1)} %shard_map.55.refs_0_.refs_1_.piece_ref), channel_id=1, source_target_pairs={{0,16},{16,0},{1,17},{17,1},{2,18},{18,2},{3,19},{19,3},{4,20},{20... | collective-permute-start | bytes 2359304 | tf_op jit(solution)/shard_map/ppermute | solution.py:389
  55.8 4.7 %collective-permute-start.5 = (f32[1,8,6,16,128]{4,3,2,1,0:T(8,128)S(1)}, f32[1,8,6,16,128]{4,3,2,1,0:T(8,128)S(1)}, u32[]{:S(2)}, u32[]{:S(2)}) collective-permute-start(f32[1,8,6,16,128]{4,3,2,1,0:T(8,128)S(1)} %shard_map.49.refs_0_), channel_id=1, source_target_pairs={{0,7},{1,0},{2,1},{3,2},{4,3},{5,4},{6,5},{7,6},{8,15},{9,8},{10,9... | collective-permute-start | bytes 1179656 | tf_op jit(solution)/shard_map/ppermute | solution.py:385
  60.5 3.0 %shard_map.52 = (f32[1,8,6,16,128]{4,3,2,1,0:T(8,128)S(1)}, f32[1,8,6,16,128]{4,3,2,1,0:T(8,128)S(1)}) custom-call(f32[2,54,16,128]{3,2,1,0:T(8,128)S(1)} %get-tuple-element.18.table_ref, f32[2,36,16,128]{3,2,1,0:T(8,128)S(1)} %get-tuple-element.19.behind_ref, f32[1,8,6,16,128]{4,3,2,1,0:T(8,128)S(1)} %shard_map.49.refs_0_, ...), custom_call_target="tpu_custom_call" | custom-call | flops 32768000 | bytes 4620288 | tf_op jit(solution)/shard_map/pallas_call | solution.py:37
  64.7 4.1 %collective-permute-done.5.refs_1_ = f32[1,8,6,16,128]{4,3,2,1,0:T(8,128)S(1)} collective-permute-done((f32[1,8,6,16,128]{4,3,2,1,0:T(8,128)S(1)}, f32[1,8,6,16,128]{4,3,2,1,0:T(8,128)S(1)}, u32[]{:S(2)}, u32[]{:S(2)}) %collective-permute-start.5) | collective-permute-done | bytes 393248 | tf_op jit(solution)/shard_map/ppermute | solution.py:385
  69.6 3.2 %shard_map.56.refs_3_ = f32[16,128]{1,0:T(8,128)S(1)} custom-call(f32[2,54,16,128]{3,2,1,0:T(8,128)S(1)} %get-tuple-element.18.table_ref, f32[2,8,6,16,128]{4,3,2,1,0:T(8,128)S(1)} %shard_map.55.refs_0_.refs_1_.piece_ref), custom_call_target="tpu_custom_call" | custom-call | flops 16384000 | bytes 1679360 | tf_op jit(solution)/shard_map/pallas_call | solution.py:37
  72.8 4.1 %shard_map.57.sofar_ref = f32[16,128]{1,0:T(8,128)S(1)} custom-call(f32[2,54,16,128]{3,2,1,0:T(8,128)S(1)} %get-tuple-element.18.table_ref, f32[1,8,6,16,128]{4,3,2,1,0:T(8,128)S(1)} %shard_map.54.refs_0_.piece_ref, f32[2,8,6,16,128]{4,3,2,1,0:T(8,128)S(1)} %shard_map.55.refs_0_.refs_1_.piece_ref, ...), custom_call_target="tpu_custom_call" | custom-call | flops 24576000 | bytes 2473984 | tf_op jit(solution)/shard_map/pallas_call | solution.py:37
  76.9 1.0 %shard_map.58 = f32[16,128]{1,0:T(8,128)S(1)} custom-call(f32[18,8,128]{2,1,0:T(8,128)S(1)} %get-tuple-element.16.refs_0_.links_ref, f32[1,8,6,16,128]{4,3,2,1,0:T(8,128)S(1)} %shard_map.53.refs_2_.top_ref.piece_ref, f32[1,8,6,16,128]{4,3,2,1,0:T(8,128)S(1)} %collective-permute-done.8.above_ref, f32[16,128]{1,0:T(8,128)S(1)} %shard_map.57.sofar_ref), custom_call_target="tpu_custom_call" | custom-call | flops 4096000 | bytes 876544 | tf_op jit(solution)/shard_map/pallas_call | solution.py:37
  77.9 3.9 %collective-permute-start.11 = (f32[16,128]{1,0:T(8,128)S(1)}, f32[16,128]{1,0:T(8,128)S(1)}, u32[]{:S(2)}, u32[]{:S(2)}) collective-permute-start(f32[16,128]{1,0:T(8,128)S(1)} %shard_map.58), channel_id=1, source_target_pairs={{0,3},{1,2},{2,1},{3,0},{4,7},{5,6},{6,5},{7,4},{8,11},{9,10},{10,... | collective-permute-start | bytes 24584 | tf_op jit(solution)/shard_map/ppermute | solution.py:389
  82.3 1.2 %collective-permute-done.11 = f32[16,128]{1,0:T(8,128)S(1)} collective-permute-done((f32[16,128]{1,0:T(8,128)S(1)}, f32[16,128]{1,0:T(8,128)S(1)}, u32[]{:S(2)}, u32[]{:S(2)}) %collective-permute-start.11) | collective-permute-done | bytes 8224 | tf_op jit(solution)/shard_map/ppermute | solution.py:389
  83.4 1.9 %collective-permute-start.9 = (f32[16,128]{1,0:T(8,128)S(1)}, f32[16,128]{1,0:T(8,128)S(1)}, u32[]{:S(2)}, u32[]{:S(2)}) collective-permute-start(f32[16,128]{1,0:T(8,128)S(1)} %shard_map.58), channel_id=1, source_target_pairs={{0,1},{1,0},{2,3},{3,2},{4,5},{5,4},{6,7},{7,6},{8,9},{9,8},{10,11... | collective-permute-start | bytes 24584 | tf_op jit(solution)/shard_map/ppermute | solution.py:389
  85.5 1.6 %collective-permute-done.9 = f32[16,128]{1,0:T(8,128)S(1)} collective-permute-done((f32[16,128]{1,0:T(8,128)S(1)}, f32[16,128]{1,0:T(8,128)S(1)}, u32[]{:S(2)}, u32[]{:S(2)}) %collective-permute-start.9) | collective-permute-done | bytes 8224 | tf_op jit(solution)/shard_map/ppermute | solution.py:389
  87.1 3.4 %collective-permute-start.14 = (f32[16,128]{1,0:T(8,128)S(1)}, f32[16,128]{1,0:T(8,128)S(1)}, u32[]{:S(2)}, u32[]{:S(2)}) collective-permute-start(f32[16,128]{1,0:T(8,128)S(1)} %add_add_fusion.refs_0_), channel_id=1, source_target_pairs={{0,20},{1,21},{2,22},{3,23},{4,16},{5,17},{6,18},{7,19},{16,4},{17... | collective-permute-start | bytes 24584 | tf_op jit(solution)/shard_map/ppermute | solution.py:399
  91.5 0.8 shard_map.59.refs_0_
  93.1 0.8 shard_map.62.refs_0_
  94.7 0.9 collective-permute-done.12.refs_1_
  95.6 4.8 %shard_map.65 = (f32[6144,128]{1,0:T(8,128)}, f32[2,2,2,16,16]{4,3,2,1,0:T(8,128)}) custom-call(s32[3]{0:T(128)S(1)} %pad_add_fusion.pick_ref.slot_ref, f32[16,128]{1,0:T(8,128)S(1)} %add_add_fusion.refs_0_, f32[16,128]{1,0:T(8,128)S(1)} %collective-permute-done.12.refs_1_, f32[3072,128]{1,0:T(8,128)S(1)} %shard_map.61.refs_2_, ...), custom_call_target="tpu_custom_call" | custom-call | flops 1000000 | bytes 6332416 | tf_op jit(solution)/shard_map/pallas_call | solution.py:45
  (36 shorter events, 6.9 us)
Async XLA Ops:
  1.7 9.5 %collective-permute-start = (f32[54,4,512]{2,1,0:T(4,128)S(1)}, f32[54,4,512]{2,1,0:T(4,128)S(1)}, u32[]{:S(2)}, u32[]{:S(2)}) collective-permute-start(f32[54,4,512]{2,1,0:T(4,128)S(1)} %dynamic-slice_bitcast_fusion), channel_id=1, source_target_pairs={{0,8},{8,0},{1,9},{9,1},{2,10},{10,2},{3,11},{11,3},{4,12},{12,4},... | collective-permute-start | bytes 1327112 | tf_op jit(solution)/shard_map/ppermute | solution.py:389
  2.3 1.9 %copy-start = (f32[2,16,2,3,4,1024]{5,4,3,2,1,0:T(4,128)S(1)}, f32[2,16,2,3,4,1024]{5,4,3,2,1,0:T(4,128)}, u32[]{:S(2)}) copy-start(f32[2,16,2,3,4,1024]{5,4,3,2,1,0:T(4,128)} %param.3) | copy-start | bytes 9437188
  4.2 7.0 %copy-start.1 = (f32[4,3,2,3,3,4,512]{6,5,4,3,2,1,0:T(4,128)S(1)}, f32[4,3,2,3,3,4,512]{6,5,4,3,2,1,0:T(4,128)}, u32[]{:S(2)}) copy-start(f32[4,3,2,3,3,4,512]{6,5,4,3,2,1,0:T(4,128)} %param.2) | copy-start | bytes 5308420
  5.5 20.5 %collective-permute-start.4 = (f32[1,8,6,16,128]{4,3,2,1,0:T(8,128)S(1)}, f32[1,8,6,16,128]{4,3,2,1,0:T(8,128)S(1)}, u32[]{:S(2)}, u32[]{:S(2)}) collective-permute-start(f32[1,8,6,16,128]{4,3,2,1,0:T(8,128)S(1)} %get-tuple-element.21.refs_2_.refs_4_), channel_id=1, source_target_pairs={{0,1},{1,2},{2,3},{3,4},{4,5},{5,6},{6,7},{7,0},{8,9},{9,10},{10,1... | collective-permute-start | bytes 1179656 | tf_op jit(solution)/shard_map/ppermute | solution.py:385
  8.1 24.8 %collective-permute-start.2 = (f32[1,8,6,16,128]{4,3,2,1,0:T(8,128)S(1)}, f32[1,8,6,16,128]{4,3,2,1,0:T(8,128)S(1)}, u32[]{:S(2)}, u32[]{:S(2)}) collective-permute-start(f32[1,8,6,16,128]{4,3,2,1,0:T(8,128)S(1)} %get-tuple-element.17.refs_0_.refs_3_), channel_id=1, source_target_pairs={{0,7},{1,0},{2,1},{3,2},{4,3},{5,4},{6,5},{7,6},{8,15},{9,8},{10,9... | collective-permute-start | bytes 1179656 | tf_op jit(solution)/shard_map/ppermute | solution.py:385
  13.6 13.6 %collective-permute-start.1 = (f32[18,8,128]{2,1,0:T(8,128)S(1)}, f32[18,8,128]{2,1,0:T(8,128)S(1)}, u32[]{:S(2)}, u32[]{:S(2)}) collective-permute-start(f32[18,8,128]{2,1,0:T(8,128)S(1)} %get-tuple-element.16.refs_0_.links_ref), channel_id=1, source_target_pairs={{0,1},{1,2},{2,3},{3,4},{4,5},{5,6},{6,7},{7,0},{8,9},{9,10},{10,1... | collective-permute-start | bytes 221192 | tf_op jit(solution)/shard_map/ppermute | solution.py:385
  27.4 19.9 %collective-permute-start.6 = (f32[1,8,6,16,128]{4,3,2,1,0:T(8,128)S(1)}, f32[1,8,6,16,128]{4,3,2,1,0:T(8,128)S(1)}, u32[]{:S(2)}, u32[]{:S(2)}) collective-permute-start(f32[1,8,6,16,128]{4,3,2,1,0:T(8,128)S(1)} %shard_map.46.refs_0_.refs_3_), channel_id=1, source_target_pairs={{0,7},{1,0},{2,1},{3,2},{4,3},{5,4},{6,5},{7,6},{8,15},{9,8},{10,9... | collective-permute-start | bytes 1179656 | tf_op jit(solution)/shard_map/ppermute | solution.py:385
  33.2 17.6 %collective-permute-start.3 = (f32[1,8,6,16,128]{4,3,2,1,0:T(8,128)S(1)}, f32[1,8,6,16,128]{4,3,2,1,0:T(8,128)S(1)}, u32[]{:S(2)}, u32[]{:S(2)}) collective-permute-start(f32[1,8,6,16,128]{4,3,2,1,0:T(8,128)S(1)} %shard_map.45.refs_2_.refs_4_), channel_id=1, source_target_pairs={{0,1},{1,2},{2,3},{3,4},{4,5},{5,6},{6,7},{7,0},{8,9},{9,10},{10,1... | collective-permute-start | bytes 1179656 | tf_op jit(solution)/shard_map/ppermute | solution.py:385
  47.5 16.1 %collective-permute-start.7 = (f32[1,8,6,16,128]{4,3,2,1,0:T(8,128)S(1)}, f32[1,8,6,16,128]{4,3,2,1,0:T(8,128)S(1)}, u32[]{:S(2)}, u32[]{:S(2)}) collective-permute-start(f32[1,8,6,16,128]{4,3,2,1,0:T(8,128)S(1)} %shard_map.51.refs_2_), channel_id=1, source_target_pairs={{0,1},{1,2},{2,3},{3,4},{4,5},{5,6},{6,7},{7,0},{8,9},{9,10},{10,1... | collective-permute-start | bytes 1179656 | tf_op jit(solution)/shard_map/ppermute | solution.py:385
  54.3 36.8 %collective-permute-start.17 = (f32[2,8,6,16,128]{4,3,2,1,0:T(8,128)S(1)}, f32[2,8,6,16,128]{4,3,2,1,0:T(8,128)S(1)}, u32[]{:S(2)}, u32[]{:S(2)}) collective-permute-start(f32[2,8,6,16,128]{4,3,2,1,0:T(8,128)S(1)} %shard_map.55.refs_0_.refs_1_.piece_ref), channel_id=1, source_target_pairs={{0,16},{16,0},{1,17},{17,1},{2,18},{18,2},{3,19},{19,3},{4,20},{20... | collective-permute-start | bytes 2359304 | tf_op jit(solution)/shard_map/ppermute | solution.py:389
  55.8 13.0 %collective-permute-start.5 = (f32[1,8,6,16,128]{4,3,2,1,0:T(8,128)S(1)}, f32[1,8,6,16,128]{4,3,2,1,0:T(8,128)S(1)}, u32[]{:S(2)}, u32[]{:S(2)}) collective-permute-start(f32[1,8,6,16,128]{4,3,2,1,0:T(8,128)S(1)} %shard_map.49.refs_0_), channel_id=1, source_target_pairs={{0,7},{1,0},{2,1},{3,2},{4,3},{5,4},{6,5},{7,6},{8,15},{9,8},{10,9... | collective-permute-start | bytes 1179656 | tf_op jit(solution)/shard_map/ppermute | solution.py:385
  63.8 13.1 %collective-permute-start.8 = (f32[1,8,6,16,128]{4,3,2,1,0:T(8,128)S(1)}, f32[1,8,6,16,128]{4,3,2,1,0:T(8,128)S(1)}, u32[]{:S(2)}, u32[]{:S(2)}) collective-permute-start(f32[1,8,6,16,128]{4,3,2,1,0:T(8,128)S(1)} %shard_map.54.refs_0_.piece_ref), channel_id=1, source_target_pairs={{0,7},{1,0},{2,1},{3,2},{4,3},{5,4},{6,5},{7,6},{8,15},{9,8},{10,9... | collective-permute-start | bytes 1179656 | tf_op jit(solution)/shard_map/ppermute | solution.py:385
  64.2 29.7 %collective-permute-start.16 = (f32[1,8,6,16,128]{4,3,2,1,0:T(8,128)S(1)}, f32[1,8,6,16,128]{4,3,2,1,0:T(8,128)S(1)}, u32[]{:S(2)}, u32[]{:S(2)}) collective-permute-start(f32[1,8,6,16,128]{4,3,2,1,0:T(8,128)S(1)} %shard_map.54.refs_0_.piece_ref), channel_id=1, source_target_pairs={{0,16},{16,0},{1,17},{17,1},{2,18},{18,2},{3,19},{19,3},{4,20},{20... | collective-permute-start | bytes 1179656 | tf_op jit(solution)/shard_map/ppermute | solution.py:389
  69.0 25.3 %collective-permute-start.15 = (f32[1,8,6,16,128]{4,3,2,1,0:T(8,128)S(1)}, f32[1,8,6,16,128]{4,3,2,1,0:T(8,128)S(1)}, u32[]{:S(2)}, u32[]{:S(2)}) collective-permute-start(f32[1,8,6,16,128]{4,3,2,1,0:T(8,128)S(1)} %shard_map.53.refs_2_.top_ref.piece_ref), channel_id=1, source_target_pairs={{0,16},{16,0},{1,17},{17,1},{2,18},{18,2},{3,19},{19,3},{4,20},{20... | collective-permute-start | bytes 1179656 | tf_op jit(solution)/shard_map/ppermute | solution.py:389
  77.9 5.6 %collective-permute-start.11 = (f32[16,128]{1,0:T(8,128)S(1)}, f32[16,128]{1,0:T(8,128)S(1)}, u32[]{:S(2)}, u32[]{:S(2)}) collective-permute-start(f32[16,128]{1,0:T(8,128)S(1)} %shard_map.58), channel_id=1, source_target_pairs={{0,3},{1,2},{2,1},{3,0},{4,7},{5,6},{6,5},{7,4},{8,11},{9,10},{10,... | collective-permute-start | bytes 24584 | tf_op jit(solution)/shard_map/ppermute | solution.py:389
  81.8 3.7 %collective-permute-start.10 = (f32[16,128]{1,0:T(8,128)S(1)}, f32[16,128]{1,0:T(8,128)S(1)}, u32[]{:S(2)}, u32[]{:S(2)}) collective-permute-start(f32[16,128]{1,0:T(8,128)S(1)} %shard_map.58), channel_id=1, source_target_pairs={{0,2},{1,3},{2,0},{3,1},{4,6},{5,7},{6,4},{7,5},{8,10},{9,11},{10,... | collective-permute-start | bytes 24584 | tf_op jit(solution)/shard_map/ppermute | solution.py:389
  83.4 3.7 %collective-permute-start.9 = (f32[16,128]{1,0:T(8,128)S(1)}, f32[16,128]{1,0:T(8,128)S(1)}, u32[]{:S(2)}, u32[]{:S(2)}) collective-permute-start(f32[16,128]{1,0:T(8,128)S(1)} %shard_map.58), channel_id=1, source_target_pairs={{0,1},{1,0},{2,3},{3,2},{4,5},{5,4},{6,7},{7,6},{8,9},{9,8},{10,11... | collective-permute-start | bytes 24584 | tf_op jit(solution)/shard_map/ppermute | solution.py:389
  87.1 7.6 %collective-permute-start.14 = (f32[16,128]{1,0:T(8,128)S(1)}, f32[16,128]{1,0:T(8,128)S(1)}, u32[]{:S(2)}, u32[]{:S(2)}) collective-permute-start(f32[16,128]{1,0:T(8,128)S(1)} %add_add_fusion.refs_0_), channel_id=1, source_target_pairs={{0,20},{1,21},{2,22},{3,23},{4,16},{5,17},{6,18},{7,19},{16,4},{17... | collective-permute-start | bytes 24584 | tf_op jit(solution)/shard_map/ppermute | solution.py:399
  90.5 4.2 %collective-permute-start.13 = (f32[16,128]{1,0:T(8,128)S(1)}, f32[16,128]{1,0:T(8,128)S(1)}, u32[]{:S(2)}, u32[]{:S(2)}) collective-permute-start(f32[16,128]{1,0:T(8,128)S(1)} %add_add_fusion.refs_0_), channel_id=1, source_target_pairs={{0,16},{1,17},{2,18},{3,19},{4,20},{5,21},{6,22},{7,23},{16,0},{17... | collective-permute-start | bytes 24584 | tf_op jit(solution)/shard_map/ppermute | solution.py:399
  91.0 4.6 %collective-permute-start.12 = (f32[16,128]{1,0:T(8,128)S(1)}, f32[16,128]{1,0:T(8,128)S(1)}, u32[]{:S(2)}, u32[]{:S(2)}) collective-permute-start(f32[16,128]{1,0:T(8,128)S(1)} %add_add_fusion.refs_0_), channel_id=1, source_target_pairs={{0,4},{1,5},{2,6},{3,7},{4,0},{5,1},{6,2},{7,3},{8,12},{9,13},{10,... | collective-permute-start | bytes 24584 | tf_op jit(solution)/shard_map/ppermute | solution.py:389

commit v2 on v1

--- a/solution.py
+++ b/solution.py
@@ -106,10 +106,10 @@
     lax.fori_loop(0, rows, body, 0)
 
 
-def ends_kernel(depth, pieces, pick_ref, far_ref, raw_ref, *refs):
-    *out_refs, sems = refs
+def planes_kernel(depth, pieces, pick_ref, far_ref, *refs):
+    *out_refs, raw_ref, sems = refs
     out = plane_refs(out_refs, pieces)
-    rows, _, vecs, _ = out[0].shape
+    rows, _, vecs, _ = out[pieces[0][0]].shape
     size = raw_ref.shape[0]
     parts = 2
     copies = []
@@ -121,12 +121,6 @@
     for k in range(parts):
         copies[k].wait()
         take_planes(out, raw_ref, k * (vecs // parts), vecs // parts, rows, depth)
-
-
-def rest_kernel(depth, pieces, raw_ref, *out_refs):
-    out = plane_refs(out_refs, pieces)
-    rows, _, vecs, _ = out[pieces[0][0]].shape
-    take_planes(out, raw_ref, 0, vecs, rows, depth)
 
 
 def link_kernel(depth, half, pick_ref, far_ref, came_ref, table_ref, behind_ref, top_ref, sem):
@@ -367,7 +361,7 @@
 
             lax.fori_loop(0, each, body, 0)
 
-        @pl.when(step == (k + 1) * steps - 2)
+        @pl.when(step == k * steps)
         def _(n=n, slot=slot, normalised=normalised):
             packed, norm, down = normalised()
             across = lax.rsqrt(jnp.sum(norm, axis=0, keepdims=True)[:, 0:n])
@@ -424,28 +418,27 @@
     half = rows // 2
     sem = pltpu.SemaphoreType.DMA
 
-    raw, *got = call(
-        functools.partial(ends_kernel, depth, [pieces[k] for k in ends]),
-        [shape_of(many, LANES)] + [field[k] for k in ends],
-        to_rows(vectors), pick=pick, far=(0,), scratch=[sem((2,))], ops=1e5,
-    )
+    view = pltpu.with_memory_space_constraint(to_rows(vectors), pltpu.HBM)
+
+    def taken(todo):
+        return call(
+            functools.partial(planes_kernel, depth, [pieces[k] for k in todo]), [field[k] for k in todo],
+            view, pick=pick, far=(0,), scratch=[pltpu.VMEM((many, LANES), F32), sem((2,))], ops=1e5,
+        )
+
     start = [None] * len(pieces)
-    for k, x in zip(ends, got):
+    for k, x in zip(ends, taken(ends)):
         start[k] = x
     flat = links.reshape((links.shape[0], 54) + links.shape[-2:])
     given = lax.dynamic_index_in_dim(flat, 2 * (1 - core) + mine, 0, keepdims=False)
     came = flipped(given, "ta", 1)
     if inner:
-        got = call(
-            functools.partial(rest_kernel, depth, [pieces[k] for k in inner]),
-            [field[k] for k in inner], raw, ops=1e5,
-        )
-        for k, x in zip(inner, got):
+        for k, x in zip(inner, taken(inner)):
             start[k] = x
     table, behind, top_links = call(
         functools.partial(link_kernel, depth, half),
         [shape_of(2, 54, half * depth, LANES), shape_of(2, 36, half * depth, LANES), shape_of(18, rows, LANES)],
-        to_rows(links).reshape(-1, 54, half * depth, LANES),
+        pltpu.with_memory_space_constraint(to_rows(links).reshape(-1, 54, half * depth, LANES), pltpu.HBM),
         to_rows(came).reshape(54, half * depth, LANES),
         pick=pick, far=(0,), scratch=[sem], ops=1e6,
     )
@@ -517,7 +510,7 @@
             )
         return out
 
-    steps = 4
+    steps = 1
     assert vecs % steps == 0
 
     def target(step, pick):

time: 101 us -> 98 us (0.970)
  waiting for transfers between devices: 25.4 us -> 23.1 us
  local copies, waits for them, and re-layouts: 2.94 us -> 1.05 us
  Pallas kernels: 40.6 us -> 42.1 us
    ppermute x8, waiting for transfers between devices: 21.6 us -> 19.3 us  [shifted(): return lax.ppermute(x, axis, [(i, (i + by) % n) for i in range(n)])]
    pallas_call x3 -> x4, Pallas kernels: 8.47 us -> 10.7 us  [call(): return pl.pallas_call(kernel, grid_spec=spec, **params)(pick, *args)]
    unnamed x4 -> x0, local copies, waits for them, and re-layouts: 1.89 us -> none
    pallas_call x22 -> x21, Pallas kernels: 32.2 us -> 31.5 us  [call(): pl.pallas_call(kernel, in_specs=in_specs, out_specs=out_specs, scratch_sh...]
  transfers between devices with their start and end apart: 18 -> 18, of which waited for: 8 -> 8; matrix products, arithmetic and copies ran while one was open for 0% -> 0% of each run, Pallas kernels for 36% -> 40%
where the time goes in v2:
time: 98 us; the launch traced here: 97.7 us
  Pallas kernels  42.1 us (43%)
  starting transfers between devices  30.5 us (31%)
  waiting for transfers between devices  23.1 us (24%)
  local copies, waits for them, and re-layouts  1.05 us (1%)
    pallas_call x21, Pallas kernels, call(): pl.pallas_call(kernel, in_specs=in_specs, out_specs=out_specs, scratch_sh...  31.5 us
    ppermute x8, waiting for transfers between devices, shifted(): return lax.ppermute(x, axis, [(i, (i + by) % n) for i in range(n)])  19.3 us
    ppermute x8, starting transfers between devices, shifted(): return lax.ppermute(x, axis, [(i, (i + by) % n) for i in range(n)])  16.5 us
    pallas_call x4, Pallas kernels, call(): return pl.pallas_call(kernel, grid_spec=spec, **params)(pick, *args)  10.7 us
    ppermute x8, starting transfers between devices, flipped(): lax.ppermute(x, axis, [(i, i ^ bit) for i in range(lax.axis_size(axis))])  9.99 us
    ppermute x2, starting transfers between devices, across(): lax.ppermute(x, ('cfg', 'sa'), [(i, i ^ cfg * size + bits) for i in pairs])  3.94 us
    ppermute x8, waiting for transfers between devices, flipped(): lax.ppermute(x, axis, [(i, i ^ bit) for i in range(lax.axis_size(axis))])  3.8 us
  transfers between devices with their start and end apart: 18, of which 8 were waited for; matrix products, arithmetic and copies ran while one was open for 0% of the time, Pallas kernels for 40%

profile of v2, /device:TPU:0, one launch (start us, length us, event | category | flops | bytes accessed | tf_op | source)
XLA Modules:
  0.0 97.7 jit_solution(16129445936665995729)
XLA Ops:
  0.6 1.0 %dynamic-slice_bitcast_fusion = f32[54,4,512]{2,1,0:T(4,128)S(1)} fusion(f32[4,54,4,512]{3,2,1,0:T(4,128)} %bitcast.29, s32[]{:T(128)S(6)} %select_n.12), kind=kLoop, calls=%fused_computation | loop fusion | bytes 884740 | tf_op jit(solution)/shard_map/jit(dynamic_index_in_dim)/squeeze | solution.py:433
  2.3 2.3 %shard_map.42 = (f32[1,8,6,16,128]{4,3,2,1,0:T(8,128)S(1)}, f32[1,8,6,16,128]{4,3,2,1,0:T(8,128)S(1)}) custom-call(s32[3]{0:T(128)S(1)} %pad_add_fusion.pick_ref.slot_ref, f32[6144,128]{1,0:T(8,128)} %bitcast.27), custom_call_target="tpu_custom_call" | custom-call | flops 100000 | bytes 3932160 | tf_op jit(solution)/shard_map/pallas_call | solution.py:45
  4.6 2.6 %collective-permute-start.4 = (f32[1,8,6,16,128]{4,3,2,1,0:T(8,128)S(1)}, f32[1,8,6,16,128]{4,3,2,1,0:T(8,128)S(1)}, u32[]{:S(2)}, u32[]{:S(2)}) collective-permute-start(f32[1,8,6,16,128]{4,3,2,1,0:T(8,128)S(1)} %get-tuple-element.19.refs_2_.refs_4_), channel_id=1, source_target_pairs={{0,1},{1,2},{2,3},{3,4},{4,5},{5,6},{6,7},{7,0},{8,9},{9,10},{10,1... | collective-permute-start | bytes 1179656 | tf_op jit(solution)/shard_map/ppermute | solution.py:379
  7.2 3.1 %collective-permute-start.2 = (f32[1,8,6,16,128]{4,3,2,1,0:T(8,128)S(1)}, f32[1,8,6,16,128]{4,3,2,1,0:T(8,128)S(1)}, u32[]{:S(2)}, u32[]{:S(2)}) collective-permute-start(f32[1,8,6,16,128]{4,3,2,1,0:T(8,128)S(1)} %get-tuple-element.16.refs_0_.refs_3_), channel_id=1, source_target_pairs={{0,7},{1,0},{2,1},{3,2},{4,3},{5,4},{6,5},{7,6},{8,15},{9,8},{10,9... | collective-permute-start | bytes 1179656 | tf_op jit(solution)/shard_map/ppermute | solution.py:379
  10.3 3.1 %shard_map.41 = (f32[2,54,16,128]{3,2,1,0:T(8,128)S(1)}, f32[2,36,16,128]{3,2,1,0:T(8,128)S(1)}, f32[18,8,128]{2,1,0:T(8,128)S(1)}) custom-call(s32[3]{0:T(128)S(1)} %pad_add_fusion.pick_ref.slot_ref, f32[4,54,16,128]{3,2,1,0:T(8,128)} %bitcast.30, f32[54,16,128]{2,1,0:T(8,128)S(1)} %bitcast.26), custom_call_target="tpu_custom_call" | custom-call | flops 1000000 | bytes 3760128 | tf_op jit(solution)/shard_map/pallas_call | solution.py:45
  13.5 2.3 %shard_map.43.refs_1_.refs_3_ = f32[2,8,6,16,128]{4,3,2,1,0:T(8,128)S(1)} custom-call(s32[3]{0:T(128)S(1)} %pad_add_fusion.pick_ref.slot_ref, f32[6144,128]{1,0:T(8,128)} %bitcast.28), custom_call_target="tpu_custom_call" | custom-call | flops 100000 | bytes 3932160 | tf_op jit(solution)/shard_map/pallas_call | solution.py:45
  15.8 3.0 %shard_map.44 = (f32[1,8,6,16,128]{4,3,2,1,0:T(8,128)S(1)}, f32[1,8,6,16,128]{4,3,2,1,0:T(8,128)S(1)}) custom-call(f32[2,54,16,128]{3,2,1,0:T(8,128)S(1)} %get-tuple-element.17.table_ref, f32[2,36,16,128]{3,2,1,0:T(8,128)S(1)} %get-tuple-element.18.behind_ref, f32[1,8,6,16,128]{4,3,2,1,0:T(8,128)S(1)} %get-tuple-element.16.refs_0_.refs_3_, ...), custom_call_target="tpu_custom_call" | custom-call | flops 32768000 | bytes 3833856 | tf_op jit(solution)/shard_map/pallas_call | solution.py:37
  18.8 6.3 %collective-permute-done.4.refs_1_ = f32[1,8,6,16,128]{4,3,2,1,0:T(8,128)S(1)} collective-permute-done((f32[1,8,6,16,128]{4,3,2,1,0:T(8,128)S(1)}, f32[1,8,6,16,128]{4,3,2,1,0:T(8,128)S(1)}, u32[]{:S(2)}, u32[]{:S(2)}) %collective-permute-start.4) | collective-permute-done | bytes 393248 | tf_op jit(solution)/shard_map/ppermute | solution.py:379
  25.1 1.1 %collective-permute-done.1.refs_0_ = f32[18,8,128]{2,1,0:T(8,128)S(1)} collective-permute-done((f32[18,8,128]{2,1,0:T(8,128)S(1)}, f32[18,8,128]{2,1,0:T(8,128)S(1)}, u32[]{:S(2)}, u32[]{:S(2)}) %collective-permute-start.1) | collective-permute-done | bytes 73760 | tf_op jit(solution)/shard_map/ppermute | solution.py:379
  26.5 5.6 %collective-permute-start.6 = (f32[1,8,6,16,128]{4,3,2,1,0:T(8,128)S(1)}, f32[1,8,6,16,128]{4,3,2,1,0:T(8,128)S(1)}, u32[]{:S(2)}, u32[]{:S(2)}) collective-permute-start(f32[1,8,6,16,128]{4,3,2,1,0:T(8,128)S(1)} %shard_map.46.refs_0_.refs_3_), channel_id=1, source_target_pairs={{0,7},{1,0},{2,1},{3,2},{4,3},{5,4},{6,5},{7,6},{8,15},{9,8},{10,9... | collective-permute-start | bytes 1179656 | tf_op jit(solution)/shard_map/ppermute | solution.py:379
  32.3 3.2 %shard_map.47.refs_1_.refs_3_ = f32[2,8,6,16,128]{4,3,2,1,0:T(8,128)S(1)} custom-call(f32[2,54,16,128]{3,2,1,0:T(8,128)S(1)} %get-tuple-element.17.table_ref, f32[2,36,16,128]{3,2,1,0:T(8,128)S(1)} %get-tuple-element.18.behind_ref, f32[1,8,6,16,128]{4,3,2,1,0:T(8,128)S(1)} %get-tuple-element.16.refs_0_.refs_3_, ...), custom_call_target="tpu_custom_call" | custom-call | flops 32768000 | bytes 3833856 | tf_op jit(solution)/shard_map/pallas_call | solution.py:37
  35.5 3.0 %shard_map.48 = (f32[1,8,6,16,128]{4,3,2,1,0:T(8,128)S(1)}, f32[1,8,6,16,128]{4,3,2,1,0:T(8,128)S(1)}) custom-call(f32[2,54,16,128]{3,2,1,0:T(8,128)S(1)} %get-tuple-element.17.table_ref, f32[2,36,16,128]{3,2,1,0:T(8,128)S(1)} %get-tuple-element.18.behind_ref, f32[1,8,6,16,128]{4,3,2,1,0:T(8,128)S(1)} %shard_map.46.refs_0_.refs_3_, ...), custom_call_target="tpu_custom_call" | custom-call | flops 32768000 | bytes 4620288 | tf_op jit(solution)/shard_map/pallas_call | solution.py:37
  38.6 7.8 %collective-permute-done.6.refs_1_ = f32[1,8,6,16,128]{4,3,2,1,0:T(8,128)S(1)} collective-permute-done((f32[1,8,6,16,128]{4,3,2,1,0:T(8,128)S(1)}, f32[1,8,6,16,128]{4,3,2,1,0:T(8,128)S(1)}, u32[]{:S(2)}, u32[]{:S(2)}) %collective-permute-start.6) | collective-permute-done | bytes 393248 | tf_op jit(solution)/shard_map/ppermute | solution.py:379
  46.6 3.2 %shard_map.50.refs_1_ = f32[2,8,6,16,128]{4,3,2,1,0:T(8,128)S(1)} custom-call(f32[2,54,16,128]{3,2,1,0:T(8,128)S(1)} %get-tuple-element.17.table_ref, f32[2,36,16,128]{3,2,1,0:T(8,128)S(1)} %get-tuple-element.18.behind_ref, f32[1,8,6,16,128]{4,3,2,1,0:T(8,128)S(1)} %shard_map.46.refs_0_.refs_3_, f32[2,8,6,16,128]{4,3,2,1,0:T(8,128)S(1)} %shard_map.47.refs_1_.refs_3_, ...), custom_call_target="tpu_custom_call" | custom-call | flops 32768000 | bytes 4620288 | tf_op jit(solution)/shard_map/pallas_call | solution.py:37
  50.1 3.2 %shard_map.55.refs_0_.refs_1_.piece_ref = f32[2,8,6,16,128]{4,3,2,1,0:T(8,128)S(1)} custom-call(f32[2,54,16,128]{3,2,1,0:T(8,128)S(1)} %get-tuple-element.17.table_ref, f32[2,36,16,128]{3,2,1,0:T(8,128)S(1)} %get-tuple-element.18.behind_ref, f32[1,8,6,16,128]{4,3,2,1,0:T(8,128)S(1)} %shard_map.49.refs_0_, f32[2,8,6,16,128]{4,3,2,1,0:T(8,128)S(1)} %shard_map.50.refs_1_, ...), custom_call_target="tpu_custom_call" | custom-call | flops 32768000 | bytes 4620288 | tf_op jit(solution)/shard_map/pallas_call | solution.py:37
  53.4 1.6 %collective-permute-start.17 = (f32[2,8,6,16,128]{4,3,2,1,0:T(8,128)S(1)}, f32[2,8,6,16,128]{4,3,2,1,0:T(8,128)S(1)}, u32[]{:S(2)}, u32[]{:S(2)}) collective-permute-start(f32[2,8,6,16,128]{4,3,2,1,0:T(8,128)S(1)} %shard_map.55.refs_0_.refs_1_.piece_ref), channel_id=1, source_target_pairs={{0,16},{16,0},{1,17},{17,1},{2,18},{18,2},{3,19},{19,3},{4,20},{20... | collective-permute-start | bytes 2359304 | tf_op jit(solution)/shard_map/ppermute | solution.py:383
  54.9 4.7 %collective-permute-start.5 = (f32[1,8,6,16,128]{4,3,2,1,0:T(8,128)S(1)}, f32[1,8,6,16,128]{4,3,2,1,0:T(8,128)S(1)}, u32[]{:S(2)}, u32[]{:S(2)}) collective-permute-start(f32[1,8,6,16,128]{4,3,2,1,0:T(8,128)S(1)} %shard_map.49.refs_0_), channel_id=1, source_target_pairs={{0,7},{1,0},{2,1},{3,2},{4,3},{5,4},{6,5},{7,6},{8,15},{9,8},{10,9... | collective-permute-start | bytes 1179656 | tf_op jit(solution)/shard_map/ppermute | solution.py:379
  59.6 3.0 %shard_map.52 = (f32[1,8,6,16,128]{4,3,2,1,0:T(8,128)S(1)}, f32[1,8,6,16,128]{4,3,2,1,0:T(8,128)S(1)}) custom-call(f32[2,54,16,128]{3,2,1,0:T(8,128)S(1)} %get-tuple-element.17.table_ref, f32[2,36,16,128]{3,2,1,0:T(8,128)S(1)} %get-tuple-element.18.behind_ref, f32[1,8,6,16,128]{4,3,2,1,0:T(8,128)S(1)} %shard_map.49.refs_0_, ...), custom_call_target="tpu_custom_call" | custom-call | flops 32768000 | bytes 4620288 | tf_op jit(solution)/shard_map/pallas_call | solution.py:37
  63.9 4.1 %collective-permute-done.5.refs_1_ = f32[1,8,6,16,128]{4,3,2,1,0:T(8,128)S(1)} collective-permute-done((f32[1,8,6,16,128]{4,3,2,1,0:T(8,128)S(1)}, f32[1,8,6,16,128]{4,3,2,1,0:T(8,128)S(1)}, u32[]{:S(2)}, u32[]{:S(2)}) %collective-permute-start.5) | collective-permute-done | bytes 393248 | tf_op jit(solution)/shard_map/ppermute | solution.py:379
  68.2 0.6 collective-permute-start.15
  68.8 3.2 %shard_map.56.refs_3_ = f32[16,128]{1,0:T(8,128)S(1)} custom-call(f32[2,54,16,128]{3,2,1,0:T(8,128)S(1)} %get-tuple-element.17.table_ref, f32[2,8,6,16,128]{4,3,2,1,0:T(8,128)S(1)} %shard_map.55.refs_0_.refs_1_.piece_ref), custom_call_target="tpu_custom_call" | custom-call | flops 16384000 | bytes 1679360 | tf_op jit(solution)/shard_map/pallas_call | solution.py:37
  71.9 4.1 %shard_map.57.sofar_ref = f32[16,128]{1,0:T(8,128)S(1)} custom-call(f32[2,54,16,128]{3,2,1,0:T(8,128)S(1)} %get-tuple-element.17.table_ref, f32[1,8,6,16,128]{4,3,2,1,0:T(8,128)S(1)} %shard_map.54.refs_0_.piece_ref, f32[2,8,6,16,128]{4,3,2,1,0:T(8,128)S(1)} %shard_map.55.refs_0_.refs_1_.piece_ref, ...), custom_call_target="tpu_custom_call" | custom-call | flops 24576000 | bytes 2473984 | tf_op jit(solution)/shard_map/pallas_call | solution.py:37
  76.0 1.0 %shard_map.58 = f32[16,128]{1,0:T(8,128)S(1)} custom-call(f32[18,8,128]{2,1,0:T(8,128)S(1)} %get-tuple-element.15.refs_0_.links_ref, f32[1,8,6,16,128]{4,3,2,1,0:T(8,128)S(1)} %shard_map.53.refs_2_.top_ref.piece_ref, f32[1,8,6,16,128]{4,3,2,1,0:T(8,128)S(1)} %collective-permute-done.8.above_ref, f32[16,128]{1,0:T(8,128)S(1)} %shard_map.57.sofar_ref), custom_call_target="tpu_custom_call" | custom-call | flops 4096000 | bytes 876544 | tf_op jit(solution)/shard_map/pallas_call | solution.py:37
  77.0 3.9 %collective-permute-start.11 = (f32[16,128]{1,0:T(8,128)S(1)}, f32[16,128]{1,0:T(8,128)S(1)}, u32[]{:S(2)}, u32[]{:S(2)}) collective-permute-start(f32[16,128]{1,0:T(8,128)S(1)} %shard_map.58), channel_id=1, source_target_pairs={{0,3},{1,2},{2,1},{3,0},{4,7},{5,6},{6,5},{7,4},{8,11},{9,10},{10,... | collective-permute-start | bytes 24584 | tf_op jit(solution)/shard_map/ppermute | solution.py:383
  81.4 1.2 %collective-permute-done.11 = f32[16,128]{1,0:T(8,128)S(1)} collective-permute-done((f32[16,128]{1,0:T(8,128)S(1)}, f32[16,128]{1,0:T(8,128)S(1)}, u32[]{:S(2)}, u32[]{:S(2)}) %collective-permute-start.11) | collective-permute-done | bytes 8224 | tf_op jit(solution)/shard_map/ppermute | solution.py:383
  82.6 1.9 %collective-permute-start.9 = (f32[16,128]{1,0:T(8,128)S(1)}, f32[16,128]{1,0:T(8,128)S(1)}, u32[]{:S(2)}, u32[]{:S(2)}) collective-permute-start(f32[16,128]{1,0:T(8,128)S(1)} %shard_map.58), channel_id=1, source_target_pairs={{0,1},{1,0},{2,3},{3,2},{4,5},{5,4},{6,7},{7,6},{8,9},{9,8},{10,11... | collective-permute-start | bytes 24584 | tf_op jit(solution)/shard_map/ppermute | solution.py:383
  84.6 1.6 %collective-permute-done.9 = f32[16,128]{1,0:T(8,128)S(1)} collective-permute-done((f32[16,128]{1,0:T(8,128)S(1)}, f32[16,128]{1,0:T(8,128)S(1)}, u32[]{:S(2)}, u32[]{:S(2)}) %collective-permute-start.9) | collective-permute-done | bytes 8224 | tf_op jit(solution)/shard_map/ppermute | solution.py:383
  86.2 3.4 %collective-permute-start.14 = (f32[16,128]{1,0:T(8,128)S(1)}, f32[16,128]{1,0:T(8,128)S(1)}, u32[]{:S(2)}, u32[]{:S(2)}) collective-permute-start(f32[16,128]{1,0:T(8,128)S(1)} %add_add_fusion.refs_0_), channel_id=1, source_target_pairs={{0,20},{1,21},{2,22},{3,23},{4,16},{5,17},{6,18},{7,19},{16,4},{17... | collective-permute-start | bytes 24584 | tf_op jit(solution)/shard_map/ppermute | solution.py:393
  90.6 0.8 shard_map.59.refs_0_
  92.2 0.8 shard_map.62.refs_0_
  93.9 0.9 collective-permute-done.12.refs_1_
  94.7 3.0 %shard_map.65 = (f32[6144,128]{1,0:T(8,128)}, f32[2,2,2,16,16]{4,3,2,1,0:T(8,128)}) custom-call(s32[3]{0:T(128)S(1)} %pad_add_fusion.pick_ref.slot_ref, f32[16,128]{1,0:T(8,128)S(1)} %add_add_fusion.refs_0_, f32[16,128]{1,0:T(8,128)S(1)} %collective-permute-done.12.refs_1_, f32[3072,128]{1,0:T(8,128)S(1)} %shard_map.61.refs_2_, ...), custom_call_target="tpu_custom_call" | custom-call | flops 1000000 | bytes 6332416 | tf_op jit(solution)/shard_map/pallas_call | solution.py:45
  (32 shorter events, 6.3 us)
Async XLA Ops:
  1.7 8.6 %collective-permute-start = (f32[54,4,512]{2,1,0:T(4,128)S(1)}, f32[54,4,512]{2,1,0:T(4,128)S(1)}, u32[]{:S(2)}, u32[]{:S(2)}) collective-permute-start(f32[54,4,512]{2,1,0:T(4,128)S(1)} %dynamic-slice_bitcast_fusion), channel_id=1, source_target_pairs={{0,8},{8,0},{1,9},{9,1},{2,10},{10,2},{3,11},{11,3},{4,12},{12,4},... | collective-permute-start | bytes 1327112 | tf_op jit(solution)/shard_map/ppermute | solution.py:383
  4.6 20.5 %collective-permute-start.4 = (f32[1,8,6,16,128]{4,3,2,1,0:T(8,128)S(1)}, f32[1,8,6,16,128]{4,3,2,1,0:T(8,128)S(1)}, u32[]{:S(2)}, u32[]{:S(2)}) collective-permute-start(f32[1,8,6,16,128]{4,3,2,1,0:T(8,128)S(1)} %get-tuple-element.19.refs_2_.refs_4_), channel_id=1, source_target_pairs={{0,1},{1,2},{2,3},{3,4},{4,5},{5,6},{6,7},{7,0},{8,9},{9,10},{10,1... | collective-permute-start | bytes 1179656 | tf_op jit(solution)/shard_map/ppermute | solution.py:379
  7.2 24.8 %collective-permute-start.2 = (f32[1,8,6,16,128]{4,3,2,1,0:T(8,128)S(1)}, f32[1,8,6,16,128]{4,3,2,1,0:T(8,128)S(1)}, u32[]{:S(2)}, u32[]{:S(2)}) collective-permute-start(f32[1,8,6,16,128]{4,3,2,1,0:T(8,128)S(1)} %get-tuple-element.16.refs_0_.refs_3_), channel_id=1, source_target_pairs={{0,7},{1,0},{2,1},{3,2},{4,3},{5,4},{6,5},{7,6},{8,15},{9,8},{10,9... | collective-permute-start | bytes 1179656 | tf_op jit(solution)/shard_map/ppermute | solution.py:379
  13.4 12.8 %collective-permute-start.1 = (f32[18,8,128]{2,1,0:T(8,128)S(1)}, f32[18,8,128]{2,1,0:T(8,128)S(1)}, u32[]{:S(2)}, u32[]{:S(2)}) collective-permute-start(f32[18,8,128]{2,1,0:T(8,128)S(1)} %get-tuple-element.15.refs_0_.links_ref), channel_id=1, source_target_pairs={{0,1},{1,2},{2,3},{3,4},{4,5},{5,6},{6,7},{7,0},{8,9},{9,10},{10,1... | collective-permute-start | bytes 221192 | tf_op jit(solution)/shard_map/ppermute | solution.py:379
  26.5 19.9 %collective-permute-start.6 = (f32[1,8,6,16,128]{4,3,2,1,0:T(8,128)S(1)}, f32[1,8,6,16,128]{4,3,2,1,0:T(8,128)S(1)}, u32[]{:S(2)}, u32[]{:S(2)}) collective-permute-start(f32[1,8,6,16,128]{4,3,2,1,0:T(8,128)S(1)} %shard_map.46.refs_0_.refs_3_), channel_id=1, source_target_pairs={{0,7},{1,0},{2,1},{3,2},{4,3},{5,4},{6,5},{7,6},{8,15},{9,8},{10,9... | collective-permute-start | bytes 1179656 | tf_op jit(solution)/shard_map/ppermute | solution.py:379
  32.3 17.6 %collective-permute-start.3 = (f32[1,8,6,16,128]{4,3,2,1,0:T(8,128)S(1)}, f32[1,8,6,16,128]{4,3,2,1,0:T(8,128)S(1)}, u32[]{:S(2)}, u32[]{:S(2)}) collective-permute-start(f32[1,8,6,16,128]{4,3,2,1,0:T(8,128)S(1)} %shard_map.45.refs_2_.refs_4_), channel_id=1, source_target_pairs={{0,1},{1,2},{2,3},{3,4},{4,5},{5,6},{6,7},{7,0},{8,9},{9,10},{10,1... | collective-permute-start | bytes 1179656 | tf_op jit(solution)/shard_map/ppermute | solution.py:379
  46.6 16.1 %collective-permute-start.7 = (f32[1,8,6,16,128]{4,3,2,1,0:T(8,128)S(1)}, f32[1,8,6,16,128]{4,3,2,1,0:T(8,128)S(1)}, u32[]{:S(2)}, u32[]{:S(2)}) collective-permute-start(f32[1,8,6,16,128]{4,3,2,1,0:T(8,128)S(1)} %shard_map.51.refs_2_), channel_id=1, source_target_pairs={{0,1},{1,2},{2,3},{3,4},{4,5},{5,6},{6,7},{7,0},{8,9},{9,10},{10,1... | collective-permute-start | bytes 1179656 | tf_op jit(solution)/shard_map/ppermute | solution.py:379
  53.4 36.8 %collective-permute-start.17 = (f32[2,8,6,16,128]{4,3,2,1,0:T(8,128)S(1)}, f32[2,8,6,16,128]{4,3,2,1,0:T(8,128)S(1)}, u32[]{:S(2)}, u32[]{:S(2)}) collective-permute-start(f32[2,8,6,16,128]{4,3,2,1,0:T(8,128)S(1)} %shard_map.55.refs_0_.refs_1_.piece_ref), channel_id=1, source_target_pairs={{0,16},{16,0},{1,17},{17,1},{2,18},{18,2},{3,19},{19,3},{4,20},{20... | collective-permute-start | bytes 2359304 | tf_op jit(solution)/shard_map/ppermute | solution.py:383
  54.9 13.0 %collective-permute-start.5 = (f32[1,8,6,16,128]{4,3,2,1,0:T(8,128)S(1)}, f32[1,8,6,16,128]{4,3,2,1,0:T(8,128)S(1)}, u32[]{:S(2)}, u32[]{:S(2)}) collective-permute-start(f32[1,8,6,16,128]{4,3,2,1,0:T(8,128)S(1)} %shard_map.49.refs_0_), channel_id=1, source_target_pairs={{0,7},{1,0},{2,1},{3,2},{4,3},{5,4},{6,5},{7,6},{8,15},{9,8},{10,9... | collective-permute-start | bytes 1179656 | tf_op jit(solution)/shard_map/ppermute | solution.py:379
  62.9 13.1 %collective-permute-start.8 = (f32[1,8,6,16,128]{4,3,2,1,0:T(8,128)S(1)}, f32[1,8,6,16,128]{4,3,2,1,0:T(8,128)S(1)}, u32[]{:S(2)}, u32[]{:S(2)}) collective-permute-start(f32[1,8,6,16,128]{4,3,2,1,0:T(8,128)S(1)} %shard_map.54.refs_0_.piece_ref), channel_id=1, source_target_pairs={{0,7},{1,0},{2,1},{3,2},{4,3},{5,4},{6,5},{7,6},{8,15},{9,8},{10,9... | collective-permute-start | bytes 1179656 | tf_op jit(solution)/shard_map/ppermute | solution.py:379
  63.3 29.7 %collective-permute-start.16 = (f32[1,8,6,16,128]{4,3,2,1,0:T(8,128)S(1)}, f32[1,8,6,16,128]{4,3,2,1,0:T(8,128)S(1)}, u32[]{:S(2)}, u32[]{:S(2)}) collective-permute-start(f32[1,8,6,16,128]{4,3,2,1,0:T(8,128)S(1)} %shard_map.54.refs_0_.piece_ref), channel_id=1, source_target_pairs={{0,16},{16,0},{1,17},{17,1},{2,18},{18,2},{3,19},{19,3},{4,20},{20... | collective-permute-start | bytes 1179656 | tf_op jit(solution)/shard_map/ppermute | solution.py:383
  68.2 25.3 %collective-permute-start.15 = (f32[1,8,6,16,128]{4,3,2,1,0:T(8,128)S(1)}, f32[1,8,6,16,128]{4,3,2,1,0:T(8,128)S(1)}, u32[]{:S(2)}, u32[]{:S(2)}) collective-permute-start(f32[1,8,6,16,128]{4,3,2,1,0:T(8,128)S(1)} %shard_map.53.refs_2_.top_ref.piece_ref), channel_id=1, source_target_pairs={{0,16},{16,0},{1,17},{17,1},{2,18},{18,2},{3,19},{19,3},{4,20},{20... | collective-permute-start | bytes 1179656 | tf_op jit(solution)/shard_map/ppermute | solution.py:383
  77.0 5.6 %collective-permute-start.11 = (f32[16,128]{1,0:T(8,128)S(1)}, f32[16,128]{1,0:T(8,128)S(1)}, u32[]{:S(2)}, u32[]{:S(2)}) collective-permute-start(f32[16,128]{1,0:T(8,128)S(1)} %shard_map.58), channel_id=1, source_target_pairs={{0,3},{1,2},{2,1},{3,0},{4,7},{5,6},{6,5},{7,4},{8,11},{9,10},{10,... | collective-permute-start | bytes 24584 | tf_op jit(solution)/shard_map/ppermute | solution.py:383
  80.9 3.7 %collective-permute-start.10 = (f32[16,128]{1,0:T(8,128)S(1)}, f32[16,128]{1,0:T(8,128)S(1)}, u32[]{:S(2)}, u32[]{:S(2)}) collective-permute-start(f32[16,128]{1,0:T(8,128)S(1)} %shard_map.58), channel_id=1, source_target_pairs={{0,2},{1,3},{2,0},{3,1},{4,6},{5,7},{6,4},{7,5},{8,10},{9,11},{10,... | collective-permute-start | bytes 24584 | tf_op jit(solution)/shard_map/ppermute | solution.py:383
  82.6 3.7 %collective-permute-start.9 = (f32[16,128]{1,0:T(8,128)S(1)}, f32[16,128]{1,0:T(8,128)S(1)}, u32[]{:S(2)}, u32[]{:S(2)}) collective-permute-start(f32[16,128]{1,0:T(8,128)S(1)} %shard_map.58), channel_id=1, source_target_pairs={{0,1},{1,0},{2,3},{3,2},{4,5},{5,4},{6,7},{7,6},{8,9},{9,8},{10,11... | collective-permute-start | bytes 24584 | tf_op jit(solution)/shard_map/ppermute | solution.py:383
  86.2 7.6 %collective-permute-start.14 = (f32[16,128]{1,0:T(8,128)S(1)}, f32[16,128]{1,0:T(8,128)S(1)}, u32[]{:S(2)}, u32[]{:S(2)}) collective-permute-start(f32[16,128]{1,0:T(8,128)S(1)} %add_add_fusion.refs_0_), channel_id=1, source_target_pairs={{0,20},{1,21},{2,22},{3,23},{4,16},{5,17},{6,18},{7,19},{16,4},{17... | collective-permute-start | bytes 24584 | tf_op jit(solution)/shard_map/ppermute | solution.py:393
  89.6 4.2 %collective-permute-start.13 = (f32[16,128]{1,0:T(8,128)S(1)}, f32[16,128]{1,0:T(8,128)S(1)}, u32[]{:S(2)}, u32[]{:S(2)}) collective-permute-start(f32[16,128]{1,0:T(8,128)S(1)} %add_add_fusion.refs_0_), channel_id=1, source_target_pairs={{0,16},{1,17},{2,18},{3,19},{4,20},{5,21},{6,22},{7,23},{16,0},{17... | collective-permute-start | bytes 24584 | tf_op jit(solution)/shard_map/ppermute | solution.py:393
  90.2 4.6 %collective-permute-start.12 = (f32[16,128]{1,0:T(8,128)S(1)}, f32[16,128]{1,0:T(8,128)S(1)}, u32[]{:S(2)}, u32[]{:S(2)}) collective-permute-start(f32[16,128]{1,0:T(8,128)S(1)} %add_add_fusion.refs_0_), channel_id=1, source_target_pairs={{0,4},{1,5},{2,6},{3,7},{4,0},{5,1},{6,2},{7,3},{8,12},{9,13},{10,... | collective-permute-start | bytes 24584 | tf_op jit(solution)/shard_map/ppermute | solution.py:383

commit v3 on v2

--- a/solution.py
+++ b/solution.py
@@ -22,7 +22,7 @@
     return jax.ShapeDtypeStruct(dims, dtype)
 
 
-def call(kernel, outs, *args, ops=1e6, scratch=(), pick=None, far=(), place=None, grid=1, alias=None):
+def call(kernel, outs, *args, ops=1e6, scratch=(), pick=None, far=(), far_out=(), alias=None):
     size = sum(a.size * 4 for a in args) + sum(4 * o.size for o in jax.tree.leaves(outs))
     several = isinstance(outs, (list, tuple))
     params = dict(
@@ -37,10 +37,9 @@
         return pl.pallas_call(
             kernel, in_specs=in_specs, out_specs=out_specs, scratch_shapes=scratch, **params
         )(*args)
-    if place is not None:
-        out_specs = [pl.BlockSpec(*place)] + out_specs[1:]
+    out_specs = [FAR if k in far_out else VMEM for k in range(len(outs))]
     spec = pltpu.PrefetchScalarGridSpec(
-        num_scalar_prefetch=1, grid=(grid,), in_specs=in_specs, out_specs=out_specs, scratch_shapes=scratch
+        num_scalar_prefetch=1, grid=(1,), in_specs=in_specs, out_specs=out_specs, scratch_shapes=scratch
     )
     return pl.pallas_call(kernel, grid_spec=spec, **params)(pick, *args)
 
@@ -330,48 +329,42 @@
     lax.fori_loop(0, rows, body, 0)
 
 
-def final_kernel(steps, slot_ref, *refs):
-    out_ref, grams_ref, scale_ref = refs[-3:]
-    step = pl.program_id(0)
+def final_kernel(chunks, slot_ref, *refs):
+    far_ref, grams_ref, scale_ref, ready_ref, sems = refs[-5:]
+    copies = []
     for k in range(2):
         term0, term1, field_ref = refs[3 * k : 3 * k + 3]
         n = term0.shape[0]
+        size = field_ref.shape[0] // n
+        each = n // chunks
         slot = slot_ref[0] if k == 0 else 1 - slot_ref[0]
-
-        def normalised(term0=term0, term1=term1):
-            packed = term0[...] + term1[...]
-            norm = norms_of(packed)
-            return packed, norm, lax.rsqrt(jnp.sum(norm, axis=1, keepdims=True))
-
-        @pl.when(step == k * steps)
-        def _(n=n, normalised=normalised):
-            scale_ref[...] = jnp.broadcast_to(normalised()[2], (n, LANES))
-
-        @pl.when((step >= k * steps) & (step < (k + 1) * steps))
-        def _(k=k, n=n, field_ref=field_ref):
-            size = field_ref.shape[0] // n
-            each = n // steps
-
-            def body(i, _):
-                vec = (step - k * steps) * each + i
-                source = pl.ds(pl.multiple_of(vec * size, 8), size)
-                target = pl.ds(pl.multiple_of(i * size, 8), size)
-                out_ref[target, :] = field_ref[source, :] * scale_ref[pl.ds(vec, 1), :]
+        packed = term0[...] + term1[...]
+        norm = norms_of(packed)
+        down = lax.rsqrt(jnp.sum(norm, axis=1, keepdims=True))
+        scale_ref[...] = jnp.broadcast_to(down, (n, LANES))
+        for j in range(chunks):
+
+            def body(i, _, field_ref=field_ref, j=j, k=k):
+                vec = j * each + i
+                block = pl.ds(pl.multiple_of(vec * size, 8), size)
+                ready_ref[k, block, :] = field_ref[block, :] * scale_ref[pl.ds(vec, 1), :]
                 return 0
 
             lax.fori_loop(0, each, body, 0)
-
-        @pl.when(step == k * steps)
-        def _(n=n, slot=slot, normalised=normalised):
-            packed, norm, down = normalised()
-            across = lax.rsqrt(jnp.sum(norm, axis=0, keepdims=True)[:, 0:n])
-            scale = down * across
-            over_re, over_im = packed[:, 0:n], packed[:, n : 2 * n]
-            hop_re, hop_im = packed[:, 4 * n : 5 * n], packed[:, 5 * n : 6 * n]
-            grams_ref[slot, 0, 0] = over_re * scale
-            grams_ref[slot, 0, 1] = over_im * scale
-            grams_ref[slot, 1, 0] = (6.0 * over_re - (hop_re + hop_re.T)) * scale
-            grams_ref[slot, 1, 1] = (6.0 * over_im - (hop_im - hop_im.T)) * scale
+            part = pl.ds(j * each * size, each * size)
+            target = pl.ds(slot * (n * size) + j * each * size, each * size)
+            copies.append(pltpu.make_async_copy(ready_ref.at[k, part], far_ref.at[target], sems.at[k, j]))
+            copies[-1].start()
+        across = lax.rsqrt(jnp.sum(norm, axis=0, keepdims=True)[:, 0:n])
+        scale = down * across
+        over_re, over_im = packed[:, 0:n], packed[:, n : 2 * n]
+        hop_re, hop_im = packed[:, 4 * n : 5 * n], packed[:, 5 * n : 6 * n]
+        grams_ref[slot, 0, 0] = over_re * scale
+        grams_ref[slot, 0, 1] = over_im * scale
+        grams_ref[slot, 1, 0] = (6.0 * over_re - (hop_re + hop_re.T)) * scale
+        grams_ref[slot, 1, 1] = (6.0 * over_im - (hop_im - hop_im.T)) * scale
+    for copy in copies:
+        copy.wait()
 
 
 def shifted(x, axis, by):
@@ -426,14 +419,15 @@
             view, pick=pick, far=(0,), scratch=[pltpu.VMEM((many, LANES), F32), sem((2,))], ops=1e5,
         )
 
+    first, rest = ends[-1:], [k for k in range(len(pieces)) if k != ends[-1]]
     start = [None] * len(pieces)
-    for k, x in zip(ends, taken(ends)):
+    for k, x in zip(first, taken(first)):
         start[k] = x
     flat = links.reshape((links.shape[0], 54) + links.shape[-2:])
     given = lax.dynamic_index_in_dim(flat, 2 * (1 - core) + mine, 0, keepdims=False)
     came = flipped(given, "ta", 1)
-    if inner:
-        for k, x in zip(inner, taken(inner)):
+    if rest:
+        for k, x in zip(rest, taken(rest)):
             start[k] = x
     table, behind, top_links = call(
         functools.partial(link_kernel, depth, half),
@@ -490,8 +484,10 @@
         middle = pieces[1]
         sofar = grams_of(inner, [(z, True, z + 1 in middle) for z in middle], None)
     above = shifted(three[0], "sa", -1)
-    tasks = [(z, True, z + 1 < depth) for z in sorted({0, depth - 1})]
-    if inner:
+    if len(ends) == 2:
+        sofar = grams_of([0] + inner[:1], [(0, True, bool(inner))], sofar)
+    tasks = [(depth - 1, True, False)]
+    if depth > 1:
         tasks.append((depth - 2, False, True))
     sofar = grams_of(range(len(pieces)), tasks, sofar)
     sofar = call(
@@ -510,18 +506,13 @@
             )
         return out
 
-    steps = 1
-    assert vecs % steps == 0
-
-    def target(step, pick):
-        slot = jnp.where(step < steps, pick[0], 1 - pick[0])
-        return slot * steps + lax.rem(step, steps), 0
-
+    chunks = 4
+    assert vecs % chunks == 0
     out, grams = call(
-        functools.partial(final_kernel, steps), [shape_of(2 * many, LANES), shape_of(2, 2, 2, vecs, vecs)],
+        functools.partial(final_kernel, chunks), [shape_of(2 * many, LANES), shape_of(2, 2, 2, vecs, vecs)],
         *sum_mine, scattered(three), *sum_other, scattered(other),
-        pick=pick, place=((many // steps, LANES), target), grid=2 * steps, ops=1e6,
-        scratch=[pltpu.VMEM((vecs, LANES), F32)],
+        pick=pick, far_out=(0,), ops=1e6,
+        scratch=[pltpu.VMEM((vecs, LANES), F32), pltpu.VMEM((2, many, LANES), F32), sem((2, chunks))],
     )
     return from_rows(out, vectors.shape), grams
 

time: 98 us -> 99.1 us (1.011)
  waiting for transfers between devices: 23.1 us -> 26.9 us
  starting transfers between devices: 30.5 us -> 27.4 us
    ppermute x8, starting transfers between devices: 9.99 us -> 7.22 us  [flipped(): lax.ppermute(x, axis, [(i, i ^ bit) for i in range(lax.axis_size(axis))])]
    ppermute x8, waiting for transfers between devices: 3.8 us -> 5.91 us  [flipped(): lax.ppermute(x, axis, [(i, i ^ bit) for i in range(lax.axis_size(axis))])]
    ppermute x8, waiting for transfers between devices: 19.3 us -> 21 us  [shifted(): return lax.ppermute(x, axis, [(i, (i + by) % n) for i in range(n)])]
    pallas_call x21 -> x22, Pallas kernels: 31.5 us -> 31.6 us  [call(): pl.pallas_call(kernel, in_specs=in_specs, out_specs=out_specs, scratch_sh...]
where the time goes in v3:
time: 99.1 us; the launch traced here: 98.8 us
  Pallas kernels  42.5 us (43%)
  starting transfers between devices  27.4 us (28%)
  waiting for transfers between devices  26.9 us (27%)
  local copies, waits for them, and re-layouts  1.05 us (1%)
    pallas_call x22, Pallas kernels, call(): pl.pallas_call(kernel, in_specs=in_specs, out_specs=out_specs, scratch_sh...  31.6 us
    ppermute x8, waiting for transfers between devices, shifted(): return lax.ppermute(x, axis, [(i, (i + by) % n) for i in range(n)])  21 us
    ppermute x8, starting transfers between devices, shifted(): return lax.ppermute(x, axis, [(i, (i + by) % n) for i in range(n)])  16.2 us
    pallas_call x4, Pallas kernels, call(): return pl.pallas_call(kernel, grid_spec=spec, **params)(pick, *args)  10.9 us
    ppermute x8, starting transfers between devices, flipped(): lax.ppermute(x, axis, [(i, i ^ bit) for i in range(lax.axis_size(axis))])  7.22 us
    ppermute x8, waiting for transfers between devices, flipped(): lax.ppermute(x, axis, [(i, i ^ bit) for i in range(lax.axis_size(axis))])  5.91 us
    ppermute x2, starting transfers between devices, across(): lax.ppermute(x, ('cfg', 'sa'), [(i, i ^ cfg * size + bits) for i in pairs])  4.01 us
  transfers between devices with their start and end apart: 18, of which 8 were waited for; matrix products, arithmetic and copies ran while one was open for 0% of the time, Pallas kernels for 40%

profile of v3, /device:TPU:0, one launch (start us, length us, event | category | flops | bytes accessed | tf_op | source)
XLA Modules:
  0.0 98.8 jit_solution(3304368469683489663)
XLA Ops:
  0.6 1.0 %dynamic-slice_bitcast_fusion = f32[54,4,512]{2,1,0:T(4,128)S(1)} fusion(f32[4,54,4,512]{3,2,1,0:T(4,128)} %bitcast.29, s32[]{:T(128)S(6)} %select_n.12), kind=kLoop, calls=%fused_computation | loop fusion | bytes 884740 | tf_op jit(solution)/shard_map/jit(dynamic_index_in_dim)/squeeze | solution.py:427
  2.3 2.2 %shard_map.43.refs_2_.refs_4_ = f32[1,8,6,16,128]{4,3,2,1,0:T(8,128)S(1)} custom-call(s32[3]{0:T(128)S(1)} %pad_add_fusion.pick_ref.slot_ref, f32[6144,128]{1,0:T(8,128)} %bitcast.27), custom_call_target="tpu_custom_call" | custom-call | flops 100000 | bytes 3538944 | tf_op jit(solution)/shard_map/pallas_call | solution.py:44
  4.5 2.6 %collective-permute-start.4 = (f32[1,8,6,16,128]{4,3,2,1,0:T(8,128)S(1)}, f32[1,8,6,16,128]{4,3,2,1,0:T(8,128)S(1)}, u32[]{:S(2)}, u32[]{:S(2)}) collective-permute-start(f32[1,8,6,16,128]{4,3,2,1,0:T(8,128)S(1)} %shard_map.43.refs_2_.refs_4_), channel_id=1, source_target_pairs={{0,1},{1,2},{2,3},{3,4},{4,5},{5,6},{6,7},{7,0},{8,9},{9,10},{10,1... | collective-permute-start | bytes 1179656 | tf_op jit(solution)/shard_map/ppermute | solution.py:372
  7.1 2.6 %shard_map.42 = (f32[1,8,6,16,128]{4,3,2,1,0:T(8,128)S(1)}, f32[2,8,6,16,128]{4,3,2,1,0:T(8,128)S(1)}) custom-call(s32[3]{0:T(128)S(1)} %pad_add_fusion.pick_ref.slot_ref, f32[6144,128]{1,0:T(8,128)} %bitcast.28), custom_call_target="tpu_custom_call" | custom-call | flops 100000 | bytes 4325376 | tf_op jit(solution)/shard_map/pallas_call | solution.py:44
  9.7 3.1 %collective-permute-start.2 = (f32[1,8,6,16,128]{4,3,2,1,0:T(8,128)S(1)}, f32[1,8,6,16,128]{4,3,2,1,0:T(8,128)S(1)}, u32[]{:S(2)}, u32[]{:S(2)}) collective-permute-start(f32[1,8,6,16,128]{4,3,2,1,0:T(8,128)S(1)} %get-tuple-element.16.refs_0_.refs_3_), channel_id=1, source_target_pairs={{0,7},{1,0},{2,1},{3,2},{4,3},{5,4},{6,5},{7,6},{8,15},{9,8},{10,9... | collective-permute-start | bytes 1179656 | tf_op jit(solution)/shard_map/ppermute | solution.py:372
  12.8 3.1 %shard_map.41 = (f32[2,54,16,128]{3,2,1,0:T(8,128)S(1)}, f32[2,36,16,128]{3,2,1,0:T(8,128)S(1)}, f32[18,8,128]{2,1,0:T(8,128)S(1)}) custom-call(s32[3]{0:T(128)S(1)} %pad_add_fusion.pick_ref.slot_ref, f32[4,54,16,128]{3,2,1,0:T(8,128)} %bitcast.30, f32[54,16,128]{2,1,0:T(8,128)S(1)} %bitcast.26), custom_call_target="tpu_custom_call" | custom-call | flops 1000000 | bytes 3760128 | tf_op jit(solution)/shard_map/pallas_call | solution.py:44
  15.9 3.0 %shard_map.44 = (f32[1,8,6,16,128]{4,3,2,1,0:T(8,128)S(1)}, f32[1,8,6,16,128]{4,3,2,1,0:T(8,128)S(1)}) custom-call(f32[2,54,16,128]{3,2,1,0:T(8,128)S(1)} %get-tuple-element.17.table_ref, f32[2,36,16,128]{3,2,1,0:T(8,128)S(1)} %get-tuple-element.18.behind_ref, f32[1,8,6,16,128]{4,3,2,1,0:T(8,128)S(1)} %get-tuple-element.16.refs_0_.refs_3_, ...), custom_call_target="tpu_custom_call" | custom-call | flops 32768000 | bytes 3833856 | tf_op jit(solution)/shard_map/pallas_call | solution.py:37
  18.9 6.1 %collective-permute-done.4.refs_1_ = f32[1,8,6,16,128]{4,3,2,1,0:T(8,128)S(1)} collective-permute-done((f32[1,8,6,16,128]{4,3,2,1,0:T(8,128)S(1)}, f32[1,8,6,16,128]{4,3,2,1,0:T(8,128)S(1)}, u32[]{:S(2)}, u32[]{:S(2)}) %collective-permute-start.4) | collective-permute-done | bytes 393248 | tf_op jit(solution)/shard_map/ppermute | solution.py:372
  25.0 1.1 %collective-permute-done.1.refs_0_ = f32[18,8,128]{2,1,0:T(8,128)S(1)} collective-permute-done((f32[18,8,128]{2,1,0:T(8,128)S(1)}, f32[18,8,128]{2,1,0:T(8,128)S(1)}, u32[]{:S(2)}, u32[]{:S(2)}) %collective-permute-start.1) | collective-permute-done | bytes 73760 | tf_op jit(solution)/shard_map/ppermute | solution.py:372
  26.3 5.6 %collective-permute-start.6 = (f32[1,8,6,16,128]{4,3,2,1,0:T(8,128)S(1)}, f32[1,8,6,16,128]{4,3,2,1,0:T(8,128)S(1)}, u32[]{:S(2)}, u32[]{:S(2)}) collective-permute-start(f32[1,8,6,16,128]{4,3,2,1,0:T(8,128)S(1)} %shard_map.46.refs_0_.refs_3_), channel_id=1, source_target_pairs={{0,7},{1,0},{2,1},{3,2},{4,3},{5,4},{6,5},{7,6},{8,15},{9,8},{10,9... | collective-permute-start | bytes 1179656 | tf_op jit(solution)/shard_map/ppermute | solution.py:372
  32.2 3.2 %shard_map.47.refs_1_.refs_3_ = f32[2,8,6,16,128]{4,3,2,1,0:T(8,128)S(1)} custom-call(f32[2,54,16,128]{3,2,1,0:T(8,128)S(1)} %get-tuple-element.17.table_ref, f32[2,36,16,128]{3,2,1,0:T(8,128)S(1)} %get-tuple-element.18.behind_ref, f32[1,8,6,16,128]{4,3,2,1,0:T(8,128)S(1)} %get-tuple-element.16.refs_0_.refs_3_, ...), custom_call_target="tpu_custom_call" | custom-call | flops 32768000 | bytes 3833856 | tf_op jit(solution)/shard_map/pallas_call | solution.py:37
  35.4 3.0 %shard_map.48 = (f32[1,8,6,16,128]{4,3,2,1,0:T(8,128)S(1)}, f32[1,8,6,16,128]{4,3,2,1,0:T(8,128)S(1)}) custom-call(f32[2,54,16,128]{3,2,1,0:T(8,128)S(1)} %get-tuple-element.17.table_ref, f32[2,36,16,128]{3,2,1,0:T(8,128)S(1)} %get-tuple-element.18.behind_ref, f32[1,8,6,16,128]{4,3,2,1,0:T(8,128)S(1)} %shard_map.46.refs_0_.refs_3_, ...), custom_call_target="tpu_custom_call" | custom-call | flops 32768000 | bytes 4620288 | tf_op jit(solution)/shard_map/pallas_call | solution.py:37
  38.4 8.3 %collective-permute-done.6.refs_1_ = f32[1,8,6,16,128]{4,3,2,1,0:T(8,128)S(1)} collective-permute-done((f32[1,8,6,16,128]{4,3,2,1,0:T(8,128)S(1)}, f32[1,8,6,16,128]{4,3,2,1,0:T(8,128)S(1)}, u32[]{:S(2)}, u32[]{:S(2)}) %collective-permute-start.6) | collective-permute-done | bytes 393248 | tf_op jit(solution)/shard_map/ppermute | solution.py:372
  47.0 3.2 %shard_map.50.refs_1_ = f32[2,8,6,16,128]{4,3,2,1,0:T(8,128)S(1)} custom-call(f32[2,54,16,128]{3,2,1,0:T(8,128)S(1)} %get-tuple-element.17.table_ref, f32[2,36,16,128]{3,2,1,0:T(8,128)S(1)} %get-tuple-element.18.behind_ref, f32[1,8,6,16,128]{4,3,2,1,0:T(8,128)S(1)} %shard_map.46.refs_0_.refs_3_, f32[2,8,6,16,128]{4,3,2,1,0:T(8,128)S(1)} %shard_map.47.refs_1_.refs_3_, ...), custom_call_target="tpu_custom_call" | custom-call | flops 32768000 | bytes 4620288 | tf_op jit(solution)/shard_map/pallas_call | solution.py:37
  50.5 3.2 %shard_map.55.refs_0_.refs_1_.piece_ref = f32[2,8,6,16,128]{4,3,2,1,0:T(8,128)S(1)} custom-call(f32[2,54,16,128]{3,2,1,0:T(8,128)S(1)} %get-tuple-element.17.table_ref, f32[2,36,16,128]{3,2,1,0:T(8,128)S(1)} %get-tuple-element.18.behind_ref, f32[1,8,6,16,128]{4,3,2,1,0:T(8,128)S(1)} %shard_map.49.refs_0_, f32[2,8,6,16,128]{4,3,2,1,0:T(8,128)S(1)} %shard_map.50.refs_1_, ...), custom_call_target="tpu_custom_call" | custom-call | flops 32768000 | bytes 4620288 | tf_op jit(solution)/shard_map/pallas_call | solution.py:37
  53.8 1.6 %collective-permute-start.17 = (f32[2,8,6,16,128]{4,3,2,1,0:T(8,128)S(1)}, f32[2,8,6,16,128]{4,3,2,1,0:T(8,128)S(1)}, u32[]{:S(2)}, u32[]{:S(2)}) collective-permute-start(f32[2,8,6,16,128]{4,3,2,1,0:T(8,128)S(1)} %shard_map.55.refs_0_.refs_1_.piece_ref), channel_id=1, source_target_pairs={{0,16},{16,0},{1,17},{17,1},{2,18},{18,2},{3,19},{19,3},{4,20},{20... | collective-permute-start | bytes 2359304 | tf_op jit(solution)/shard_map/ppermute | solution.py:376
  55.3 4.7 %collective-permute-start.5 = (f32[1,8,6,16,128]{4,3,2,1,0:T(8,128)S(1)}, f32[1,8,6,16,128]{4,3,2,1,0:T(8,128)S(1)}, u32[]{:S(2)}, u32[]{:S(2)}) collective-permute-start(f32[1,8,6,16,128]{4,3,2,1,0:T(8,128)S(1)} %shard_map.49.refs_0_), channel_id=1, source_target_pairs={{0,7},{1,0},{2,1},{3,2},{4,3},{5,4},{6,5},{7,6},{8,15},{9,8},{10,9... | collective-permute-start | bytes 1179656 | tf_op jit(solution)/shard_map/ppermute | solution.py:372
  60.0 3.0 %shard_map.52 = (f32[1,8,6,16,128]{4,3,2,1,0:T(8,128)S(1)}, f32[1,8,6,16,128]{4,3,2,1,0:T(8,128)S(1)}) custom-call(f32[2,54,16,128]{3,2,1,0:T(8,128)S(1)} %get-tuple-element.17.table_ref, f32[2,36,16,128]{3,2,1,0:T(8,128)S(1)} %get-tuple-element.18.behind_ref, f32[1,8,6,16,128]{4,3,2,1,0:T(8,128)S(1)} %shard_map.49.refs_0_, ...), custom_call_target="tpu_custom_call" | custom-call | flops 32768000 | bytes 4620288 | tf_op jit(solution)/shard_map/pallas_call | solution.py:37
  64.0 5.5 %collective-permute-done.5.refs_1_ = f32[1,8,6,16,128]{4,3,2,1,0:T(8,128)S(1)} collective-permute-done((f32[1,8,6,16,128]{4,3,2,1,0:T(8,128)S(1)}, f32[1,8,6,16,128]{4,3,2,1,0:T(8,128)S(1)}, u32[]{:S(2)}, u32[]{:S(2)}) %collective-permute-start.5) | collective-permute-done | bytes 393248 | tf_op jit(solution)/shard_map/ppermute | solution.py:372
  69.8 0.9 collective-permute-start.15
  70.6 3.2 %shard_map.56.refs_2_ = f32[16,128]{1,0:T(8,128)S(1)} custom-call(f32[2,54,16,128]{3,2,1,0:T(8,128)S(1)} %get-tuple-element.17.table_ref, f32[2,8,6,16,128]{4,3,2,1,0:T(8,128)S(1)} %shard_map.55.refs_0_.refs_1_.piece_ref), custom_call_target="tpu_custom_call" | custom-call | flops 16384000 | bytes 1679360 | tf_op jit(solution)/shard_map/pallas_call | solution.py:37
  73.8 1.8 %shard_map.57.refs_3_ = f32[16,128]{1,0:T(8,128)S(1)} custom-call(f32[2,54,16,128]{3,2,1,0:T(8,128)S(1)} %get-tuple-element.17.table_ref, f32[1,8,6,16,128]{4,3,2,1,0:T(8,128)S(1)} %shard_map.54.refs_0_.piece_ref, f32[2,8,6,16,128]{4,3,2,1,0:T(8,128)S(1)} %shard_map.55.refs_0_.refs_1_.piece_ref, f32[16,128]{1,0:T(8,128)S(1)} %shard_map.56.refs_2_), custom_call_target="tpu_custom_call" | custom-call | flops 8192000 | bytes 2080768 | tf_op jit(solution)/shard_map/pallas_call | solution.py:37
  75.6 2.5 %shard_map.58.sofar_ref = f32[16,128]{1,0:T(8,128)S(1)} custom-call(f32[2,54,16,128]{3,2,1,0:T(8,128)S(1)} %get-tuple-element.17.table_ref, f32[1,8,6,16,128]{4,3,2,1,0:T(8,128)S(1)} %shard_map.54.refs_0_.piece_ref, f32[2,8,6,16,128]{4,3,2,1,0:T(8,128)S(1)} %shard_map.55.refs_0_.refs_1_.piece_ref, ...), custom_call_target="tpu_custom_call" | custom-call | flops 16384000 | bytes 2473984 | tf_op jit(solution)/shard_map/pallas_call | solution.py:37
  78.0 1.0 %shard_map.59 = f32[16,128]{1,0:T(8,128)S(1)} custom-call(f32[18,8,128]{2,1,0:T(8,128)S(1)} %get-tuple-element.15.refs_0_.links_ref, f32[1,8,6,16,128]{4,3,2,1,0:T(8,128)S(1)} %shard_map.53.refs_2_.top_ref.piece_ref, f32[1,8,6,16,128]{4,3,2,1,0:T(8,128)S(1)} %collective-permute-done.8.above_ref, f32[16,128]{1,0:T(8,128)S(1)} %shard_map.58.sofar_ref), custom_call_target="tpu_custom_call" | custom-call | flops 4096000 | bytes 876544 | tf_op jit(solution)/shard_map/pallas_call | solution.py:37
  79.0 1.9 %collective-permute-start.11 = (f32[16,128]{1,0:T(8,128)S(1)}, f32[16,128]{1,0:T(8,128)S(1)}, u32[]{:S(2)}, u32[]{:S(2)}) collective-permute-start(f32[16,128]{1,0:T(8,128)S(1)} %shard_map.59), channel_id=1, source_target_pairs={{0,3},{1,2},{2,1},{3,0},{4,7},{5,6},{6,5},{7,4},{8,11},{9,10},{10,... | collective-permute-start | bytes 24584 | tf_op jit(solution)/shard_map/ppermute | solution.py:376
  81.4 2.2 %collective-permute-done.11 = f32[16,128]{1,0:T(8,128)S(1)} collective-permute-done((f32[16,128]{1,0:T(8,128)S(1)}, f32[16,128]{1,0:T(8,128)S(1)}, u32[]{:S(2)}, u32[]{:S(2)}) %collective-permute-start.11) | collective-permute-done | bytes 8224 | tf_op jit(solution)/shard_map/ppermute | solution.py:376
  83.6 0.9 collective-permute-start.9
  84.6 2.6 %collective-permute-done.9 = f32[16,128]{1,0:T(8,128)S(1)} collective-permute-done((f32[16,128]{1,0:T(8,128)S(1)}, f32[16,128]{1,0:T(8,128)S(1)}, u32[]{:S(2)}, u32[]{:S(2)}) %collective-permute-start.9) | collective-permute-done | bytes 8224 | tf_op jit(solution)/shard_map/ppermute | solution.py:376
  87.2 3.5 %collective-permute-start.14 = (f32[16,128]{1,0:T(8,128)S(1)}, f32[16,128]{1,0:T(8,128)S(1)}, u32[]{:S(2)}, u32[]{:S(2)}) collective-permute-start(f32[16,128]{1,0:T(8,128)S(1)} %add_add_fusion.refs_0_), channel_id=1, source_target_pairs={{0,20},{1,21},{2,22},{3,23},{4,16},{5,17},{6,18},{7,19},{16,4},{17... | collective-permute-start | bytes 24584 | tf_op jit(solution)/shard_map/ppermute | solution.py:386
  93.2 0.8 shard_map.63.refs_0_
  94.9 0.9 collective-permute-done.12.refs_1_
  95.8 3.0 %shard_map.66 = (f32[6144,128]{1,0:T(8,128)}, f32[2,2,2,16,16]{4,3,2,1,0:T(8,128)}) custom-call(s32[3]{0:T(128)S(1)} %pad_add_fusion.pick_ref.slot_ref, f32[16,128]{1,0:T(8,128)S(1)} %add_add_fusion.refs_0_, f32[16,128]{1,0:T(8,128)S(1)} %collective-permute-done.12.refs_1_, f32[3072,128]{1,0:T(8,128)S(1)} %shard_map.62.refs_2_, ...), custom_call_target="tpu_custom_call" | custom-call | flops 1000000 | bytes 6332416 | tf_op jit(solution)/shard_map/pallas_call | solution.py:44
  (33 shorter events, 6.7 us)
Async XLA Ops:
  1.7 11.1 %collective-permute-start = (f32[54,4,512]{2,1,0:T(4,128)S(1)}, f32[54,4,512]{2,1,0:T(4,128)S(1)}, u32[]{:S(2)}, u32[]{:S(2)}) collective-permute-start(f32[54,4,512]{2,1,0:T(4,128)S(1)} %dynamic-slice_bitcast_fusion), channel_id=1, source_target_pairs={{0,8},{8,0},{1,9},{9,1},{2,10},{10,2},{3,11},{11,3},{4,12},{12,4},... | collective-permute-start | bytes 1327112 | tf_op jit(solution)/shard_map/ppermute | solution.py:376
  4.5 20.5 %collective-permute-start.4 = (f32[1,8,6,16,128]{4,3,2,1,0:T(8,128)S(1)}, f32[1,8,6,16,128]{4,3,2,1,0:T(8,128)S(1)}, u32[]{:S(2)}, u32[]{:S(2)}) collective-permute-start(f32[1,8,6,16,128]{4,3,2,1,0:T(8,128)S(1)} %shard_map.43.refs_2_.refs_4_), channel_id=1, source_target_pairs={{0,1},{1,2},{2,3},{3,4},{4,5},{5,6},{6,7},{7,0},{8,9},{9,10},{10,1... | collective-permute-start | bytes 1179656 | tf_op jit(solution)/shard_map/ppermute | solution.py:372
  9.7 22.2 %collective-permute-start.2 = (f32[1,8,6,16,128]{4,3,2,1,0:T(8,128)S(1)}, f32[1,8,6,16,128]{4,3,2,1,0:T(8,128)S(1)}, u32[]{:S(2)}, u32[]{:S(2)}) collective-permute-start(f32[1,8,6,16,128]{4,3,2,1,0:T(8,128)S(1)} %get-tuple-element.16.refs_0_.refs_3_), channel_id=1, source_target_pairs={{0,7},{1,0},{2,1},{3,2},{4,3},{5,4},{6,5},{7,6},{8,15},{9,8},{10,9... | collective-permute-start | bytes 1179656 | tf_op jit(solution)/shard_map/ppermute | solution.py:372
  15.9 10.2 %collective-permute-start.1 = (f32[18,8,128]{2,1,0:T(8,128)S(1)}, f32[18,8,128]{2,1,0:T(8,128)S(1)}, u32[]{:S(2)}, u32[]{:S(2)}) collective-permute-start(f32[18,8,128]{2,1,0:T(8,128)S(1)} %get-tuple-element.15.refs_0_.links_ref), channel_id=1, source_target_pairs={{0,1},{1,2},{2,3},{3,4},{4,5},{5,6},{6,7},{7,0},{8,9},{9,10},{10,1... | collective-permute-start | bytes 221192 | tf_op jit(solution)/shard_map/ppermute | solution.py:372
  26.3 20.4 %collective-permute-start.6 = (f32[1,8,6,16,128]{4,3,2,1,0:T(8,128)S(1)}, f32[1,8,6,16,128]{4,3,2,1,0:T(8,128)S(1)}, u32[]{:S(2)}, u32[]{:S(2)}) collective-permute-start(f32[1,8,6,16,128]{4,3,2,1,0:T(8,128)S(1)} %shard_map.46.refs_0_.refs_3_), channel_id=1, source_target_pairs={{0,7},{1,0},{2,1},{3,2},{4,3},{5,4},{6,5},{7,6},{8,15},{9,8},{10,9... | collective-permute-start | bytes 1179656 | tf_op jit(solution)/shard_map/ppermute | solution.py:372
  32.1 18.1 %collective-permute-start.3 = (f32[1,8,6,16,128]{4,3,2,1,0:T(8,128)S(1)}, f32[1,8,6,16,128]{4,3,2,1,0:T(8,128)S(1)}, u32[]{:S(2)}, u32[]{:S(2)}) collective-permute-start(f32[1,8,6,16,128]{4,3,2,1,0:T(8,128)S(1)} %shard_map.45.refs_2_.refs_4_), channel_id=1, source_target_pairs={{0,1},{1,2},{2,3},{3,4},{4,5},{5,6},{6,7},{7,0},{8,9},{9,10},{10,1... | collective-permute-start | bytes 1179656 | tf_op jit(solution)/shard_map/ppermute | solution.py:372
  47.0 16.1 %collective-permute-start.7 = (f32[1,8,6,16,128]{4,3,2,1,0:T(8,128)S(1)}, f32[1,8,6,16,128]{4,3,2,1,0:T(8,128)S(1)}, u32[]{:S(2)}, u32[]{:S(2)}) collective-permute-start(f32[1,8,6,16,128]{4,3,2,1,0:T(8,128)S(1)} %shard_map.51.refs_2_), channel_id=1, source_target_pairs={{0,1},{1,2},{2,3},{3,4},{4,5},{5,6},{6,7},{7,0},{8,9},{9,10},{10,1... | collective-permute-start | bytes 1179656 | tf_op jit(solution)/shard_map/ppermute | solution.py:372
  53.8 37.5 %collective-permute-start.17 = (f32[2,8,6,16,128]{4,3,2,1,0:T(8,128)S(1)}, f32[2,8,6,16,128]{4,3,2,1,0:T(8,128)S(1)}, u32[]{:S(2)}, u32[]{:S(2)}) collective-permute-start(f32[2,8,6,16,128]{4,3,2,1,0:T(8,128)S(1)} %shard_map.55.refs_0_.refs_1_.piece_ref), channel_id=1, source_target_pairs={{0,16},{16,0},{1,17},{17,1},{2,18},{18,2},{3,19},{19,3},{4,20},{20... | collective-permute-start | bytes 2359304 | tf_op jit(solution)/shard_map/ppermute | solution.py:376
  55.3 14.2 %collective-permute-start.5 = (f32[1,8,6,16,128]{4,3,2,1,0:T(8,128)S(1)}, f32[1,8,6,16,128]{4,3,2,1,0:T(8,128)S(1)}, u32[]{:S(2)}, u32[]{:S(2)}) collective-permute-start(f32[1,8,6,16,128]{4,3,2,1,0:T(8,128)S(1)} %shard_map.49.refs_0_), channel_id=1, source_target_pairs={{0,7},{1,0},{2,1},{3,2},{4,3},{5,4},{6,5},{7,6},{8,15},{9,8},{10,9... | collective-permute-start | bytes 1179656 | tf_op jit(solution)/shard_map/ppermute | solution.py:372
  63.3 14.7 %collective-permute-start.8 = (f32[1,8,6,16,128]{4,3,2,1,0:T(8,128)S(1)}, f32[1,8,6,16,128]{4,3,2,1,0:T(8,128)S(1)}, u32[]{:S(2)}, u32[]{:S(2)}) collective-permute-start(f32[1,8,6,16,128]{4,3,2,1,0:T(8,128)S(1)} %shard_map.54.refs_0_.piece_ref), channel_id=1, source_target_pairs={{0,7},{1,0},{2,1},{3,2},{4,3},{5,4},{6,5},{7,6},{8,15},{9,8},{10,9... | collective-permute-start | bytes 1179656 | tf_op jit(solution)/shard_map/ppermute | solution.py:372
  63.4 30.7 %collective-permute-start.16 = (f32[1,8,6,16,128]{4,3,2,1,0:T(8,128)S(1)}, f32[1,8,6,16,128]{4,3,2,1,0:T(8,128)S(1)}, u32[]{:S(2)}, u32[]{:S(2)}) collective-permute-start(f32[1,8,6,16,128]{4,3,2,1,0:T(8,128)S(1)} %shard_map.54.refs_0_.piece_ref), channel_id=1, source_target_pairs={{0,16},{16,0},{1,17},{17,1},{2,18},{18,2},{3,19},{19,3},{4,20},{20... | collective-permute-start | bytes 1179656 | tf_op jit(solution)/shard_map/ppermute | solution.py:376
  69.8 24.7 %collective-permute-start.15 = (f32[1,8,6,16,128]{4,3,2,1,0:T(8,128)S(1)}, f32[1,8,6,16,128]{4,3,2,1,0:T(8,128)S(1)}, u32[]{:S(2)}, u32[]{:S(2)}) collective-permute-start(f32[1,8,6,16,128]{4,3,2,1,0:T(8,128)S(1)} %shard_map.53.refs_2_.top_ref.piece_ref), channel_id=1, source_target_pairs={{0,16},{16,0},{1,17},{17,1},{2,18},{18,2},{3,19},{19,3},{4,20},{20... | collective-permute-start | bytes 1179656 | tf_op jit(solution)/shard_map/ppermute | solution.py:376
  79.0 4.6 %collective-permute-start.11 = (f32[16,128]{1,0:T(8,128)S(1)}, f32[16,128]{1,0:T(8,128)S(1)}, u32[]{:S(2)}, u32[]{:S(2)}) collective-permute-start(f32[16,128]{1,0:T(8,128)S(1)} %shard_map.59), channel_id=1, source_target_pairs={{0,3},{1,2},{2,1},{3,0},{4,7},{5,6},{6,5},{7,4},{8,11},{9,10},{10,... | collective-permute-start | bytes 24584 | tf_op jit(solution)/shard_map/ppermute | solution.py:376
  80.9 3.7 %collective-permute-start.10 = (f32[16,128]{1,0:T(8,128)S(1)}, f32[16,128]{1,0:T(8,128)S(1)}, u32[]{:S(2)}, u32[]{:S(2)}) collective-permute-start(f32[16,128]{1,0:T(8,128)S(1)} %shard_map.59), channel_id=1, source_target_pairs={{0,2},{1,3},{2,0},{3,1},{4,6},{5,7},{6,4},{7,5},{8,10},{9,11},{10,... | collective-permute-start | bytes 24584 | tf_op jit(solution)/shard_map/ppermute | solution.py:376
  83.6 3.7 %collective-permute-start.9 = (f32[16,128]{1,0:T(8,128)S(1)}, f32[16,128]{1,0:T(8,128)S(1)}, u32[]{:S(2)}, u32[]{:S(2)}) collective-permute-start(f32[16,128]{1,0:T(8,128)S(1)} %shard_map.59), channel_id=1, source_target_pairs={{0,1},{1,0},{2,3},{3,2},{4,5},{5,4},{6,7},{7,6},{8,9},{9,8},{10,11... | collective-permute-start | bytes 24584 | tf_op jit(solution)/shard_map/ppermute | solution.py:376
  87.2 7.6 %collective-permute-start.14 = (f32[16,128]{1,0:T(8,128)S(1)}, f32[16,128]{1,0:T(8,128)S(1)}, u32[]{:S(2)}, u32[]{:S(2)}) collective-permute-start(f32[16,128]{1,0:T(8,128)S(1)} %add_add_fusion.refs_0_), channel_id=1, source_target_pairs={{0,20},{1,21},{2,22},{3,23},{4,16},{5,17},{6,18},{7,19},{16,4},{17... | collective-permute-start | bytes 24584 | tf_op jit(solution)/shard_map/ppermute | solution.py:386
  90.7 4.1 %collective-permute-start.13 = (f32[16,128]{1,0:T(8,128)S(1)}, f32[16,128]{1,0:T(8,128)S(1)}, u32[]{:S(2)}, u32[]{:S(2)}) collective-permute-start(f32[16,128]{1,0:T(8,128)S(1)} %add_add_fusion.refs_0_), channel_id=1, source_target_pairs={{0,16},{1,17},{2,18},{3,19},{4,20},{5,21},{6,22},{7,23},{16,0},{17... | collective-permute-start | bytes 24584 | tf_op jit(solution)/shard_map/ppermute | solution.py:386
  91.3 4.6 %collective-permute-start.12 = (f32[16,128]{1,0:T(8,128)S(1)}, f32[16,128]{1,0:T(8,128)S(1)}, u32[]{:S(2)}, u32[]{:S(2)}) collective-permute-start(f32[16,128]{1,0:T(8,128)S(1)} %add_add_fusion.refs_0_), channel_id=1, source_target_pairs={{0,4},{1,5},{2,6},{3,7},{4,0},{5,1},{6,2},{7,3},{8,12},{9,13},{10,... | collective-permute-start | bytes 24584 | tf_op jit(solution)/shard_map/ppermute | solution.py:376

commit v4 on v3

--- a/solution.py
+++ b/solution.py
@@ -10,6 +10,7 @@
 
 LX = 32
 LANES = 128
+DEG = 3
 SCALE = 5.5
 F32 = jnp.float32
 BF16 = jnp.bfloat16
@@ -222,15 +223,27 @@
         lax.fori_loop(0, rows, body, 0)
 
 
-def close_kernel(factor, behind, *refs):
+def whole_plane(message_ref, base_ref, links_ref, factor, back, c):
+    plane = [message_ref[0, c, q] for q in range(6)]
+    if base_ref is not None:
+        total = [jnp.zeros_like(plane[0]) for _ in range(6)]
+        multiply_into(total, lambda q: base_ref[0, c, q], edge_rows(links_ref, c, plane[0].shape[0]), back)
+        plane = [p + t * factor for p, t in zip(plane, total)]
+    return plane
+
+
+def close_kernel(factor, factor_before, behind, based, *refs):
+    refs = list(refs)
     part_ref, out_ref = refs[-2].at[0], refs[-1].at[0]
     rows, _, vecs, _ = out_ref.shape
+    each = 3 if based else 2
 
     def body(c, _):
         total = [jnp.zeros((vecs, LANES), F32) for _ in range(6)]
         for k, back in enumerate(behind):
-            links_ref, halo_ref = refs[2 * k : 2 * k + 2]
-            multiply_into(total, lambda q: halo_ref[0, c, q], edge_rows(links_ref, c, vecs), back)
+            links_ref, halo_ref, *base = refs[each * k : each * (k + 1)]
+            halo = whole_plane(halo_ref, base[0] if based else None, links_ref, factor_before, not back, c)
+            multiply_into(total, lambda q: halo[q], edge_rows(links_ref, c, vecs), back)
         for q in range(6):
             out_ref[c, q] = part_ref[c, q] + total[q] * factor
         return 0
@@ -295,13 +308,15 @@
     out_ref[...] = part + sofar_ref[...] if more else part
 
 
-def last_hop_kernel(links_ref, top_ref, above_ref, sofar_ref, out_ref, acc_ref):
+def last_hop_kernel(factor, links_ref, top_ref, above_ref, *refs):
+    *base, sofar_ref, out_ref, acc_ref = refs
     rows, _, vecs, _ = top_ref.shape[1:]
     acc_ref[...] = jnp.zeros_like(acc_ref)
 
     def sides(c):
         total = [jnp.zeros((vecs, LANES), F32) for _ in range(6)]
-        multiply_into(total, lambda q: above_ref[0, c, q], edge_rows(links_ref, c, vecs), False)
+        above = whole_plane(above_ref, base[0] if base else None, links_ref, factor, True, c)
+        multiply_into(total, lambda q: above[q], edge_rows(links_ref, c, vecs), False)
         return [top_ref[0, c, q] for q in range(6)], total
 
     products(acc_ref, rows, False, sides)
@@ -438,29 +453,42 @@
     )
     prior = shifted(top_links, "sa", 1)
 
-    def advance(cur, old):
-        factor = -(1.0 if old is None else 2.0) / SCALE
-        low = shifted(cur[-1], "sa", 1)
-        high = shifted(cur[0], "sa", -1)
+    early = depth > 1
+
+    def factor_of(step):
+        return -(1.0 if step == 0 else 2.0) / SCALE
+
+    def sent(planes, upwards=True):
+        low = None
+        if upwards:
+            low = shifted(planes[-1], "sa", 1)
+        return low, shifted(planes[0], "sa", -1)
+
+    def advance(step, cur, old, messages):
         new = [None] * len(pieces)
         for todo in (inner, ends):
             if todo:
                 got = call(
-                    functools.partial(part_kernel, depth, pieces, todo, factor, old is None),
-                    [field[k] for k in todo], table, behind, *cur, *([] if old is None else [old[k] for k in todo]),
+                    functools.partial(part_kernel, depth, pieces, todo, factor_of(step), old is None),
+                    [field[k] for k in todo], table, behind, *cur,
+                    *([] if old is None else [old[k] for k in todo]),
                     ops=work * sum(len(pieces[k]) for k in todo),
                 )
                 for k, x in zip(todo, got):
                     new[k] = x
-        sides = [(0, True, prior, low), (len(pieces) - 1, False, top_links, high)]
+        following = sent(new, step + 1 < DEG) if early else None
+        based = early and old is not None
+        sides = [(0, True, prior, messages[0]), (len(pieces) - 1, False, top_links, messages[1])]
         for k in ends:
             used = [side for side in sides if side[0] == k]
-            operands = [x for side in used for x in side[2:]]
+            operands = [x for side in used for x in (*side[2:], *([old[k]] if based else []))]
             (new[k],) = call(
-                functools.partial(close_kernel, factor, [side[1] for side in used]),
+                functools.partial(
+                    close_kernel, factor_of(step), factor_of(step - 1), [side[1] for side in used], based
+                ),
                 [field[k]], *operands, new[k], ops=work / 6,
             )
-        return new
+        return new, following or sent(new, step + 1 < DEG)
 
     packed = shape_of(vecs, LANES)
     acc = [pltpu.VMEM((4 * vecs, 8 * vecs), F32)]
@@ -475,15 +503,16 @@
             scratch=acc, ops=work * len(tasks) / 2,
         )
 
-    one = advance(start, None)
-    two = advance(one, start)
-    three = advance(two, one)
+    old, three, messages = None, start, sent(start)
+    for step in range(DEG):
+        fresh, messages = advance(step, three, old, messages)
+        old, three = three, fresh
+    above = messages[1]
 
     sofar = None
     if inner:
         middle = pieces[1]
         sofar = grams_of(inner, [(z, True, z + 1 in middle) for z in middle], None)
-    above = shifted(three[0], "sa", -1)
     if len(ends) == 2:
         sofar = grams_of([0] + inner[:1], [(0, True, bool(inner))], sofar)
     tasks = [(depth - 1, True, False)]
@@ -491,7 +520,8 @@
         tasks.append((depth - 2, False, True))
     sofar = grams_of(range(len(pieces)), tasks, sofar)
     sofar = call(
-        last_hop_kernel, packed, top_links, three[-1], above, sofar,
+        functools.partial(last_hop_kernel, factor_of(DEG - 1)), packed,
+        top_links, three[-1], above, *([old[-1]] if early else []), sofar,
         scratch=acc, ops=work / 4,
     )
     sum_mine, sum_other = summed(sofar)

time: 99.1 us -> 117 us (1.18)
  waiting for transfers between devices: 26.9 us -> 36.9 us
  starting transfers between devices: 27.4 us -> 35 us
    ppermute x8, waiting for transfers between devices: 21 us -> 32.7 us  [shifted(): return lax.ppermute(x, axis, [(i, (i + by) % n) for i in range(n)])]
    ppermute x8, starting transfers between devices: 16.2 us -> 19.5 us  [shifted(): return lax.ppermute(x, axis, [(i, (i + by) % n) for i in range(n)])]
    ppermute x8, starting transfers between devices: 7.22 us -> 10.2 us  [flipped(): lax.ppermute(x, axis, [(i, i ^ bit) for i in range(lax.axis_size(axis))])]
    ppermute x8, waiting for transfers between devices: 5.91 us -> 4.18 us  [flipped(): lax.ppermute(x, axis, [(i, i ^ bit) for i in range(lax.axis_size(axis))])]
    ppermute x2, starting transfers between devices: 4.01 us -> 5.31 us  [across(): lax.ppermute(x, ('cfg', 'sa'), [(i, i ^ cfg * size + bits) for i in pairs])]
  transfers between devices with their start and end apart: 18 -> 18, of which waited for: 8 -> 7; matrix products, arithmetic and copies ran while one was open for 0% -> 0% of each run, Pallas kernels for 40% -> 31%
where the time goes in v4:
time: 117 us
  Pallas kernels  43.3 us (37%)
  waiting for transfers between devices  36.9 us (32%)
  starting transfers between devices  35 us (30%)
    ppermute x8, waiting for transfers between devices, shifted(): return lax.ppermute(x, axis, [(i, (i + by) % n) for i in range(n)])  32.7 us
    pallas_call x22, Pallas kernels, call(): pl.pallas_call(kernel, in_specs=in_specs, out_specs=out_specs, scratch_sh...  32.4 us
    ppermute x8, starting transfers between devices, shifted(): return lax.ppermute(x, axis, [(i, (i + by) % n) for i in range(n)])  19.5 us
    pallas_call x4, Pallas kernels, call(): return pl.pallas_call(kernel, grid_spec=spec, **params)(pick, *args)  10.9 us
    ppermute x8, starting transfers between devices, flipped(): lax.ppermute(x, axis, [(i, i ^ bit) for i in range(lax.axis_size(axis))])  10.2 us
    ppermute x2, starting transfers between devices, across(): lax.ppermute(x, ('cfg', 'sa'), [(i, i ^ cfg * size + bits) for i in pairs])  5.31 us
    ppermute x8, waiting for transfers between devices, flipped(): lax.ppermute(x, axis, [(i, i ^ bit) for i in range(lax.axis_size(axis))])  4.18 us
  transfers between devices with their start and end apart: 18, of which 7 were waited for; matrix products, arithmetic and copies ran while one was open for 0% of the time, Pallas kernels for 31%

profile of v4, /device:TPU:0, one launch (start us, length us, event | category | flops | bytes accessed | tf_op | source)
XLA Modules:
  0.0 117.2 jit_solution(2111364468117590820)
XLA Ops:
  0.6 1.0 dynamic-slice_bitcast_fusion
  2.3 2.6 %shard_map.43 = (f32[1,8,6,16,128]{4,3,2,1,0:T(8,128)S(1)}, f32[2,8,6,16,128]{4,3,2,1,0:T(8,128)S(1)}) custom-call(s32[3]{0:T(128)S(1)} %pad_add_fusion.pick_ref.slot_ref, f32[6144,128]{1,0:T(8,128)} %bitcast.27), custom_call_target="tpu_custom_call" | custom-call | flops 100000 | bytes 4325376 | tf_op jit(solution)/shard_map/pallas_call | solution.py:45
  4.9 5.6 %collective-permute-start.3 = (f32[1,8,6,16,128]{4,3,2,1,0:T(8,128)S(1)}, f32[1,8,6,16,128]{4,3,2,1,0:T(8,128)S(1)}, u32[]{:S(2)}, u32[]{:S(2)}) collective-permute-start(f32[1,8,6,16,128]{4,3,2,1,0:T(8,128)S(1)} %get-tuple-element.18.refs_0_.refs_3_.refs_2_), channel_id=1, source_target_pairs={{0,7},{1,0},{2,1},{3,2},{4,3},{5,4},{6,5},{7,6},{8,15},{9,8},{10,9... | collective-permute-start | bytes 1179656 | tf_op jit(solution)/shard_map/ppermute | solution.py:387
  10.5 2.2 %shard_map.42.refs_2_.refs_4_ = f32[1,8,6,16,128]{4,3,2,1,0:T(8,128)S(1)} custom-call(s32[3]{0:T(128)S(1)} %pad_add_fusion.pick_ref.slot_ref, f32[6144,128]{1,0:T(8,128)} %bitcast.28), custom_call_target="tpu_custom_call" | custom-call | flops 100000 | bytes 3538944 | tf_op jit(solution)/shard_map/pallas_call | solution.py:45
  12.8 3.1 %shard_map.41 = (f32[2,54,16,128]{3,2,1,0:T(8,128)S(1)}, f32[2,36,16,128]{3,2,1,0:T(8,128)S(1)}, f32[18,8,128]{2,1,0:T(8,128)S(1)}) custom-call(s32[3]{0:T(128)S(1)} %pad_add_fusion.pick_ref.slot_ref, f32[4,54,16,128]{3,2,1,0:T(8,128)} %bitcast.30, f32[54,16,128]{2,1,0:T(8,128)S(1)} %bitcast.26), custom_call_target="tpu_custom_call" | custom-call | flops 1000000 | bytes 3760128 | tf_op jit(solution)/shard_map/pallas_call | solution.py:45
  15.9 3.0 %shard_map.44 = (f32[1,8,6,16,128]{4,3,2,1,0:T(8,128)S(1)}, f32[1,8,6,16,128]{4,3,2,1,0:T(8,128)S(1)}) custom-call(f32[2,54,16,128]{3,2,1,0:T(8,128)S(1)} %get-tuple-element.16.table_ref, f32[2,36,16,128]{3,2,1,0:T(8,128)S(1)} %get-tuple-element.17.behind_ref, f32[1,8,6,16,128]{4,3,2,1,0:T(8,128)S(1)} %get-tuple-element.18.refs_0_.refs_3_.refs_2_, ...), custom_call_target="tpu_custom_call" | custom-call | flops 32768000 | bytes 3833856 | tf_op jit(solution)/shard_map/pallas_call | solution.py:38
  18.9 4.8 %collective-permute-start.6 = (f32[1,8,6,16,128]{4,3,2,1,0:T(8,128)S(1)}, f32[1,8,6,16,128]{4,3,2,1,0:T(8,128)S(1)}, u32[]{:S(2)}, u32[]{:S(2)}) collective-permute-start(f32[1,8,6,16,128]{4,3,2,1,0:T(8,128)S(1)} %get-tuple-element.20.refs_2_), channel_id=1, source_target_pairs={{0,7},{1,0},{2,1},{3,2},{4,3},{5,4},{6,5},{7,6},{8,15},{9,8},{10,9... | collective-permute-start | bytes 1179656 | tf_op jit(solution)/shard_map/ppermute | solution.py:387
  23.9 3.2 %shard_map.46.refs_1_.refs_3_ = f32[2,8,6,16,128]{4,3,2,1,0:T(8,128)S(1)} custom-call(f32[2,54,16,128]{3,2,1,0:T(8,128)S(1)} %get-tuple-element.16.table_ref, f32[2,36,16,128]{3,2,1,0:T(8,128)S(1)} %get-tuple-element.17.behind_ref, f32[1,8,6,16,128]{4,3,2,1,0:T(8,128)S(1)} %get-tuple-element.18.refs_0_.refs_3_.refs_2_, ...), custom_call_target="tpu_custom_call" | custom-call | flops 32768000 | bytes 3833856 | tf_op jit(solution)/shard_map/pallas_call | solution.py:38
  27.1 7.2 %collective-permute-done.2.refs_1_ = f32[1,8,6,16,128]{4,3,2,1,0:T(8,128)S(1)} collective-permute-done((f32[1,8,6,16,128]{4,3,2,1,0:T(8,128)S(1)}, f32[1,8,6,16,128]{4,3,2,1,0:T(8,128)S(1)}, u32[]{:S(2)}, u32[]{:S(2)}) %collective-permute-start.2) | collective-permute-done | bytes 393248 | tf_op jit(solution)/shard_map/ppermute | solution.py:387
  34.3 10.0 %collective-permute-done.1.refs_0_ = f32[18,8,128]{2,1,0:T(8,128)S(1)} collective-permute-done((f32[18,8,128]{2,1,0:T(8,128)S(1)}, f32[18,8,128]{2,1,0:T(8,128)S(1)}, u32[]{:S(2)}, u32[]{:S(2)}) %collective-permute-start.1) | collective-permute-done | bytes 73760 | tf_op jit(solution)/shard_map/ppermute | solution.py:387
  44.5 3.2 %shard_map.50.refs_1_ = f32[2,8,6,16,128]{4,3,2,1,0:T(8,128)S(1)} custom-call(f32[2,54,16,128]{3,2,1,0:T(8,128)S(1)} %get-tuple-element.16.table_ref, f32[2,36,16,128]{3,2,1,0:T(8,128)S(1)} %get-tuple-element.17.behind_ref, f32[1,8,6,16,128]{4,3,2,1,0:T(8,128)S(1)} %shard_map.45.refs_0_.refs_3_.refs_2_, f32[2,8,6,16,128]{4,3,2,1,0:T(8,128)S(1)} %shard_map.46.refs_1_.refs_3_, ...), custom_call_target="tpu_custom_call" | custom-call | flops 32768000 | bytes 4620288 | tf_op jit(solution)/shard_map/pallas_call | solution.py:38
  47.8 3.0 %shard_map.48 = (f32[1,8,6,16,128]{4,3,2,1,0:T(8,128)S(1)}, f32[1,8,6,16,128]{4,3,2,1,0:T(8,128)S(1)}) custom-call(f32[2,54,16,128]{3,2,1,0:T(8,128)S(1)} %get-tuple-element.16.table_ref, f32[2,36,16,128]{3,2,1,0:T(8,128)S(1)} %get-tuple-element.17.behind_ref, f32[1,8,6,16,128]{4,3,2,1,0:T(8,128)S(1)} %shard_map.45.refs_0_.refs_3_.refs_2_, ...), custom_call_target="tpu_custom_call" | custom-call | flops 32768000 | bytes 4620288 | tf_op jit(solution)/shard_map/pallas_call | solution.py:38
  51.6 3.2 %shard_map.55.refs_0_.refs_1_.piece_ref = f32[2,8,6,16,128]{4,3,2,1,0:T(8,128)S(1)} custom-call(f32[2,54,16,128]{3,2,1,0:T(8,128)S(1)} %get-tuple-element.16.table_ref, f32[2,36,16,128]{3,2,1,0:T(8,128)S(1)} %get-tuple-element.17.behind_ref, f32[1,8,6,16,128]{4,3,2,1,0:T(8,128)S(1)} %shard_map.49.refs_0_, f32[2,8,6,16,128]{4,3,2,1,0:T(8,128)S(1)} %shard_map.50.refs_1_, ...), custom_call_target="tpu_custom_call" | custom-call | flops 32768000 | bytes 4620288 | tf_op jit(solution)/shard_map/pallas_call | solution.py:38
  54.9 1.6 %collective-permute-start.17 = (f32[2,8,6,16,128]{4,3,2,1,0:T(8,128)S(1)}, f32[2,8,6,16,128]{4,3,2,1,0:T(8,128)S(1)}, u32[]{:S(2)}, u32[]{:S(2)}) collective-permute-start(f32[2,8,6,16,128]{4,3,2,1,0:T(8,128)S(1)} %shard_map.55.refs_0_.refs_1_.piece_ref), channel_id=1, source_target_pairs={{0,16},{16,0},{1,17},{17,1},{2,18},{18,2},{3,19},{19,3},{4,20},{20... | collective-permute-start | bytes 2359304 | tf_op jit(solution)/shard_map/ppermute | solution.py:391
  56.4 2.5 %collective-permute-start.8 = (f32[1,8,6,16,128]{4,3,2,1,0:T(8,128)S(1)}, f32[1,8,6,16,128]{4,3,2,1,0:T(8,128)S(1)}, u32[]{:S(2)}, u32[]{:S(2)}) collective-permute-start(f32[1,8,6,16,128]{4,3,2,1,0:T(8,128)S(1)} %get-tuple-element.23.refs_3_), channel_id=1, source_target_pairs={{0,1},{1,2},{2,3},{3,4},{4,5},{5,6},{6,7},{7,0},{8,9},{9,10},{10,1... | collective-permute-start | bytes 1179656 | tf_op jit(solution)/shard_map/ppermute | solution.py:387
  58.9 4.6 %collective-permute-start.4 = (f32[1,8,6,16,128]{4,3,2,1,0:T(8,128)S(1)}, f32[1,8,6,16,128]{4,3,2,1,0:T(8,128)S(1)}, u32[]{:S(2)}, u32[]{:S(2)}) collective-permute-start(f32[1,8,6,16,128]{4,3,2,1,0:T(8,128)S(1)} %get-tuple-element.22.refs_3_), channel_id=1, source_target_pairs={{0,7},{1,0},{2,1},{3,2},{4,3},{5,4},{6,5},{7,6},{8,15},{9,8},{10,9... | collective-permute-start | bytes 1179656 | tf_op jit(solution)/shard_map/ppermute | solution.py:387
  63.5 3.0 %shard_map.52 = (f32[1,8,6,16,128]{4,3,2,1,0:T(8,128)S(1)}, f32[1,8,6,16,128]{4,3,2,1,0:T(8,128)S(1)}) custom-call(f32[2,54,16,128]{3,2,1,0:T(8,128)S(1)} %get-tuple-element.16.table_ref, f32[2,36,16,128]{3,2,1,0:T(8,128)S(1)} %get-tuple-element.17.behind_ref, f32[1,8,6,16,128]{4,3,2,1,0:T(8,128)S(1)} %shard_map.49.refs_0_, ...), custom_call_target="tpu_custom_call" | custom-call | flops 32768000 | bytes 4620288 | tf_op jit(solution)/shard_map/pallas_call | solution.py:38
  66.5 2.1 %collective-permute-start.7 = (f32[1,8,6,16,128]{4,3,2,1,0:T(8,128)S(1)}, f32[1,8,6,16,128]{4,3,2,1,0:T(8,128)S(1)}, u32[]{:S(2)}, u32[]{:S(2)}) collective-permute-start(f32[1,8,6,16,128]{4,3,2,1,0:T(8,128)S(1)} %get-tuple-element.25.refs_3_), channel_id=1, source_target_pairs={{0,7},{1,0},{2,1},{3,2},{4,3},{5,4},{6,5},{7,6},{8,15},{9,8},{10,9... | collective-permute-start | bytes 1179656 | tf_op jit(solution)/shard_map/ppermute | solution.py:387
  68.6 15.5 %collective-permute-done.8.refs_1_ = f32[1,8,6,16,128]{4,3,2,1,0:T(8,128)S(1)} collective-permute-done((f32[1,8,6,16,128]{4,3,2,1,0:T(8,128)S(1)}, f32[1,8,6,16,128]{4,3,2,1,0:T(8,128)S(1)}, u32[]{:S(2)}, u32[]{:S(2)}) %collective-permute-start.8) | collective-permute-done | bytes 393248 | tf_op jit(solution)/shard_map/ppermute | solution.py:387
  85.5 1.6 %collective-permute-start.15 = (f32[1,8,6,16,128]{4,3,2,1,0:T(8,128)S(1)}, f32[1,8,6,16,128]{4,3,2,1,0:T(8,128)S(1)}, u32[]{:S(2)}, u32[]{:S(2)}) collective-permute-start(f32[1,8,6,16,128]{4,3,2,1,0:T(8,128)S(1)} %shard_map.53.refs_2_.top_ref.piece_ref), channel_id=1, source_target_pairs={{0,16},{16,0},{1,17},{17,1},{2,18},{18,2},{3,19},{19,3},{4,20},{20... | collective-permute-start | bytes 1179656 | tf_op jit(solution)/shard_map/ppermute | solution.py:391
  87.0 3.2 %shard_map.56.refs_2_ = f32[16,128]{1,0:T(8,128)S(1)} custom-call(f32[2,54,16,128]{3,2,1,0:T(8,128)S(1)} %get-tuple-element.16.table_ref, f32[2,8,6,16,128]{4,3,2,1,0:T(8,128)S(1)} %shard_map.55.refs_0_.refs_1_.piece_ref), custom_call_target="tpu_custom_call" | custom-call | flops 16384000 | bytes 1679360 | tf_op jit(solution)/shard_map/pallas_call | solution.py:38
  90.2 1.8 %shard_map.57.refs_3_ = f32[16,128]{1,0:T(8,128)S(1)} custom-call(f32[2,54,16,128]{3,2,1,0:T(8,128)S(1)} %get-tuple-element.16.table_ref, f32[1,8,6,16,128]{4,3,2,1,0:T(8,128)S(1)} %shard_map.54.refs_0_.piece_ref, f32[2,8,6,16,128]{4,3,2,1,0:T(8,128)S(1)} %shard_map.55.refs_0_.refs_1_.piece_ref, f32[16,128]{1,0:T(8,128)S(1)} %shard_map.56.refs_2_), custom_call_target="tpu_custom_call" | custom-call | flops 8192000 | bytes 2080768 | tf_op jit(solution)/shard_map/pallas_call | solution.py:38
  92.0 2.5 %shard_map.58.refs_1_ = f32[16,128]{1,0:T(8,128)S(1)} custom-call(f32[2,54,16,128]{3,2,1,0:T(8,128)S(1)} %get-tuple-element.16.table_ref, f32[1,8,6,16,128]{4,3,2,1,0:T(8,128)S(1)} %shard_map.54.refs_0_.piece_ref, f32[2,8,6,16,128]{4,3,2,1,0:T(8,128)S(1)} %shard_map.55.refs_0_.refs_1_.piece_ref, ...), custom_call_target="tpu_custom_call" | custom-call | flops 16384000 | bytes 2473984 | tf_op jit(solution)/shard_map/pallas_call | solution.py:38
  94.4 1.2 shard_map.59
  95.6 3.5 %collective-permute-start.11 = (f32[16,128]{1,0:T(8,128)S(1)}, f32[16,128]{1,0:T(8,128)S(1)}, u32[]{:S(2)}, u32[]{:S(2)}) collective-permute-start(f32[16,128]{1,0:T(8,128)S(1)} %shard_map.59), channel_id=1, source_target_pairs={{0,3},{1,2},{2,1},{3,0},{4,7},{5,6},{6,5},{7,4},{8,11},{9,10},{10,... | collective-permute-start | bytes 24584 | tf_op jit(solution)/shard_map/ppermute | solution.py:391
  99.5 1.2 collective-permute-done.11
  100.7 1.9 %collective-permute-start.9 = (f32[16,128]{1,0:T(8,128)S(1)}, f32[16,128]{1,0:T(8,128)S(1)}, u32[]{:S(2)}, u32[]{:S(2)}) collective-permute-start(f32[16,128]{1,0:T(8,128)S(1)} %shard_map.59), channel_id=1, source_target_pairs={{0,1},{1,0},{2,3},{3,2},{4,5},{5,4},{6,7},{7,6},{8,9},{9,8},{10,11... | collective-permute-start | bytes 24584 | tf_op jit(solution)/shard_map/ppermute | solution.py:391
  102.7 1.6 %collective-permute-done.9 = f32[16,128]{1,0:T(8,128)S(1)} collective-permute-done((f32[16,128]{1,0:T(8,128)S(1)}, f32[16,128]{1,0:T(8,128)S(1)}, u32[]{:S(2)}, u32[]{:S(2)}) %collective-permute-start.9) | collective-permute-done | bytes 8224 | tf_op jit(solution)/shard_map/ppermute | solution.py:391
  104.4 3.8 %collective-permute-start.14 = (f32[16,128]{1,0:T(8,128)S(1)}, f32[16,128]{1,0:T(8,128)S(1)}, u32[]{:S(2)}, u32[]{:S(2)}) collective-permute-start(f32[16,128]{1,0:T(8,128)S(1)} %add_add_fusion.refs_0_), channel_id=1, source_target_pairs={{0,20},{1,21},{2,22},{3,23},{4,16},{5,17},{6,18},{7,19},{16,4},{17... | collective-permute-start | bytes 24584 | tf_op jit(solution)/shard_map/ppermute | solution.py:401
  108.2 1.5 %collective-permute-start.13 = (f32[16,128]{1,0:T(8,128)S(1)}, f32[16,128]{1,0:T(8,128)S(1)}, u32[]{:S(2)}, u32[]{:S(2)}) collective-permute-start(f32[16,128]{1,0:T(8,128)S(1)} %add_add_fusion.refs_0_), channel_id=1, source_target_pairs={{0,16},{1,17},{2,18},{3,19},{4,20},{5,21},{6,22},{7,23},{16,0},{17... | collective-permute-start | bytes 24584 | tf_op jit(solution)/shard_map/ppermute | solution.py:401
  112.9 1.3 %collective-permute-done.12.refs_1_ = f32[16,128]{1,0:T(8,128)S(1)} collective-permute-done((f32[16,128]{1,0:T(8,128)S(1)}, f32[16,128]{1,0:T(8,128)S(1)}, u32[]{:S(2)}, u32[]{:S(2)}) %collective-permute-start.12) | collective-permute-done | bytes 8224 | tf_op jit(solution)/shard_map/ppermute | solution.py:391
  114.2 3.0 %shard_map.66 = (f32[6144,128]{1,0:T(8,128)}, f32[2,2,2,16,16]{4,3,2,1,0:T(8,128)}) custom-call(s32[3]{0:T(128)S(1)} %pad_add_fusion.pick_ref.slot_ref, f32[16,128]{1,0:T(8,128)S(1)} %add_add_fusion.refs_0_, f32[16,128]{1,0:T(8,128)S(1)} %collective-permute-done.12.refs_1_, f32[3072,128]{1,0:T(8,128)S(1)} %shard_map.62.refs_2_, ...), custom_call_target="tpu_custom_call" | custom-call | flops 1000000 | bytes 6332416 | tf_op jit(solution)/shard_map/pallas_call | solution.py:45
  (33 shorter events, 7.1 us)
Async XLA Ops:
  1.7 11.1 %collective-permute-start = (f32[54,4,512]{2,1,0:T(4,128)S(1)}, f32[54,4,512]{2,1,0:T(4,128)S(1)}, u32[]{:S(2)}, u32[]{:S(2)}) collective-permute-start(f32[54,4,512]{2,1,0:T(4,128)S(1)} %dynamic-slice_bitcast_fusion), channel_id=1, source_target_pairs={{0,8},{8,0},{1,9},{9,1},{2,10},{10,2},{3,11},{11,3},{4,12},{12,4},... | collective-permute-start | bytes 1327112 | tf_op jit(solution)/shard_map/ppermute | solution.py:391
  4.9 18.7 %collective-permute-start.3 = (f32[1,8,6,16,128]{4,3,2,1,0:T(8,128)S(1)}, f32[1,8,6,16,128]{4,3,2,1,0:T(8,128)S(1)}, u32[]{:S(2)}, u32[]{:S(2)}) collective-permute-start(f32[1,8,6,16,128]{4,3,2,1,0:T(8,128)S(1)} %get-tuple-element.18.refs_0_.refs_3_.refs_2_), channel_id=1, source_target_pairs={{0,7},{1,0},{2,1},{3,2},{4,3},{5,4},{6,5},{7,6},{8,15},{9,8},{10,9... | collective-permute-start | bytes 1179656 | tf_op jit(solution)/shard_map/ppermute | solution.py:387
  12.7 21.6 %collective-permute-start.2 = (f32[1,8,6,16,128]{4,3,2,1,0:T(8,128)S(1)}, f32[1,8,6,16,128]{4,3,2,1,0:T(8,128)S(1)}, u32[]{:S(2)}, u32[]{:S(2)}) collective-permute-start(f32[1,8,6,16,128]{4,3,2,1,0:T(8,128)S(1)} %shard_map.42.refs_2_.refs_4_), channel_id=1, source_target_pairs={{0,1},{1,2},{2,3},{3,4},{4,5},{5,6},{6,7},{7,0},{8,9},{9,10},{10,1... | collective-permute-start | bytes 1179656 | tf_op jit(solution)/shard_map/ppermute | solution.py:387
  18.9 31.9 %collective-permute-start.6 = (f32[1,8,6,16,128]{4,3,2,1,0:T(8,128)S(1)}, f32[1,8,6,16,128]{4,3,2,1,0:T(8,128)S(1)}, u32[]{:S(2)}, u32[]{:S(2)}) collective-permute-start(f32[1,8,6,16,128]{4,3,2,1,0:T(8,128)S(1)} %get-tuple-element.20.refs_2_), channel_id=1, source_target_pairs={{0,7},{1,0},{2,1},{3,2},{4,3},{5,4},{6,5},{7,6},{8,15},{9,8},{10,9... | collective-permute-start | bytes 1179656 | tf_op jit(solution)/shard_map/ppermute | solution.py:387
  23.6 27.6 %collective-permute-start.5 = (f32[1,8,6,16,128]{4,3,2,1,0:T(8,128)S(1)}, f32[1,8,6,16,128]{4,3,2,1,0:T(8,128)S(1)}, u32[]{:S(2)}, u32[]{:S(2)}) collective-permute-start(f32[1,8,6,16,128]{4,3,2,1,0:T(8,128)S(1)} %get-tuple-element.21.refs_2_), channel_id=1, source_target_pairs={{0,1},{1,2},{2,3},{3,4},{4,5},{5,6},{6,7},{7,0},{8,9},{9,10},{10,1... | collective-permute-start | bytes 1179656 | tf_op jit(solution)/shard_map/ppermute | solution.py:387
  23.6 20.7 %collective-permute-start.1 = (f32[18,8,128]{2,1,0:T(8,128)S(1)}, f32[18,8,128]{2,1,0:T(8,128)S(1)}, u32[]{:S(2)}, u32[]{:S(2)}) collective-permute-start(f32[18,8,128]{2,1,0:T(8,128)S(1)} %get-tuple-element.15.refs_0_.links_ref), channel_id=1, source_target_pairs={{0,1},{1,2},{2,3},{3,4},{4,5},{5,6},{6,7},{7,0},{8,9},{9,10},{10,1... | collective-permute-start | bytes 221192 | tf_op jit(solution)/shard_map/ppermute | solution.py:387
  54.9 54.8 %collective-permute-start.17 = (f32[2,8,6,16,128]{4,3,2,1,0:T(8,128)S(1)}, f32[2,8,6,16,128]{4,3,2,1,0:T(8,128)S(1)}, u32[]{:S(2)}, u32[]{:S(2)}) collective-permute-start(f32[2,8,6,16,128]{4,3,2,1,0:T(8,128)S(1)} %shard_map.55.refs_0_.refs_1_.piece_ref), channel_id=1, source_target_pairs={{0,16},{16,0},{1,17},{17,1},{2,18},{18,2},{3,19},{19,3},{4,20},{20... | collective-permute-start | bytes 2359304 | tf_op jit(solution)/shard_map/ppermute | solution.py:391
  56.4 27.6 %collective-permute-start.8 = (f32[1,8,6,16,128]{4,3,2,1,0:T(8,128)S(1)}, f32[1,8,6,16,128]{4,3,2,1,0:T(8,128)S(1)}, u32[]{:S(2)}, u32[]{:S(2)}) collective-permute-start(f32[1,8,6,16,128]{4,3,2,1,0:T(8,128)S(1)} %get-tuple-element.23.refs_3_), channel_id=1, source_target_pairs={{0,1},{1,2},{2,3},{3,4},{4,5},{5,6},{6,7},{7,0},{8,9},{9,10},{10,1... | collective-permute-start | bytes 1179656 | tf_op jit(solution)/shard_map/ppermute | solution.py:387
  58.9 26.2 %collective-permute-start.4 = (f32[1,8,6,16,128]{4,3,2,1,0:T(8,128)S(1)}, f32[1,8,6,16,128]{4,3,2,1,0:T(8,128)S(1)}, u32[]{:S(2)}, u32[]{:S(2)}) collective-permute-start(f32[1,8,6,16,128]{4,3,2,1,0:T(8,128)S(1)} %get-tuple-element.22.refs_3_), channel_id=1, source_target_pairs={{0,7},{1,0},{2,1},{3,2},{4,3},{5,4},{6,5},{7,6},{8,15},{9,8},{10,9... | collective-permute-start | bytes 1179656 | tf_op jit(solution)/shard_map/ppermute | solution.py:387
  66.5 27.9 %collective-permute-start.7 = (f32[1,8,6,16,128]{4,3,2,1,0:T(8,128)S(1)}, f32[1,8,6,16,128]{4,3,2,1,0:T(8,128)S(1)}, u32[]{:S(2)}, u32[]{:S(2)}) collective-permute-start(f32[1,8,6,16,128]{4,3,2,1,0:T(8,128)S(1)} %get-tuple-element.25.refs_3_), channel_id=1, source_target_pairs={{0,7},{1,0},{2,1},{3,2},{4,3},{5,4},{6,5},{7,6},{8,15},{9,8},{10,9... | collective-permute-start | bytes 1179656 | tf_op jit(solution)/shard_map/ppermute | solution.py:387
  84.5 27.6 %collective-permute-start.16 = (f32[1,8,6,16,128]{4,3,2,1,0:T(8,128)S(1)}, f32[1,8,6,16,128]{4,3,2,1,0:T(8,128)S(1)}, u32[]{:S(2)}, u32[]{:S(2)}) collective-permute-start(f32[1,8,6,16,128]{4,3,2,1,0:T(8,128)S(1)} %shard_map.54.refs_0_.piece_ref), channel_id=1, source_target_pairs={{0,16},{16,0},{1,17},{17,1},{2,18},{18,2},{3,19},{19,3},{4,20},{20... | collective-permute-start | bytes 1179656 | tf_op jit(solution)/shard_map/ppermute | solution.py:391
  85.5 27.0 %collective-permute-start.15 = (f32[1,8,6,16,128]{4,3,2,1,0:T(8,128)S(1)}, f32[1,8,6,16,128]{4,3,2,1,0:T(8,128)S(1)}, u32[]{:S(2)}, u32[]{:S(2)}) collective-permute-start(f32[1,8,6,16,128]{4,3,2,1,0:T(8,128)S(1)} %shard_map.53.refs_2_.top_ref.piece_ref), channel_id=1, source_target_pairs={{0,16},{16,0},{1,17},{17,1},{2,18},{18,2},{3,19},{19,3},{4,20},{20... | collective-permute-start | bytes 1179656 | tf_op jit(solution)/shard_map/ppermute | solution.py:391
  95.6 5.1 %collective-permute-start.11 = (f32[16,128]{1,0:T(8,128)S(1)}, f32[16,128]{1,0:T(8,128)S(1)}, u32[]{:S(2)}, u32[]{:S(2)}) collective-permute-start(f32[16,128]{1,0:T(8,128)S(1)} %shard_map.59), channel_id=1, source_target_pairs={{0,3},{1,2},{2,1},{3,0},{4,7},{5,6},{6,5},{7,4},{8,11},{9,10},{10,... | collective-permute-start | bytes 24584 | tf_op jit(solution)/shard_map/ppermute | solution.py:391
  99.1 3.7 %collective-permute-start.10 = (f32[16,128]{1,0:T(8,128)S(1)}, f32[16,128]{1,0:T(8,128)S(1)}, u32[]{:S(2)}, u32[]{:S(2)}) collective-permute-start(f32[16,128]{1,0:T(8,128)S(1)} %shard_map.59), channel_id=1, source_target_pairs={{0,2},{1,3},{2,0},{3,1},{4,6},{5,7},{6,4},{7,5},{8,10},{9,11},{10,... | collective-permute-start | bytes 24584 | tf_op jit(solution)/shard_map/ppermute | solution.py:391
  100.7 3.7 %collective-permute-start.9 = (f32[16,128]{1,0:T(8,128)S(1)}, f32[16,128]{1,0:T(8,128)S(1)}, u32[]{:S(2)}, u32[]{:S(2)}) collective-permute-start(f32[16,128]{1,0:T(8,128)S(1)} %shard_map.59), channel_id=1, source_target_pairs={{0,1},{1,0},{2,3},{3,2},{4,5},{5,4},{6,7},{7,6},{8,9},{9,8},{10,11... | collective-permute-start | bytes 24584 | tf_op jit(solution)/shard_map/ppermute | solution.py:391
  104.4 8.5 %collective-permute-start.14 = (f32[16,128]{1,0:T(8,128)S(1)}, f32[16,128]{1,0:T(8,128)S(1)}, u32[]{:S(2)}, u32[]{:S(2)}) collective-permute-start(f32[16,128]{1,0:T(8,128)S(1)} %add_add_fusion.refs_0_), channel_id=1, source_target_pairs={{0,20},{1,21},{2,22},{3,23},{4,16},{5,17},{6,18},{7,19},{16,4},{17... | collective-permute-start | bytes 24584 | tf_op jit(solution)/shard_map/ppermute | solution.py:401
  108.2 4.7 %collective-permute-start.13 = (f32[16,128]{1,0:T(8,128)S(1)}, f32[16,128]{1,0:T(8,128)S(1)}, u32[]{:S(2)}, u32[]{:S(2)}) collective-permute-start(f32[16,128]{1,0:T(8,128)S(1)} %add_add_fusion.refs_0_), channel_id=1, source_target_pairs={{0,16},{1,17},{2,18},{3,19},{4,20},{5,21},{6,22},{7,23},{16,0},{17... | collective-permute-start | bytes 24584 | tf_op jit(solution)/shard_map/ppermute | solution.py:401
  109.7 4.6 %collective-permute-start.12 = (f32[16,128]{1,0:T(8,128)S(1)}, f32[16,128]{1,0:T(8,128)S(1)}, u32[]{:S(2)}, u32[]{:S(2)}) collective-permute-start(f32[16,128]{1,0:T(8,128)S(1)} %add_add_fusion.refs_0_), channel_id=1, source_target_pairs={{0,4},{1,5},{2,6},{3,7},{4,0},{5,1},{6,2},{7,3},{8,12},{9,13},{10,... | collective-permute-start | bytes 24584 | tf_op jit(solution)/shard_map/ppermute | solution.py:391

commit v5 on v3

--- a/solution.py
+++ b/solution.py
@@ -16,6 +16,7 @@
 VMEM = pl.BlockSpec(memory_space=pltpu.VMEM)
 FAR = pl.BlockSpec(memory_space=pltpu.HBM)
 GRANT = 16 * 2**20
+GROUP = 8
 
 
 def shape_of(*dims, dtype=F32):
@@ -249,17 +250,20 @@
 
 
 def products(acc_ref, rows, own, sides):
-    def body(pair, _):
+    group = min(rows, GROUP)
+    assert rows % group == 0
+
+    def body(step, _):
         stacks = [[], []]
-        for c in (2 * pair, 2 * pair + 1):
-            for stack, tiles in zip(stacks, sides(c)):
+        for k in range(group):
+            for stack, tiles in zip(stacks, sides(group * step + k)):
                 stack.append(jnp.concatenate(high_low(tiles), axis=0))
         left, right = [jnp.concatenate(s, axis=1) for s in stacks]
         right = jnp.concatenate([left if own else jnp.zeros_like(left), right], axis=0)
         acc_ref[...] += lax.dot_general(left, right, (((1,), (1,)), ((), ())), preferred_element_type=F32)
         return 0
 
-    lax.fori_loop(0, rows // 2, body, 0)
+    lax.fori_loop(0, rows // group, body, 0)
 
 
 def packed_product(acc, n):
@@ -329,32 +333,43 @@
     lax.fori_loop(0, rows, body, 0)
 
 
-def final_kernel(chunks, slot_ref, *refs):
-    far_ref, grams_ref, scale_ref, ready_ref, sems = refs[-5:]
+def scale_out(field_ref, far_ref, slot, inverse, chunks, scale_ref, ready_ref, sems):
+    n = inverse.shape[0]
+    size = field_ref.shape[0] // n
+    each = n // chunks
+    scale_ref[...] = jnp.broadcast_to(inverse, (n, LANES))
     copies = []
-    for k in range(2):
-        term0, term1, field_ref = refs[3 * k : 3 * k + 3]
-        n = term0.shape[0]
-        size = field_ref.shape[0] // n
-        each = n // chunks
-        slot = slot_ref[0] if k == 0 else 1 - slot_ref[0]
-        packed = term0[...] + term1[...]
+    for j in range(chunks):
+
+        def body(i, _, j=j):
+            vec = j * each + i
+            block = pl.ds(pl.multiple_of(vec * size, 8), size)
+            ready_ref[block, :] = field_ref[block, :] * scale_ref[pl.ds(vec, 1), :]
+            return 0
+
+        lax.fori_loop(0, each, body, 0)
+        part = pl.ds(j * each * size, each * size)
+        target = pl.ds(slot * (n * size) + j * each * size, each * size)
+        copies.append(pltpu.make_async_copy(ready_ref.at[part], far_ref.at[target], sems.at[j]))
+        copies[-1].start()
+    return copies
+
+
+def mine_kernel(chunks, slot_ref, sum_ref, field_ref, far_ref, *scratch):
+    inverse = lax.rsqrt(jnp.sum(norms_of(sum_ref[...]), axis=1, keepdims=True))
+    for copy in scale_out(field_ref, far_ref, slot_ref[0], inverse, chunks, *scratch):
+        copy.wait()
+
+
+def other_kernel(chunks, slot_ref, mine_ref, other_ref, field_ref, _, far_ref, grams_ref, *scratch):
+    parts = []
+    for slot, ref in ((1 - slot_ref[0], other_ref), (slot_ref[0], mine_ref)):
+        packed = ref[...]
         norm = norms_of(packed)
-        down = lax.rsqrt(jnp.sum(norm, axis=1, keepdims=True))
-        scale_ref[...] = jnp.broadcast_to(down, (n, LANES))
-        for j in range(chunks):
-
-            def body(i, _, field_ref=field_ref, j=j, k=k):
-                vec = j * each + i
-                block = pl.ds(pl.multiple_of(vec * size, 8), size)
-                ready_ref[k, block, :] = field_ref[block, :] * scale_ref[pl.ds(vec, 1), :]
-                return 0
-
-            lax.fori_loop(0, each, body, 0)
-            part = pl.ds(j * each * size, each * size)
-            target = pl.ds(slot * (n * size) + j * each * size, each * size)
-            copies.append(pltpu.make_async_copy(ready_ref.at[k, part], far_ref.at[target], sems.at[k, j]))
-            copies[-1].start()
+        parts.append((slot, packed, norm, lax.rsqrt(jnp.sum(norm, axis=1, keepdims=True))))
+    copies = scale_out(field_ref, far_ref, 1 - slot_ref[0], parts[0][3], chunks, *scratch)
+    n = mine_ref.shape[0]
+    for slot, packed, norm, down in parts:
         across = lax.rsqrt(jnp.sum(norm, axis=0, keepdims=True)[:, 0:n])
         scale = down * across
         over_re, over_im = packed[:, 0:n], packed[:, n : 2 * n]
@@ -380,19 +395,12 @@
     size = lax.axis_size("sa")
     count = size.bit_length() - 1
     assert size == 1 << count
-
-    def across(x, cfg, bits):
-        pairs = range(lax.axis_size("cfg") * size)
-        return lax.ppermute(x, ("cfg", "sa"), [(i, i ^ (cfg * size + bits)) for i in pairs])
-
     bit = 1
-    for _ in range((count - 1) // 2):
-        x = x + flipped(x, "sa", bit) + flipped(x, "sa", 2 * bit) + flipped(x, "sa", 3 * bit)
-        bit *= 4
-    if count % 2 == 0:
-        x = x + flipped(x, "sa", bit)
-        bit *= 2
-    return (x, flipped(x, "sa", bit)), (across(x, 1, 0), across(x, 1, bit))
+    while bit < size:
+        bits = (bit, 2 * bit, 3 * bit) if 4 * bit <= size else (bit,)
+        x = sum([flipped(x, "sa", k) for k in bits], x)
+        bit = bit * (4 if len(bits) == 3 else 2)
+    return x
 
 
 def on_device(links, vectors):
@@ -494,7 +502,8 @@
         last_hop_kernel, packed, top_links, three[-1], above, sofar,
         scratch=acc, ops=work / 4,
     )
-    sum_mine, sum_other = summed(sofar)
+    sum_mine = summed(sofar)
+    sum_other = flipped(sum_mine, "cfg", 1)
     other = [swapped(x) for x in three]
 
     def scattered(planes):
@@ -508,11 +517,16 @@
 
     chunks = 4
     assert vecs % chunks == 0
+    scratch = [pltpu.VMEM((vecs, LANES), F32), pltpu.VMEM((many, LANES), F32), sem((chunks,))]
+    ours, theirs = scattered(three), scattered(other)
+    (out,) = call(
+        functools.partial(mine_kernel, chunks), [shape_of(2 * many, LANES)],
+        sum_mine, ours, pick=pick, far_out=(0,), ops=1e6, scratch=scratch,
+    )
     out, grams = call(
-        functools.partial(final_kernel, chunks), [shape_of(2 * many, LANES), shape_of(2, 2, 2, vecs, vecs)],
-        *sum_mine, scattered(three), *sum_other, scattered(other),
-        pick=pick, far_out=(0,), ops=1e6,
-        scratch=[pltpu.VMEM((vecs, LANES), F32), pltpu.VMEM((2, many, LANES), F32), sem((2, chunks))],
+        functools.partial(other_kernel, chunks), [shape_of(2 * many, LANES), shape_of(2, 2, 2, vecs, vecs)],
+        sum_mine, sum_other, theirs, out, pick=pick, far=(3,), far_out=(0,), ops=1e6, scratch=scratch,
+        alias={4: 0},
     )
     return from_rows(out, vectors.shape), grams
 

time: 99.1 us -> 99.8 us (level)
  waiting for transfers between devices: 26.9 us -> 30.7 us
  Pallas kernels: 42.5 us -> 39.3 us
    pallas_call x22, Pallas kernels: 31.6 us -> 27.1 us  [call(): pl.pallas_call(kernel, in_specs=in_specs, out_specs=out_specs, scratch_sh...]
    ppermute x8 -> x9, starting transfers between devices: 7.22 us -> 11.2 us  [flipped(): lax.ppermute(x, axis, [(i, i ^ bit) for i in range(lax.axis_size(axis))])]
    ppermute x2 -> x0, starting transfers between devices: 4.01 us -> none  [across(): lax.ppermute(x, ('cfg', 'sa'), [(i, i ^ cfg * size + bits) for i in pairs])]
    ppermute x8 -> x9, waiting for transfers between devices: 5.91 us -> 8.27 us  [flipped(): lax.ppermute(x, axis, [(i, i ^ bit) for i in range(lax.axis_size(axis))])]
    ppermute x8, waiting for transfers between devices: 21 us -> 22.5 us  [shifted(): return lax.ppermute(x, axis, [(i, (i + by) % n) for i in range(n)])]
    pallas_call x4 -> x5, Pallas kernels: 10.9 us -> 12.1 us  [call(): return pl.pallas_call(kernel, grid_spec=spec, **params)(pick, *args)]
  transfers between devices with their start and end apart: 18 -> 17, of which waited for: 8 -> 10; matrix products, arithmetic and copies ran while one was open for 0% -> 0% of each run, Pallas kernels for 40% -> 37%
where the time goes in v5:
time: 99.8 us; the launch traced here: 99.5 us
  Pallas kernels  39.3 us (39%)
  waiting for transfers between devices  30.7 us (31%)
  starting transfers between devices  27.5 us (28%)
  local copies, waits for them, and re-layouts  1.05 us (1%)
    pallas_call x22, Pallas kernels, call(): pl.pallas_call(kernel, in_specs=in_specs, out_specs=out_specs, scratch_sh...  27.1 us
    ppermute x8, waiting for transfers between devices, shifted(): return lax.ppermute(x, axis, [(i, (i + by) % n) for i in range(n)])  22.5 us
    ppermute x8, starting transfers between devices, shifted(): return lax.ppermute(x, axis, [(i, (i + by) % n) for i in range(n)])  16.2 us
    pallas_call x5, Pallas kernels, call(): return pl.pallas_call(kernel, grid_spec=spec, **params)(pick, *args)  12.1 us
    ppermute x9, starting transfers between devices, flipped(): lax.ppermute(x, axis, [(i, i ^ bit) for i in range(lax.axis_size(axis))])  11.2 us
    ppermute x9, waiting for transfers between devices, flipped(): lax.ppermute(x, axis, [(i, i ^ bit) for i in range(lax.axis_size(axis))])  8.27 us
  transfers between devices with their start and end apart: 17, of which 10 were waited for; matrix products, arithmetic and copies ran while one was open for 0% of the time, Pallas kernels for 37%

profile of v5, /device:TPU:0, one launch (start us, length us, event | category | flops | bytes accessed | tf_op | source)
XLA Modules:
  0.0 99.5 jit_solution(13699671460688540248)
XLA Ops:
  0.6 1.0 %dynamic-slice_bitcast_fusion = f32[54,4,512]{2,1,0:T(4,128)S(1)} fusion(f32[4,54,4,512]{3,2,1,0:T(4,128)} %bitcast.30, s32[]{:T(128)S(6)} %select_n.12), kind=kLoop, calls=%fused_computation | loop fusion | bytes 884740 | tf_op jit(solution)/shard_map/jit(dynamic_index_in_dim)/squeeze | solution.py:435
  2.3 2.2 %shard_map.43.refs_2_.refs_4_ = f32[1,8,6,16,128]{4,3,2,1,0:T(8,128)S(1)} custom-call(s32[3]{0:T(128)S(1)} %pad_add_fusion.pick_ref.slot_ref, f32[6144,128]{1,0:T(8,128)} %bitcast.28), custom_call_target="tpu_custom_call" | custom-call | flops 100000 | bytes 3538944 | tf_op jit(solution)/shard_map/pallas_call | solution.py:45
  4.5 2.6 %collective-permute-start.4 = (f32[1,8,6,16,128]{4,3,2,1,0:T(8,128)S(1)}, f32[1,8,6,16,128]{4,3,2,1,0:T(8,128)S(1)}, u32[]{:S(2)}, u32[]{:S(2)}) collective-permute-start(f32[1,8,6,16,128]{4,3,2,1,0:T(8,128)S(1)} %shard_map.43.refs_2_.refs_4_), channel_id=1, source_target_pairs={{0,1},{1,2},{2,3},{3,4},{4,5},{5,6},{6,7},{7,0},{8,9},{9,10},{10,1... | collective-permute-start | bytes 1179656 | tf_op jit(solution)/shard_map/ppermute | solution.py:387
  7.1 2.6 %shard_map.42 = (f32[1,8,6,16,128]{4,3,2,1,0:T(8,128)S(1)}, f32[2,8,6,16,128]{4,3,2,1,0:T(8,128)S(1)}) custom-call(s32[3]{0:T(128)S(1)} %pad_add_fusion.pick_ref.slot_ref, f32[6144,128]{1,0:T(8,128)} %bitcast.29), custom_call_target="tpu_custom_call" | custom-call | flops 100000 | bytes 4325376 | tf_op jit(solution)/shard_map/pallas_call | solution.py:45
  9.7 3.1 %collective-permute-start.2 = (f32[1,8,6,16,128]{4,3,2,1,0:T(8,128)S(1)}, f32[1,8,6,16,128]{4,3,2,1,0:T(8,128)S(1)}, u32[]{:S(2)}, u32[]{:S(2)}) collective-permute-start(f32[1,8,6,16,128]{4,3,2,1,0:T(8,128)S(1)} %get-tuple-element.16.refs_0_.refs_3_), channel_id=1, source_target_pairs={{0,7},{1,0},{2,1},{3,2},{4,3},{5,4},{6,5},{7,6},{8,15},{9,8},{10,9... | collective-permute-start | bytes 1179656 | tf_op jit(solution)/shard_map/ppermute | solution.py:387
  12.8 3.1 %shard_map.41 = (f32[2,54,16,128]{3,2,1,0:T(8,128)S(1)}, f32[2,36,16,128]{3,2,1,0:T(8,128)S(1)}, f32[18,8,128]{2,1,0:T(8,128)S(1)}) custom-call(s32[3]{0:T(128)S(1)} %pad_add_fusion.pick_ref.slot_ref, f32[4,54,16,128]{3,2,1,0:T(8,128)} %bitcast.31, f32[54,16,128]{2,1,0:T(8,128)S(1)} %bitcast.26), custom_call_target="tpu_custom_call" | custom-call | flops 1000000 | bytes 3760128 | tf_op jit(solution)/shard_map/pallas_call | solution.py:45
  15.9 3.0 %shard_map.44 = (f32[1,8,6,16,128]{4,3,2,1,0:T(8,128)S(1)}, f32[1,8,6,16,128]{4,3,2,1,0:T(8,128)S(1)}) custom-call(f32[2,54,16,128]{3,2,1,0:T(8,128)S(1)} %get-tuple-element.17.table_ref, f32[2,36,16,128]{3,2,1,0:T(8,128)S(1)} %get-tuple-element.18.behind_ref, f32[1,8,6,16,128]{4,3,2,1,0:T(8,128)S(1)} %get-tuple-element.16.refs_0_.refs_3_, ...), custom_call_target="tpu_custom_call" | custom-call | flops 32768000 | bytes 3833856 | tf_op jit(solution)/shard_map/pallas_call | solution.py:38
  18.9 6.1 %collective-permute-done.4.refs_1_ = f32[1,8,6,16,128]{4,3,2,1,0:T(8,128)S(1)} collective-permute-done((f32[1,8,6,16,128]{4,3,2,1,0:T(8,128)S(1)}, f32[1,8,6,16,128]{4,3,2,1,0:T(8,128)S(1)}, u32[]{:S(2)}, u32[]{:S(2)}) %collective-permute-start.4) | collective-permute-done | bytes 393248 | tf_op jit(solution)/shard_map/ppermute | solution.py:387
  25.0 1.1 %collective-permute-done.1.refs_0_ = f32[18,8,128]{2,1,0:T(8,128)S(1)} collective-permute-done((f32[18,8,128]{2,1,0:T(8,128)S(1)}, f32[18,8,128]{2,1,0:T(8,128)S(1)}, u32[]{:S(2)}, u32[]{:S(2)}) %collective-permute-start.1) | collective-permute-done | bytes 73760 | tf_op jit(solution)/shard_map/ppermute | solution.py:387
  26.3 5.6 %collective-permute-start.6 = (f32[1,8,6,16,128]{4,3,2,1,0:T(8,128)S(1)}, f32[1,8,6,16,128]{4,3,2,1,0:T(8,128)S(1)}, u32[]{:S(2)}, u32[]{:S(2)}) collective-permute-start(f32[1,8,6,16,128]{4,3,2,1,0:T(8,128)S(1)} %shard_map.46.refs_0_.refs_3_), channel_id=1, source_target_pairs={{0,7},{1,0},{2,1},{3,2},{4,3},{5,4},{6,5},{7,6},{8,15},{9,8},{10,9... | collective-permute-start | bytes 1179656 | tf_op jit(solution)/shard_map/ppermute | solution.py:387
  32.2 3.2 %shard_map.47.refs_1_.refs_3_ = f32[2,8,6,16,128]{4,3,2,1,0:T(8,128)S(1)} custom-call(f32[2,54,16,128]{3,2,1,0:T(8,128)S(1)} %get-tuple-element.17.table_ref, f32[2,36,16,128]{3,2,1,0:T(8,128)S(1)} %get-tuple-element.18.behind_ref, f32[1,8,6,16,128]{4,3,2,1,0:T(8,128)S(1)} %get-tuple-element.16.refs_0_.refs_3_, ...), custom_call_target="tpu_custom_call" | custom-call | flops 32768000 | bytes 3833856 | tf_op jit(solution)/shard_map/pallas_call | solution.py:38
  35.4 3.0 %shard_map.48 = (f32[1,8,6,16,128]{4,3,2,1,0:T(8,128)S(1)}, f32[1,8,6,16,128]{4,3,2,1,0:T(8,128)S(1)}) custom-call(f32[2,54,16,128]{3,2,1,0:T(8,128)S(1)} %get-tuple-element.17.table_ref, f32[2,36,16,128]{3,2,1,0:T(8,128)S(1)} %get-tuple-element.18.behind_ref, f32[1,8,6,16,128]{4,3,2,1,0:T(8,128)S(1)} %shard_map.46.refs_0_.refs_3_, ...), custom_call_target="tpu_custom_call" | custom-call | flops 32768000 | bytes 4620288 | tf_op jit(solution)/shard_map/pallas_call | solution.py:38
  38.4 8.3 %collective-permute-done.6.refs_1_ = f32[1,8,6,16,128]{4,3,2,1,0:T(8,128)S(1)} collective-permute-done((f32[1,8,6,16,128]{4,3,2,1,0:T(8,128)S(1)}, f32[1,8,6,16,128]{4,3,2,1,0:T(8,128)S(1)}, u32[]{:S(2)}, u32[]{:S(2)}) %collective-permute-start.6) | collective-permute-done | bytes 393248 | tf_op jit(solution)/shard_map/ppermute | solution.py:387
  47.0 3.2 %shard_map.50.refs_1_ = f32[2,8,6,16,128]{4,3,2,1,0:T(8,128)S(1)} custom-call(f32[2,54,16,128]{3,2,1,0:T(8,128)S(1)} %get-tuple-element.17.table_ref, f32[2,36,16,128]{3,2,1,0:T(8,128)S(1)} %get-tuple-element.18.behind_ref, f32[1,8,6,16,128]{4,3,2,1,0:T(8,128)S(1)} %shard_map.46.refs_0_.refs_3_, f32[2,8,6,16,128]{4,3,2,1,0:T(8,128)S(1)} %shard_map.47.refs_1_.refs_3_, ...), custom_call_target="tpu_custom_call" | custom-call | flops 32768000 | bytes 4620288 | tf_op jit(solution)/shard_map/pallas_call | solution.py:38
  50.5 4.8 %collective-permute-start.5 = (f32[1,8,6,16,128]{4,3,2,1,0:T(8,128)S(1)}, f32[1,8,6,16,128]{4,3,2,1,0:T(8,128)S(1)}, u32[]{:S(2)}, u32[]{:S(2)}) collective-permute-start(f32[1,8,6,16,128]{4,3,2,1,0:T(8,128)S(1)} %shard_map.49.refs_0_), channel_id=1, source_target_pairs={{0,7},{1,0},{2,1},{3,2},{4,3},{5,4},{6,5},{7,6},{8,15},{9,8},{10,9... | collective-permute-start | bytes 1179656 | tf_op jit(solution)/shard_map/ppermute | solution.py:387
  55.3 3.2 %shard_map.55.refs_0_.refs_1_.piece_ref = f32[2,8,6,16,128]{4,3,2,1,0:T(8,128)S(1)} custom-call(f32[2,54,16,128]{3,2,1,0:T(8,128)S(1)} %get-tuple-element.17.table_ref, f32[2,36,16,128]{3,2,1,0:T(8,128)S(1)} %get-tuple-element.18.behind_ref, f32[1,8,6,16,128]{4,3,2,1,0:T(8,128)S(1)} %shard_map.49.refs_0_, f32[2,8,6,16,128]{4,3,2,1,0:T(8,128)S(1)} %shard_map.50.refs_1_, ...), custom_call_target="tpu_custom_call" | custom-call | flops 32768000 | bytes 4620288 | tf_op jit(solution)/shard_map/pallas_call | solution.py:38
  58.5 1.6 %collective-permute-start.16 = (f32[2,8,6,16,128]{4,3,2,1,0:T(8,128)S(1)}, f32[2,8,6,16,128]{4,3,2,1,0:T(8,128)S(1)}, u32[]{:S(2)}, u32[]{:S(2)}) collective-permute-start(f32[2,8,6,16,128]{4,3,2,1,0:T(8,128)S(1)} %shard_map.55.refs_0_.refs_1_.piece_ref), channel_id=1, source_target_pairs={{0,16},{16,0},{1,17},{17,1},{2,18},{18,2},{3,19},{19,3},{4,20},{20... | collective-permute-start | bytes 2359304 | tf_op jit(solution)/shard_map/ppermute | solution.py:391
  60.0 3.0 %shard_map.52 = (f32[1,8,6,16,128]{4,3,2,1,0:T(8,128)S(1)}, f32[1,8,6,16,128]{4,3,2,1,0:T(8,128)S(1)}) custom-call(f32[2,54,16,128]{3,2,1,0:T(8,128)S(1)} %get-tuple-element.17.table_ref, f32[2,36,16,128]{3,2,1,0:T(8,128)S(1)} %get-tuple-element.18.behind_ref, f32[1,8,6,16,128]{4,3,2,1,0:T(8,128)S(1)} %shard_map.49.refs_0_, ...), custom_call_target="tpu_custom_call" | custom-call | flops 32768000 | bytes 4620288 | tf_op jit(solution)/shard_map/pallas_call | solution.py:38
  64.2 1.6 %collective-permute-start.15 = (f32[1,8,6,16,128]{4,3,2,1,0:T(8,128)S(1)}, f32[1,8,6,16,128]{4,3,2,1,0:T(8,128)S(1)}, u32[]{:S(2)}, u32[]{:S(2)}) collective-permute-start(f32[1,8,6,16,128]{4,3,2,1,0:T(8,128)S(1)} %shard_map.54.refs_0_.piece_ref), channel_id=1, source_target_pairs={{0,16},{16,0},{1,17},{17,1},{2,18},{18,2},{3,19},{19,3},{4,20},{20... | collective-permute-start | bytes 1179656 | tf_op jit(solution)/shard_map/ppermute | solution.py:391
  65.7 3.1 %collective-permute-done.5.refs_1_ = f32[1,8,6,16,128]{4,3,2,1,0:T(8,128)S(1)} collective-permute-done((f32[1,8,6,16,128]{4,3,2,1,0:T(8,128)S(1)}, f32[1,8,6,16,128]{4,3,2,1,0:T(8,128)S(1)}, u32[]{:S(2)}, u32[]{:S(2)}) %collective-permute-start.5) | collective-permute-done | bytes 393248 | tf_op jit(solution)/shard_map/ppermute | solution.py:387
  69.1 1.6 %collective-permute-start.14 = (f32[1,8,6,16,128]{4,3,2,1,0:T(8,128)S(1)}, f32[1,8,6,16,128]{4,3,2,1,0:T(8,128)S(1)}, u32[]{:S(2)}, u32[]{:S(2)}) collective-permute-start(f32[1,8,6,16,128]{4,3,2,1,0:T(8,128)S(1)} %shard_map.53.refs_2_.top_ref.piece_ref), channel_id=1, source_target_pairs={{0,16},{16,0},{1,17},{17,1},{2,18},{18,2},{3,19},{19,3},{4,20},{20... | collective-permute-start | bytes 1179656 | tf_op jit(solution)/shard_map/ppermute | solution.py:391
  70.6 1.4 %shard_map.56.refs_2_ = f32[16,128]{1,0:T(8,128)S(1)} custom-call(f32[2,54,16,128]{3,2,1,0:T(8,128)S(1)} %get-tuple-element.17.table_ref, f32[2,8,6,16,128]{4,3,2,1,0:T(8,128)S(1)} %shard_map.55.refs_0_.refs_1_.piece_ref), custom_call_target="tpu_custom_call" | custom-call | flops 16384000 | bytes 1679360 | tf_op jit(solution)/shard_map/pallas_call | solution.py:38
  72.1 1.0 %shard_map.57.refs_3_ = f32[16,128]{1,0:T(8,128)S(1)} custom-call(f32[2,54,16,128]{3,2,1,0:T(8,128)S(1)} %get-tuple-element.17.table_ref, f32[1,8,6,16,128]{4,3,2,1,0:T(8,128)S(1)} %shard_map.54.refs_0_.piece_ref, f32[2,8,6,16,128]{4,3,2,1,0:T(8,128)S(1)} %shard_map.55.refs_0_.refs_1_.piece_ref, f32[16,128]{1,0:T(8,128)S(1)} %shard_map.56.refs_2_), custom_call_target="tpu_custom_call" | custom-call | flops 8192000 | bytes 2080768 | tf_op jit(solution)/shard_map/pallas_call | solution.py:38
  74.1 3.1 %collective-permute-done.8.above_ref = f32[1,8,6,16,128]{4,3,2,1,0:T(8,128)S(1)} collective-permute-done((f32[1,8,6,16,128]{4,3,2,1,0:T(8,128)S(1)}, f32[1,8,6,16,128]{4,3,2,1,0:T(8,128)S(1)}, u32[]{:S(2)}, u32[]{:S(2)}) %collective-permute-start.8) | collective-permute-done | bytes 393248 | tf_op jit(solution)/shard_map/ppermute | solution.py:387
  77.7 2.3 %collective-permute-start.11 = (f32[16,128]{1,0:T(8,128)S(1)}, f32[16,128]{1,0:T(8,128)S(1)}, u32[]{:S(2)}, u32[]{:S(2)}) collective-permute-start(f32[16,128]{1,0:T(8,128)S(1)} %shard_map.59), channel_id=1, source_target_pairs={{0,3},{1,2},{2,1},{3,0},{4,7},{5,6},{6,5},{7,4},{8,11},{9,10},{10,... | collective-permute-start | bytes 24584 | tf_op jit(solution)/shard_map/ppermute | solution.py:391
  80.0 2.3 %collective-permute-done.11 = f32[16,128]{1,0:T(8,128)S(1)} collective-permute-done((f32[16,128]{1,0:T(8,128)S(1)}, f32[16,128]{1,0:T(8,128)S(1)}, u32[]{:S(2)}, u32[]{:S(2)}) %collective-permute-start.11) | collective-permute-done | bytes 8224 | tf_op jit(solution)/shard_map/ppermute | solution.py:391
  83.6 2.3 %collective-permute-done.9 = f32[16,128]{1,0:T(8,128)S(1)} collective-permute-done((f32[16,128]{1,0:T(8,128)S(1)}, f32[16,128]{1,0:T(8,128)S(1)}, u32[]{:S(2)}, u32[]{:S(2)}) %collective-permute-start.9) | collective-permute-done | bytes 8224 | tf_op jit(solution)/shard_map/ppermute | solution.py:391
  85.9 1.8 %collective-permute-start.12 = (f32[16,128]{1,0:T(8,128)S(1)}, f32[16,128]{1,0:T(8,128)S(1)}, u32[]{:S(2)}, u32[]{:S(2)}) collective-permute-start(f32[16,128]{1,0:T(8,128)S(1)} %add_add_fusion), channel_id=1, source_target_pairs={{0,4},{1,5},{2,6},{3,7},{4,0},{5,1},{6,2},{7,3},{8,12},{9,13},{10,... | collective-permute-start | bytes 24584 | tf_op jit(solution)/shard_map/ppermute | solution.py:391
  87.7 2.7 %collective-permute-done.12 = f32[16,128]{1,0:T(8,128)S(1)} collective-permute-done((f32[16,128]{1,0:T(8,128)S(1)}, f32[16,128]{1,0:T(8,128)S(1)}, u32[]{:S(2)}, u32[]{:S(2)}) %collective-permute-start.12) | collective-permute-done | bytes 8224 | tf_op jit(solution)/shard_map/ppermute | solution.py:391
  90.5 1.5 %collective-permute-start.13 = (f32[16,128]{1,0:T(8,128)S(1)}, f32[16,128]{1,0:T(8,128)S(1)}, u32[]{:S(2)}, u32[]{:S(2)}) collective-permute-start(f32[16,128]{1,0:T(8,128)S(1)} %add.33.sum_ref.mine_ref), channel_id=1, source_target_pairs={{0,16},{16,0},{1,17},{17,1},{2,18},{18,2},{3,19},{19,3},{4,20},{20... | collective-permute-start | bytes 24584 | tf_op jit(solution)/shard_map/ppermute | solution.py:391
  95.2 1.8 %shard_map.66._ = f32[6144,128]{1,0:T(8,128)} custom-call(s32[3]{0:T(128)S(1)} %pad_add_fusion.pick_ref.slot_ref, f32[16,128]{1,0:T(8,128)S(1)} %add.33.sum_ref.mine_ref, f32[3072,128]{1,0:T(8,128)S(1)} %shard_map.65.field_ref), custom_call_target="tpu_custom_call" | custom-call | flops 1000000 | bytes 4726784 | tf_op jit(solution)/shard_map/pallas_call | solution.py:45
  97.0 2.5 %shard_map.67 = (f32[6144,128]{1,0:T(8,128)}, f32[2,2,2,16,16]{4,3,2,1,0:T(8,128)}) custom-call(s32[3]{0:T(128)S(1)} %pad_add_fusion.pick_ref.slot_ref, f32[16,128]{1,0:T(8,128)S(1)} %add.33.sum_ref.mine_ref, f32[16,128]{1,0:T(8,128)S(1)} %collective-permute-done.13.other_ref, f32[3072,128]{1,0:T(8,128)S(1)} %shard_map.62.field_ref, ...), custom_call_target="tpu_custom_call", output_to_operand_aliasing={{0}: (4, {})} | custom-call | flops 1000000 | bytes 7888896 | tf_op jit(solution)/shard_map/pallas_call | solution.py:45
  (33 shorter events, 9.1 us)
Async XLA Ops:
  1.7 11.1 %collective-permute-start = (f32[54,4,512]{2,1,0:T(4,128)S(1)}, f32[54,4,512]{2,1,0:T(4,128)S(1)}, u32[]{:S(2)}, u32[]{:S(2)}) collective-permute-start(f32[54,4,512]{2,1,0:T(4,128)S(1)} %dynamic-slice_bitcast_fusion), channel_id=1, source_target_pairs={{0,8},{8,0},{1,9},{9,1},{2,10},{10,2},{3,11},{11,3},{4,12},{12,4},... | collective-permute-start | bytes 1327112 | tf_op jit(solution)/shard_map/ppermute | solution.py:391
  4.5 20.5 %collective-permute-start.4 = (f32[1,8,6,16,128]{4,3,2,1,0:T(8,128)S(1)}, f32[1,8,6,16,128]{4,3,2,1,0:T(8,128)S(1)}, u32[]{:S(2)}, u32[]{:S(2)}) collective-permute-start(f32[1,8,6,16,128]{4,3,2,1,0:T(8,128)S(1)} %shard_map.43.refs_2_.refs_4_), channel_id=1, source_target_pairs={{0,1},{1,2},{2,3},{3,4},{4,5},{5,6},{6,7},{7,0},{8,9},{9,10},{10,1... | collective-permute-start | bytes 1179656 | tf_op jit(solution)/shard_map/ppermute | solution.py:387
  9.7 22.2 %collective-permute-start.2 = (f32[1,8,6,16,128]{4,3,2,1,0:T(8,128)S(1)}, f32[1,8,6,16,128]{4,3,2,1,0:T(8,128)S(1)}, u32[]{:S(2)}, u32[]{:S(2)}) collective-permute-start(f32[1,8,6,16,128]{4,3,2,1,0:T(8,128)S(1)} %get-tuple-element.16.refs_0_.refs_3_), channel_id=1, source_target_pairs={{0,7},{1,0},{2,1},{3,2},{4,3},{5,4},{6,5},{7,6},{8,15},{9,8},{10,9... | collective-permute-start | bytes 1179656 | tf_op jit(solution)/shard_map/ppermute | solution.py:387
  15.9 10.2 %collective-permute-start.1 = (f32[18,8,128]{2,1,0:T(8,128)S(1)}, f32[18,8,128]{2,1,0:T(8,128)S(1)}, u32[]{:S(2)}, u32[]{:S(2)}) collective-permute-start(f32[18,8,128]{2,1,0:T(8,128)S(1)} %get-tuple-element.15.refs_0_.links_ref), channel_id=1, source_target_pairs={{0,1},{1,2},{2,3},{3,4},{4,5},{5,6},{6,7},{7,0},{8,9},{9,10},{10,1... | collective-permute-start | bytes 221192 | tf_op jit(solution)/shard_map/ppermute | solution.py:387
  26.3 20.4 %collective-permute-start.6 = (f32[1,8,6,16,128]{4,3,2,1,0:T(8,128)S(1)}, f32[1,8,6,16,128]{4,3,2,1,0:T(8,128)S(1)}, u32[]{:S(2)}, u32[]{:S(2)}) collective-permute-start(f32[1,8,6,16,128]{4,3,2,1,0:T(8,128)S(1)} %shard_map.46.refs_0_.refs_3_), channel_id=1, source_target_pairs={{0,7},{1,0},{2,1},{3,2},{4,3},{5,4},{6,5},{7,6},{8,15},{9,8},{10,9... | collective-permute-start | bytes 1179656 | tf_op jit(solution)/shard_map/ppermute | solution.py:387
  32.1 18.1 %collective-permute-start.3 = (f32[1,8,6,16,128]{4,3,2,1,0:T(8,128)S(1)}, f32[1,8,6,16,128]{4,3,2,1,0:T(8,128)S(1)}, u32[]{:S(2)}, u32[]{:S(2)}) collective-permute-start(f32[1,8,6,16,128]{4,3,2,1,0:T(8,128)S(1)} %shard_map.45.refs_2_.refs_4_), channel_id=1, source_target_pairs={{0,1},{1,2},{2,3},{3,4},{4,5},{5,6},{6,7},{7,0},{8,9},{9,10},{10,1... | collective-permute-start | bytes 1179656 | tf_op jit(solution)/shard_map/ppermute | solution.py:387
  47.0 16.9 %collective-permute-start.7 = (f32[1,8,6,16,128]{4,3,2,1,0:T(8,128)S(1)}, f32[1,8,6,16,128]{4,3,2,1,0:T(8,128)S(1)}, u32[]{:S(2)}, u32[]{:S(2)}) collective-permute-start(f32[1,8,6,16,128]{4,3,2,1,0:T(8,128)S(1)} %shard_map.51.refs_2_), channel_id=1, source_target_pairs={{0,1},{1,2},{2,3},{3,4},{4,5},{5,6},{6,7},{7,0},{8,9},{9,10},{10,1... | collective-permute-start | bytes 1179656 | tf_op jit(solution)/shard_map/ppermute | solution.py:387
  50.5 18.3 %collective-permute-start.5 = (f32[1,8,6,16,128]{4,3,2,1,0:T(8,128)S(1)}, f32[1,8,6,16,128]{4,3,2,1,0:T(8,128)S(1)}, u32[]{:S(2)}, u32[]{:S(2)}) collective-permute-start(f32[1,8,6,16,128]{4,3,2,1,0:T(8,128)S(1)} %shard_map.49.refs_0_), channel_id=1, source_target_pairs={{0,7},{1,0},{2,1},{3,2},{4,3},{5,4},{6,5},{7,6},{8,15},{9,8},{10,9... | collective-permute-start | bytes 1179656 | tf_op jit(solution)/shard_map/ppermute | solution.py:387
  58.5 35.1 %collective-permute-start.16 = (f32[2,8,6,16,128]{4,3,2,1,0:T(8,128)S(1)}, f32[2,8,6,16,128]{4,3,2,1,0:T(8,128)S(1)}, u32[]{:S(2)}, u32[]{:S(2)}) collective-permute-start(f32[2,8,6,16,128]{4,3,2,1,0:T(8,128)S(1)} %shard_map.55.refs_0_.refs_1_.piece_ref), channel_id=1, source_target_pairs={{0,16},{16,0},{1,17},{17,1},{2,18},{18,2},{3,19},{19,3},{4,20},{20... | collective-permute-start | bytes 2359304 | tf_op jit(solution)/shard_map/ppermute | solution.py:391
  64.1 13.1 %collective-permute-start.8 = (f32[1,8,6,16,128]{4,3,2,1,0:T(8,128)S(1)}, f32[1,8,6,16,128]{4,3,2,1,0:T(8,128)S(1)}, u32[]{:S(2)}, u32[]{:S(2)}) collective-permute-start(f32[1,8,6,16,128]{4,3,2,1,0:T(8,128)S(1)} %shard_map.54.refs_0_.piece_ref), channel_id=1, source_target_pairs={{0,7},{1,0},{2,1},{3,2},{4,3},{5,4},{6,5},{7,6},{8,15},{9,8},{10,9... | collective-permute-start | bytes 1179656 | tf_op jit(solution)/shard_map/ppermute | solution.py:387
  64.2 30.2 %collective-permute-start.15 = (f32[1,8,6,16,128]{4,3,2,1,0:T(8,128)S(1)}, f32[1,8,6,16,128]{4,3,2,1,0:T(8,128)S(1)}, u32[]{:S(2)}, u32[]{:S(2)}) collective-permute-start(f32[1,8,6,16,128]{4,3,2,1,0:T(8,128)S(1)} %shard_map.54.refs_0_.piece_ref), channel_id=1, source_target_pairs={{0,16},{16,0},{1,17},{17,1},{2,18},{18,2},{3,19},{19,3},{4,20},{20... | collective-permute-start | bytes 1179656 | tf_op jit(solution)/shard_map/ppermute | solution.py:391
  69.1 25.7 %collective-permute-start.14 = (f32[1,8,6,16,128]{4,3,2,1,0:T(8,128)S(1)}, f32[1,8,6,16,128]{4,3,2,1,0:T(8,128)S(1)}, u32[]{:S(2)}, u32[]{:S(2)}) collective-permute-start(f32[1,8,6,16,128]{4,3,2,1,0:T(8,128)S(1)} %shard_map.53.refs_2_.top_ref.piece_ref), channel_id=1, source_target_pairs={{0,16},{16,0},{1,17},{17,1},{2,18},{18,2},{3,19},{19,3},{4,20},{20... | collective-permute-start | bytes 1179656 | tf_op jit(solution)/shard_map/ppermute | solution.py:391
  77.7 4.6 %collective-permute-start.11 = (f32[16,128]{1,0:T(8,128)S(1)}, f32[16,128]{1,0:T(8,128)S(1)}, u32[]{:S(2)}, u32[]{:S(2)}) collective-permute-start(f32[16,128]{1,0:T(8,128)S(1)} %shard_map.59), channel_id=1, source_target_pairs={{0,3},{1,2},{2,1},{3,0},{4,7},{5,6},{6,5},{7,4},{8,11},{9,10},{10,... | collective-permute-start | bytes 24584 | tf_op jit(solution)/shard_map/ppermute | solution.py:391
  80.0 3.7 %collective-permute-start.10 = (f32[16,128]{1,0:T(8,128)S(1)}, f32[16,128]{1,0:T(8,128)S(1)}, u32[]{:S(2)}, u32[]{:S(2)}) collective-permute-start(f32[16,128]{1,0:T(8,128)S(1)} %shard_map.59), channel_id=1, source_target_pairs={{0,2},{1,3},{2,0},{3,1},{4,6},{5,7},{6,4},{7,5},{8,10},{9,11},{10,... | collective-permute-start | bytes 24584 | tf_op jit(solution)/shard_map/ppermute | solution.py:391
  82.3 3.7 %collective-permute-start.9 = (f32[16,128]{1,0:T(8,128)S(1)}, f32[16,128]{1,0:T(8,128)S(1)}, u32[]{:S(2)}, u32[]{:S(2)}) collective-permute-start(f32[16,128]{1,0:T(8,128)S(1)} %shard_map.59), channel_id=1, source_target_pairs={{0,1},{1,0},{2,3},{3,2},{4,5},{5,4},{6,7},{7,6},{8,9},{9,8},{10,11... | collective-permute-start | bytes 24584 | tf_op jit(solution)/shard_map/ppermute | solution.py:391
  85.9 4.5 %collective-permute-start.12 = (f32[16,128]{1,0:T(8,128)S(1)}, f32[16,128]{1,0:T(8,128)S(1)}, u32[]{:S(2)}, u32[]{:S(2)}) collective-permute-start(f32[16,128]{1,0:T(8,128)S(1)} %add_add_fusion), channel_id=1, source_target_pairs={{0,4},{1,5},{2,6},{3,7},{4,0},{5,1},{6,2},{7,3},{8,12},{9,13},{10,... | collective-permute-start | bytes 24584 | tf_op jit(solution)/shard_map/ppermute | solution.py:391
  90.5 6.6 %collective-permute-start.13 = (f32[16,128]{1,0:T(8,128)S(1)}, f32[16,128]{1,0:T(8,128)S(1)}, u32[]{:S(2)}, u32[]{:S(2)}) collective-permute-start(f32[16,128]{1,0:T(8,128)S(1)} %add.33.sum_ref.mine_ref), channel_id=1, source_target_pairs={{0,16},{16,0},{1,17},{17,1},{2,18},{18,2},{3,19},{19,3},{4,20},{20... | collective-permute-start | bytes 24584 | tf_op jit(solution)/shard_map/ppermute | solution.py:391

commit v6 on v5

--- a/solution.py
+++ b/solution.py
@@ -103,7 +103,7 @@
                 out[z][c, q, first : first + count, :] = raw_ref[pl.ds(start, count, stride=stride), :]
         return 0
 
-    lax.fori_loop(0, rows, body, 0)
+    lax.fori_loop(0, rows, body, 0, unroll=True)
 
 
 def planes_kernel(depth, pieces, pick_ref, far_ref, *refs):
@@ -123,13 +123,24 @@
         take_planes(out, raw_ref, k * (vecs // parts), vecs // parts, rows, depth)
 
 
-def link_kernel(depth, half, pick_ref, far_ref, came_ref, table_ref, behind_ref, top_ref, sem):
+def link_kernel(depth, half, pick_ref, far_ref, came_ref, table_ref, top_ref, sem):
     core = pick_ref[1]
     copy = pltpu.make_async_copy(far_ref.at[pick_ref[2]], table_ref.at[core], sem)
     copy.start()
     table_ref[1 - core] = came_ref[...]
     copy.wait()
-    count = half * depth
+
+    def top(d, _):
+        for h in range(2):
+            top_ref[d, h * half : (h + 1) * half, :] = table_ref[h, 36 + d, pl.ds(depth - 1, half, stride=depth), :]
+        return 0
+
+    lax.fori_loop(0, 18, top, 0, unroll=6)
+
+
+def shift_kernel(depth, table_ref, behind_ref):
+    count = table_ref.shape[2]
+    half = count // depth
     lane = lane_index((count, LANES))
 
     def shift(d, _):
@@ -141,11 +152,9 @@
             if half > 1:
                 before = jnp.concatenate([before, here[: count - depth]], axis=0)
             behind_ref[h, 18 + d] = behind_y(here, before, lane)
-        for h in range(2):
-            top_ref[d, h * half : (h + 1) * half, :] = table_ref[h, 36 + d, pl.ds(depth - 1, half, stride=depth), :]
         return 0
 
-    lax.fori_loop(0, 18, shift, 0)
+    lax.fori_loop(0, 18, shift, 0, unroll=3)
 
 
 def multiply_into(total, field, link, adjoint):
@@ -330,7 +339,7 @@
                 out_ref[pl.ds(start, vecs, stride=stride), :] = piece_ref[k, c, q]
         return 0
 
-    lax.fori_loop(0, rows, body, 0)
+    lax.fori_loop(0, rows, body, 0, unroll=True)
 
 
 def scale_out(field_ref, far_ref, slot, inverse, chunks, scale_ref, ready_ref, sems):
@@ -347,7 +356,7 @@
             ready_ref[block, :] = field_ref[block, :] * scale_ref[pl.ds(vec, 1), :]
             return 0
 
-        lax.fori_loop(0, each, body, 0)
+        lax.fori_loop(0, each, body, 0, unroll=4)
         part = pl.ds(j * each * size, each * size)
         target = pl.ds(slot * (n * size) + j * each * size, each * size)
         copies.append(pltpu.make_async_copy(ready_ref.at[part], far_ref.at[target], sems.at[j]))
@@ -437,14 +446,17 @@
     if rest:
         for k, x in zip(rest, taken(rest)):
             start[k] = x
-    table, behind, top_links = call(
+    table, top_links = call(
         functools.partial(link_kernel, depth, half),
-        [shape_of(2, 54, half * depth, LANES), shape_of(2, 36, half * depth, LANES), shape_of(18, rows, LANES)],
+        [shape_of(2, 54, half * depth, LANES), shape_of(18, rows, LANES)],
         pltpu.with_memory_space_constraint(to_rows(links).reshape(-1, 54, half * depth, LANES), pltpu.HBM),
         to_rows(came).reshape(54, half * depth, LANES),
         pick=pick, far=(0,), scratch=[sem], ops=1e6,
     )
     prior = shifted(top_links, "sa", 1)
+    behind = call(
+        functools.partial(shift_kernel, depth), shape_of(2, 36, half * depth, LANES), table, ops=1e6
+    )
 
     def advance(cur, old):
         factor = -(1.0 if old is None else 2.0) / SCALE
@@ -515,7 +527,7 @@
             )
         return out
 
-    chunks = 4
+    chunks = 2
     assert vecs % chunks == 0
     scratch = [pltpu.VMEM((vecs, LANES), F32), pltpu.VMEM((many, LANES), F32), sem((chunks,))]
     ours, theirs = scattered(three), scattered(other)

time: 99.8 us -> 99.6 us (level)
  Pallas kernels: 39.3 us -> 38.1 us
  waiting for transfers between devices: 30.7 us -> 31.7 us
    pallas_call x5, Pallas kernels: 12.1 us -> 10.3 us  [call(): return pl.pallas_call(kernel, grid_spec=spec, **params)(pick, *args)]
    pallas_call x22 -> x23, Pallas kernels: 27.1 us -> 27.8 us  [call(): pl.pallas_call(kernel, in_specs=in_specs, out_specs=out_specs, scratch_sh...]
  transfers between devices with their start and end apart: 17 -> 17, of which waited for: 10 -> 10; matrix products, arithmetic and copies ran while one was open for 0% -> 0% of each run, Pallas kernels for 37% -> 36%
where the time goes in v6:
time: 99.6 us; the launch traced here: 99.4 us
  Pallas kernels  38.1 us (38%)
  waiting for transfers between devices  31.7 us (32%)
  starting transfers between devices  27.5 us (28%)
  local copies, waits for them, and re-layouts  1.05 us (1%)
    pallas_call x23, Pallas kernels, call(): pl.pallas_call(kernel, in_specs=in_specs, out_specs=out_specs, scratch_sh...  27.8 us
    ppermute x8, waiting for transfers between devices, shifted(): return lax.ppermute(x, axis, [(i, (i + by) % n) for i in range(n)])  23.5 us
    ppermute x8, starting transfers between devices, shifted(): return lax.ppermute(x, axis, [(i, (i + by) % n) for i in range(n)])  16.2 us
    ppermute x9, starting transfers between devices, flipped(): lax.ppermute(x, axis, [(i, i ^ bit) for i in range(lax.axis_size(axis))])  11.2 us
    pallas_call x5, Pallas kernels, call(): return pl.pallas_call(kernel, grid_spec=spec, **params)(pick, *args)  10.3 us
    ppermute x9, waiting for transfers between devices, flipped(): lax.ppermute(x, axis, [(i, i ^ bit) for i in range(lax.axis_size(axis))])  8.26 us
  transfers between devices with their start and end apart: 17, of which 10 were waited for; matrix products, arithmetic and copies ran while one was open for 0% of the time, Pallas kernels for 36%

profile of v6, /device:TPU:0, one launch (start us, length us, event | category | flops | bytes accessed | tf_op | source)
XLA Modules:
  0.0 99.4 jit_solution(5370927746279055437)
XLA Ops:
  0.6 1.0 %dynamic-slice_bitcast_fusion = f32[54,4,512]{2,1,0:T(4,128)S(1)} fusion(f32[4,54,4,512]{3,2,1,0:T(4,128)} %bitcast.30, s32[]{:T(128)S(6)} %select_n.12), kind=kLoop, calls=%fused_computation | loop fusion | bytes 884740 | tf_op jit(solution)/shard_map/jit(dynamic_index_in_dim)/squeeze | solution.py:444
  2.3 2.1 %shard_map.44.refs_2_.refs_4_ = f32[1,8,6,16,128]{4,3,2,1,0:T(8,128)S(1)} custom-call(s32[3]{0:T(128)S(1)} %pad_add_fusion.pick_ref.slot_ref, f32[6144,128]{1,0:T(8,128)} %bitcast.28), custom_call_target="tpu_custom_call" | custom-call | flops 100000 | bytes 3538944 | tf_op jit(solution)/shard_map/pallas_call | solution.py:45
  4.4 2.6 %collective-permute-start.4 = (f32[1,8,6,16,128]{4,3,2,1,0:T(8,128)S(1)}, f32[1,8,6,16,128]{4,3,2,1,0:T(8,128)S(1)}, u32[]{:S(2)}, u32[]{:S(2)}) collective-permute-start(f32[1,8,6,16,128]{4,3,2,1,0:T(8,128)S(1)} %shard_map.44.refs_2_.refs_4_), channel_id=1, source_target_pairs={{0,1},{1,2},{2,3},{3,4},{4,5},{5,6},{6,7},{7,0},{8,9},{9,10},{10,1... | collective-permute-start | bytes 1179656 | tf_op jit(solution)/shard_map/ppermute | solution.py:396
  7.0 2.4 %shard_map.42 = (f32[1,8,6,16,128]{4,3,2,1,0:T(8,128)S(1)}, f32[2,8,6,16,128]{4,3,2,1,0:T(8,128)S(1)}) custom-call(s32[3]{0:T(128)S(1)} %pad_add_fusion.pick_ref.slot_ref, f32[6144,128]{1,0:T(8,128)} %bitcast.29), custom_call_target="tpu_custom_call" | custom-call | flops 100000 | bytes 4325376 | tf_op jit(solution)/shard_map/pallas_call | solution.py:45
  9.4 3.1 %collective-permute-start.2 = (f32[1,8,6,16,128]{4,3,2,1,0:T(8,128)S(1)}, f32[1,8,6,16,128]{4,3,2,1,0:T(8,128)S(1)}, u32[]{:S(2)}, u32[]{:S(2)}) collective-permute-start(f32[1,8,6,16,128]{4,3,2,1,0:T(8,128)S(1)} %get-tuple-element.15.refs_0_.refs_3_), channel_id=1, source_target_pairs={{0,7},{1,0},{2,1},{3,2},{4,3},{5,4},{6,5},{7,6},{8,15},{9,8},{10,9... | collective-permute-start | bytes 1179656 | tf_op jit(solution)/shard_map/ppermute | solution.py:396
  12.5 1.6 %shard_map.41 = (f32[2,54,16,128]{3,2,1,0:T(8,128)S(1)}, f32[18,8,128]{2,1,0:T(8,128)S(1)}) custom-call(s32[3]{0:T(128)S(1)} %pad_add_fusion.pick_ref.slot_ref, f32[4,54,16,128]{3,2,1,0:T(8,128)} %bitcast.31, f32[54,16,128]{2,1,0:T(8,128)S(1)} %bitcast.26), custom_call_target="tpu_custom_call" | custom-call | flops 1000000 | bytes 3170304 | tf_op jit(solution)/shard_map/pallas_call | solution.py:45
  14.8 3.0 %shard_map.45 = (f32[1,8,6,16,128]{4,3,2,1,0:T(8,128)S(1)}, f32[1,8,6,16,128]{4,3,2,1,0:T(8,128)S(1)}) custom-call(f32[2,54,16,128]{3,2,1,0:T(8,128)S(1)} %get-tuple-element.16.table_ref, f32[2,36,16,128]{3,2,1,0:T(8,128)S(1)} %shard_map.43.behind_ref, f32[1,8,6,16,128]{4,3,2,1,0:T(8,128)S(1)} %get-tuple-element.15.refs_0_.refs_3_, ...), custom_call_target="tpu_custom_call" | custom-call | flops 32768000 | bytes 3833856 | tf_op jit(solution)/shard_map/pallas_call | solution.py:38
  17.8 7.1 %collective-permute-done.4.refs_1_ = f32[1,8,6,16,128]{4,3,2,1,0:T(8,128)S(1)} collective-permute-done((f32[1,8,6,16,128]{4,3,2,1,0:T(8,128)S(1)}, f32[1,8,6,16,128]{4,3,2,1,0:T(8,128)S(1)}, u32[]{:S(2)}, u32[]{:S(2)}) %collective-permute-start.4) | collective-permute-done | bytes 393248 | tf_op jit(solution)/shard_map/ppermute | solution.py:396
  24.9 1.1 %collective-permute-done.1.refs_0_ = f32[18,8,128]{2,1,0:T(8,128)S(1)} collective-permute-done((f32[18,8,128]{2,1,0:T(8,128)S(1)}, f32[18,8,128]{2,1,0:T(8,128)S(1)}, u32[]{:S(2)}, u32[]{:S(2)}) %collective-permute-start.1) | collective-permute-done | bytes 73760 | tf_op jit(solution)/shard_map/ppermute | solution.py:396
  26.2 5.6 %collective-permute-start.6 = (f32[1,8,6,16,128]{4,3,2,1,0:T(8,128)S(1)}, f32[1,8,6,16,128]{4,3,2,1,0:T(8,128)S(1)}, u32[]{:S(2)}, u32[]{:S(2)}) collective-permute-start(f32[1,8,6,16,128]{4,3,2,1,0:T(8,128)S(1)} %shard_map.47.refs_0_.refs_3_), channel_id=1, source_target_pairs={{0,7},{1,0},{2,1},{3,2},{4,3},{5,4},{6,5},{7,6},{8,15},{9,8},{10,9... | collective-permute-start | bytes 1179656 | tf_op jit(solution)/shard_map/ppermute | solution.py:396
  32.1 3.2 %shard_map.48.refs_1_.refs_3_ = f32[2,8,6,16,128]{4,3,2,1,0:T(8,128)S(1)} custom-call(f32[2,54,16,128]{3,2,1,0:T(8,128)S(1)} %get-tuple-element.16.table_ref, f32[2,36,16,128]{3,2,1,0:T(8,128)S(1)} %shard_map.43.behind_ref, f32[1,8,6,16,128]{4,3,2,1,0:T(8,128)S(1)} %get-tuple-element.15.refs_0_.refs_3_, ...), custom_call_target="tpu_custom_call" | custom-call | flops 32768000 | bytes 3833856 | tf_op jit(solution)/shard_map/pallas_call | solution.py:38
  35.3 3.0 %shard_map.49 = (f32[1,8,6,16,128]{4,3,2,1,0:T(8,128)S(1)}, f32[1,8,6,16,128]{4,3,2,1,0:T(8,128)S(1)}) custom-call(f32[2,54,16,128]{3,2,1,0:T(8,128)S(1)} %get-tuple-element.16.table_ref, f32[2,36,16,128]{3,2,1,0:T(8,128)S(1)} %shard_map.43.behind_ref, f32[1,8,6,16,128]{4,3,2,1,0:T(8,128)S(1)} %shard_map.47.refs_0_.refs_3_, ...), custom_call_target="tpu_custom_call" | custom-call | flops 32768000 | bytes 4620288 | tf_op jit(solution)/shard_map/pallas_call | solution.py:38
  38.3 8.3 %collective-permute-done.6.refs_1_ = f32[1,8,6,16,128]{4,3,2,1,0:T(8,128)S(1)} collective-permute-done((f32[1,8,6,16,128]{4,3,2,1,0:T(8,128)S(1)}, f32[1,8,6,16,128]{4,3,2,1,0:T(8,128)S(1)}, u32[]{:S(2)}, u32[]{:S(2)}) %collective-permute-start.6) | collective-permute-done | bytes 393248 | tf_op jit(solution)/shard_map/ppermute | solution.py:396
  46.9 3.2 %shard_map.51.refs_1_ = f32[2,8,6,16,128]{4,3,2,1,0:T(8,128)S(1)} custom-call(f32[2,54,16,128]{3,2,1,0:T(8,128)S(1)} %get-tuple-element.16.table_ref, f32[2,36,16,128]{3,2,1,0:T(8,128)S(1)} %shard_map.43.behind_ref, f32[1,8,6,16,128]{4,3,2,1,0:T(8,128)S(1)} %shard_map.47.refs_0_.refs_3_, f32[2,8,6,16,128]{4,3,2,1,0:T(8,128)S(1)} %shard_map.48.refs_1_.refs_3_, ...), custom_call_target="tpu_custom_call" | custom-call | flops 32768000 | bytes 4620288 | tf_op jit(solution)/shard_map/pallas_call | solution.py:38
  50.4 4.8 %collective-permute-start.5 = (f32[1,8,6,16,128]{4,3,2,1,0:T(8,128)S(1)}, f32[1,8,6,16,128]{4,3,2,1,0:T(8,128)S(1)}, u32[]{:S(2)}, u32[]{:S(2)}) collective-permute-start(f32[1,8,6,16,128]{4,3,2,1,0:T(8,128)S(1)} %shard_map.50.refs_0_), channel_id=1, source_target_pairs={{0,7},{1,0},{2,1},{3,2},{4,3},{5,4},{6,5},{7,6},{8,15},{9,8},{10,9... | collective-permute-start | bytes 1179656 | tf_op jit(solution)/shard_map/ppermute | solution.py:396
  55.2 3.2 %shard_map.56.refs_0_.refs_1_.piece_ref = f32[2,8,6,16,128]{4,3,2,1,0:T(8,128)S(1)} custom-call(f32[2,54,16,128]{3,2,1,0:T(8,128)S(1)} %get-tuple-element.16.table_ref, f32[2,36,16,128]{3,2,1,0:T(8,128)S(1)} %shard_map.43.behind_ref, f32[1,8,6,16,128]{4,3,2,1,0:T(8,128)S(1)} %shard_map.50.refs_0_, f32[2,8,6,16,128]{4,3,2,1,0:T(8,128)S(1)} %shard_map.51.refs_1_, ...), custom_call_target="tpu_custom_call" | custom-call | flops 32768000 | bytes 4620288 | tf_op jit(solution)/shard_map/pallas_call | solution.py:38
  58.4 1.6 %collective-permute-start.16 = (f32[2,8,6,16,128]{4,3,2,1,0:T(8,128)S(1)}, f32[2,8,6,16,128]{4,3,2,1,0:T(8,128)S(1)}, u32[]{:S(2)}, u32[]{:S(2)}) collective-permute-start(f32[2,8,6,16,128]{4,3,2,1,0:T(8,128)S(1)} %shard_map.56.refs_0_.refs_1_.piece_ref), channel_id=1, source_target_pairs={{0,16},{16,0},{1,17},{17,1},{2,18},{18,2},{3,19},{19,3},{4,20},{20... | collective-permute-start | bytes 2359304 | tf_op jit(solution)/shard_map/ppermute | solution.py:400
  59.9 3.0 %shard_map.53 = (f32[1,8,6,16,128]{4,3,2,1,0:T(8,128)S(1)}, f32[1,8,6,16,128]{4,3,2,1,0:T(8,128)S(1)}) custom-call(f32[2,54,16,128]{3,2,1,0:T(8,128)S(1)} %get-tuple-element.16.table_ref, f32[2,36,16,128]{3,2,1,0:T(8,128)S(1)} %shard_map.43.behind_ref, f32[1,8,6,16,128]{4,3,2,1,0:T(8,128)S(1)} %shard_map.50.refs_0_, ...), custom_call_target="tpu_custom_call" | custom-call | flops 32768000 | bytes 4620288 | tf_op jit(solution)/shard_map/pallas_call | solution.py:38
  64.0 1.6 %collective-permute-start.15 = (f32[1,8,6,16,128]{4,3,2,1,0:T(8,128)S(1)}, f32[1,8,6,16,128]{4,3,2,1,0:T(8,128)S(1)}, u32[]{:S(2)}, u32[]{:S(2)}) collective-permute-start(f32[1,8,6,16,128]{4,3,2,1,0:T(8,128)S(1)} %shard_map.55.refs_0_.piece_ref), channel_id=1, source_target_pairs={{0,16},{16,0},{1,17},{17,1},{2,18},{18,2},{3,19},{19,3},{4,20},{20... | collective-permute-start | bytes 1179656 | tf_op jit(solution)/shard_map/ppermute | solution.py:400
  65.6 3.1 %collective-permute-done.5.refs_1_ = f32[1,8,6,16,128]{4,3,2,1,0:T(8,128)S(1)} collective-permute-done((f32[1,8,6,16,128]{4,3,2,1,0:T(8,128)S(1)}, f32[1,8,6,16,128]{4,3,2,1,0:T(8,128)S(1)}, u32[]{:S(2)}, u32[]{:S(2)}) %collective-permute-start.5) | collective-permute-done | bytes 393248 | tf_op jit(solution)/shard_map/ppermute | solution.py:396
  69.0 1.6 %collective-permute-start.14 = (f32[1,8,6,16,128]{4,3,2,1,0:T(8,128)S(1)}, f32[1,8,6,16,128]{4,3,2,1,0:T(8,128)S(1)}, u32[]{:S(2)}, u32[]{:S(2)}) collective-permute-start(f32[1,8,6,16,128]{4,3,2,1,0:T(8,128)S(1)} %shard_map.54.refs_2_.top_ref.piece_ref), channel_id=1, source_target_pairs={{0,16},{16,0},{1,17},{17,1},{2,18},{18,2},{3,19},{19,3},{4,20},{20... | collective-permute-start | bytes 1179656 | tf_op jit(solution)/shard_map/ppermute | solution.py:400
  70.5 1.4 %shard_map.57.refs_2_ = f32[16,128]{1,0:T(8,128)S(1)} custom-call(f32[2,54,16,128]{3,2,1,0:T(8,128)S(1)} %get-tuple-element.16.table_ref, f32[2,8,6,16,128]{4,3,2,1,0:T(8,128)S(1)} %shard_map.56.refs_0_.refs_1_.piece_ref), custom_call_target="tpu_custom_call" | custom-call | flops 16384000 | bytes 1679360 | tf_op jit(solution)/shard_map/pallas_call | solution.py:38
  71.9 1.0 %shard_map.58.refs_3_ = f32[16,128]{1,0:T(8,128)S(1)} custom-call(f32[2,54,16,128]{3,2,1,0:T(8,128)S(1)} %get-tuple-element.16.table_ref, f32[1,8,6,16,128]{4,3,2,1,0:T(8,128)S(1)} %shard_map.55.refs_0_.piece_ref, f32[2,8,6,16,128]{4,3,2,1,0:T(8,128)S(1)} %shard_map.56.refs_0_.refs_1_.piece_ref, f32[16,128]{1,0:T(8,128)S(1)} %shard_map.57.refs_2_), custom_call_target="tpu_custom_call" | custom-call | flops 8192000 | bytes 2080768 | tf_op jit(solution)/shard_map/pallas_call | solution.py:38
  74.0 3.1 %collective-permute-done.8.above_ref = f32[1,8,6,16,128]{4,3,2,1,0:T(8,128)S(1)} collective-permute-done((f32[1,8,6,16,128]{4,3,2,1,0:T(8,128)S(1)}, f32[1,8,6,16,128]{4,3,2,1,0:T(8,128)S(1)}, u32[]{:S(2)}, u32[]{:S(2)}) %collective-permute-start.8) | collective-permute-done | bytes 393248 | tf_op jit(solution)/shard_map/ppermute | solution.py:396
  77.6 2.3 %collective-permute-start.11 = (f32[16,128]{1,0:T(8,128)S(1)}, f32[16,128]{1,0:T(8,128)S(1)}, u32[]{:S(2)}, u32[]{:S(2)}) collective-permute-start(f32[16,128]{1,0:T(8,128)S(1)} %shard_map.60), channel_id=1, source_target_pairs={{0,3},{1,2},{2,1},{3,0},{4,7},{5,6},{6,5},{7,4},{8,11},{9,10},{10,... | collective-permute-start | bytes 24584 | tf_op jit(solution)/shard_map/ppermute | solution.py:400
  79.9 2.3 %collective-permute-done.11 = f32[16,128]{1,0:T(8,128)S(1)} collective-permute-done((f32[16,128]{1,0:T(8,128)S(1)}, f32[16,128]{1,0:T(8,128)S(1)}, u32[]{:S(2)}, u32[]{:S(2)}) %collective-permute-start.11) | collective-permute-done | bytes 8224 | tf_op jit(solution)/shard_map/ppermute | solution.py:400
  83.5 2.3 %collective-permute-done.9 = f32[16,128]{1,0:T(8,128)S(1)} collective-permute-done((f32[16,128]{1,0:T(8,128)S(1)}, f32[16,128]{1,0:T(8,128)S(1)}, u32[]{:S(2)}, u32[]{:S(2)}) %collective-permute-start.9) | collective-permute-done | bytes 8224 | tf_op jit(solution)/shard_map/ppermute | solution.py:400
  85.8 1.8 %collective-permute-start.12 = (f32[16,128]{1,0:T(8,128)S(1)}, f32[16,128]{1,0:T(8,128)S(1)}, u32[]{:S(2)}, u32[]{:S(2)}) collective-permute-start(f32[16,128]{1,0:T(8,128)S(1)} %add_add_fusion), channel_id=1, source_target_pairs={{0,4},{1,5},{2,6},{3,7},{4,0},{5,1},{6,2},{7,3},{8,12},{9,13},{10,... | collective-permute-start | bytes 24584 | tf_op jit(solution)/shard_map/ppermute | solution.py:400
  87.6 2.7 %collective-permute-done.12 = f32[16,128]{1,0:T(8,128)S(1)} collective-permute-done((f32[16,128]{1,0:T(8,128)S(1)}, f32[16,128]{1,0:T(8,128)S(1)}, u32[]{:S(2)}, u32[]{:S(2)}) %collective-permute-start.12) | collective-permute-done | bytes 8224 | tf_op jit(solution)/shard_map/ppermute | solution.py:400
  90.4 1.5 %collective-permute-start.13 = (f32[16,128]{1,0:T(8,128)S(1)}, f32[16,128]{1,0:T(8,128)S(1)}, u32[]{:S(2)}, u32[]{:S(2)}) collective-permute-start(f32[16,128]{1,0:T(8,128)S(1)} %add.33.sum_ref.mine_ref), channel_id=1, source_target_pairs={{0,16},{16,0},{1,17},{17,1},{2,18},{18,2},{3,19},{19,3},{4,20},{20... | collective-permute-start | bytes 24584 | tf_op jit(solution)/shard_map/ppermute | solution.py:400
  95.1 1.8 %shard_map.67._ = f32[6144,128]{1,0:T(8,128)} custom-call(s32[3]{0:T(128)S(1)} %pad_add_fusion.pick_ref.slot_ref, f32[16,128]{1,0:T(8,128)S(1)} %add.33.sum_ref.mine_ref, f32[3072,128]{1,0:T(8,128)S(1)} %shard_map.66.field_ref), custom_call_target="tpu_custom_call" | custom-call | flops 1000000 | bytes 4726784 | tf_op jit(solution)/shard_map/pallas_call | solution.py:45
  96.9 2.5 %shard_map.68 = (f32[6144,128]{1,0:T(8,128)}, f32[2,2,2,16,16]{4,3,2,1,0:T(8,128)}) custom-call(s32[3]{0:T(128)S(1)} %pad_add_fusion.pick_ref.slot_ref, f32[16,128]{1,0:T(8,128)S(1)} %add.33.sum_ref.mine_ref, f32[16,128]{1,0:T(8,128)S(1)} %collective-permute-done.13.other_ref, f32[3072,128]{1,0:T(8,128)S(1)} %shard_map.63.field_ref, ...), custom_call_target="tpu_custom_call", output_to_operand_aliasing={{0}: (4, {})} | custom-call | flops 1000000 | bytes 7888896 | tf_op jit(solution)/shard_map/pallas_call | solution.py:45
  (34 shorter events, 9.7 us)
Async XLA Ops:
  1.7 10.8 %collective-permute-start = (f32[54,4,512]{2,1,0:T(4,128)S(1)}, f32[54,4,512]{2,1,0:T(4,128)S(1)}, u32[]{:S(2)}, u32[]{:S(2)}) collective-permute-start(f32[54,4,512]{2,1,0:T(4,128)S(1)} %dynamic-slice_bitcast_fusion), channel_id=1, source_target_pairs={{0,8},{8,0},{1,9},{9,1},{2,10},{10,2},{3,11},{11,3},{4,12},{12,4},... | collective-permute-start | bytes 1327112 | tf_op jit(solution)/shard_map/ppermute | solution.py:400
  4.4 20.5 %collective-permute-start.4 = (f32[1,8,6,16,128]{4,3,2,1,0:T(8,128)S(1)}, f32[1,8,6,16,128]{4,3,2,1,0:T(8,128)S(1)}, u32[]{:S(2)}, u32[]{:S(2)}) collective-permute-start(f32[1,8,6,16,128]{4,3,2,1,0:T(8,128)S(1)} %shard_map.44.refs_2_.refs_4_), channel_id=1, source_target_pairs={{0,1},{1,2},{2,3},{3,4},{4,5},{5,6},{6,7},{7,0},{8,9},{9,10},{10,1... | collective-permute-start | bytes 1179656 | tf_op jit(solution)/shard_map/ppermute | solution.py:396
  9.4 22.4 %collective-permute-start.2 = (f32[1,8,6,16,128]{4,3,2,1,0:T(8,128)S(1)}, f32[1,8,6,16,128]{4,3,2,1,0:T(8,128)S(1)}, u32[]{:S(2)}, u32[]{:S(2)}) collective-permute-start(f32[1,8,6,16,128]{4,3,2,1,0:T(8,128)S(1)} %get-tuple-element.15.refs_0_.refs_3_), channel_id=1, source_target_pairs={{0,7},{1,0},{2,1},{3,2},{4,3},{5,4},{6,5},{7,6},{8,15},{9,8},{10,9... | collective-permute-start | bytes 1179656 | tf_op jit(solution)/shard_map/ppermute | solution.py:396
  14.1 11.9 %collective-permute-start.1 = (f32[18,8,128]{2,1,0:T(8,128)S(1)}, f32[18,8,128]{2,1,0:T(8,128)S(1)}, u32[]{:S(2)}, u32[]{:S(2)}) collective-permute-start(f32[18,8,128]{2,1,0:T(8,128)S(1)} %get-tuple-element.14.refs_0_.links_ref), channel_id=1, source_target_pairs={{0,1},{1,2},{2,3},{3,4},{4,5},{5,6},{6,7},{7,0},{8,9},{9,10},{10,1... | collective-permute-start | bytes 221192 | tf_op jit(solution)/shard_map/ppermute | solution.py:396
  26.2 20.4 %collective-permute-start.6 = (f32[1,8,6,16,128]{4,3,2,1,0:T(8,128)S(1)}, f32[1,8,6,16,128]{4,3,2,1,0:T(8,128)S(1)}, u32[]{:S(2)}, u32[]{:S(2)}) collective-permute-start(f32[1,8,6,16,128]{4,3,2,1,0:T(8,128)S(1)} %shard_map.47.refs_0_.refs_3_), channel_id=1, source_target_pairs={{0,7},{1,0},{2,1},{3,2},{4,3},{5,4},{6,5},{7,6},{8,15},{9,8},{10,9... | collective-permute-start | bytes 1179656 | tf_op jit(solution)/shard_map/ppermute | solution.py:396
  32.0 18.1 %collective-permute-start.3 = (f32[1,8,6,16,128]{4,3,2,1,0:T(8,128)S(1)}, f32[1,8,6,16,128]{4,3,2,1,0:T(8,128)S(1)}, u32[]{:S(2)}, u32[]{:S(2)}) collective-permute-start(f32[1,8,6,16,128]{4,3,2,1,0:T(8,128)S(1)} %shard_map.46.refs_2_.refs_4_), channel_id=1, source_target_pairs={{0,1},{1,2},{2,3},{3,4},{4,5},{5,6},{6,7},{7,0},{8,9},{9,10},{10,1... | collective-permute-start | bytes 1179656 | tf_op jit(solution)/shard_map/ppermute | solution.py:396
  46.9 16.9 %collective-permute-start.7 = (f32[1,8,6,16,128]{4,3,2,1,0:T(8,128)S(1)}, f32[1,8,6,16,128]{4,3,2,1,0:T(8,128)S(1)}, u32[]{:S(2)}, u32[]{:S(2)}) collective-permute-start(f32[1,8,6,16,128]{4,3,2,1,0:T(8,128)S(1)} %shard_map.52.refs_2_), channel_id=1, source_target_pairs={{0,1},{1,2},{2,3},{3,4},{4,5},{5,6},{6,7},{7,0},{8,9},{9,10},{10,1... | collective-permute-start | bytes 1179656 | tf_op jit(solution)/shard_map/ppermute | solution.py:396
  50.4 18.3 %collective-permute-start.5 = (f32[1,8,6,16,128]{4,3,2,1,0:T(8,128)S(1)}, f32[1,8,6,16,128]{4,3,2,1,0:T(8,128)S(1)}, u32[]{:S(2)}, u32[]{:S(2)}) collective-permute-start(f32[1,8,6,16,128]{4,3,2,1,0:T(8,128)S(1)} %shard_map.50.refs_0_), channel_id=1, source_target_pairs={{0,7},{1,0},{2,1},{3,2},{4,3},{5,4},{6,5},{7,6},{8,15},{9,8},{10,9... | collective-permute-start | bytes 1179656 | tf_op jit(solution)/shard_map/ppermute | solution.py:396
  58.4 35.1 %collective-permute-start.16 = (f32[2,8,6,16,128]{4,3,2,1,0:T(8,128)S(1)}, f32[2,8,6,16,128]{4,3,2,1,0:T(8,128)S(1)}, u32[]{:S(2)}, u32[]{:S(2)}) collective-permute-start(f32[2,8,6,16,128]{4,3,2,1,0:T(8,128)S(1)} %shard_map.56.refs_0_.refs_1_.piece_ref), channel_id=1, source_target_pairs={{0,16},{16,0},{1,17},{17,1},{2,18},{18,2},{3,19},{19,3},{4,20},{20... | collective-permute-start | bytes 2359304 | tf_op jit(solution)/shard_map/ppermute | solution.py:400
  64.0 13.1 %collective-permute-start.8 = (f32[1,8,6,16,128]{4,3,2,1,0:T(8,128)S(1)}, f32[1,8,6,16,128]{4,3,2,1,0:T(8,128)S(1)}, u32[]{:S(2)}, u32[]{:S(2)}) collective-permute-start(f32[1,8,6,16,128]{4,3,2,1,0:T(8,128)S(1)} %shard_map.55.refs_0_.piece_ref), channel_id=1, source_target_pairs={{0,7},{1,0},{2,1},{3,2},{4,3},{5,4},{6,5},{7,6},{8,15},{9,8},{10,9... | collective-permute-start | bytes 1179656 | tf_op jit(solution)/shard_map/ppermute | solution.py:396
  64.0 30.2 %collective-permute-start.15 = (f32[1,8,6,16,128]{4,3,2,1,0:T(8,128)S(1)}, f32[1,8,6,16,128]{4,3,2,1,0:T(8,128)S(1)}, u32[]{:S(2)}, u32[]{:S(2)}) collective-permute-start(f32[1,8,6,16,128]{4,3,2,1,0:T(8,128)S(1)} %shard_map.55.refs_0_.piece_ref), channel_id=1, source_target_pairs={{0,16},{16,0},{1,17},{17,1},{2,18},{18,2},{3,19},{19,3},{4,20},{20... | collective-permute-start | bytes 1179656 | tf_op jit(solution)/shard_map/ppermute | solution.py:400
  69.0 25.7 %collective-permute-start.14 = (f32[1,8,6,16,128]{4,3,2,1,0:T(8,128)S(1)}, f32[1,8,6,16,128]{4,3,2,1,0:T(8,128)S(1)}, u32[]{:S(2)}, u32[]{:S(2)}) collective-permute-start(f32[1,8,6,16,128]{4,3,2,1,0:T(8,128)S(1)} %shard_map.54.refs_2_.top_ref.piece_ref), channel_id=1, source_target_pairs={{0,16},{16,0},{1,17},{17,1},{2,18},{18,2},{3,19},{19,3},{4,20},{20... | collective-permute-start | bytes 1179656 | tf_op jit(solution)/shard_map/ppermute | solution.py:400
  77.6 4.6 %collective-permute-start.11 = (f32[16,128]{1,0:T(8,128)S(1)}, f32[16,128]{1,0:T(8,128)S(1)}, u32[]{:S(2)}, u32[]{:S(2)}) collective-permute-start(f32[16,128]{1,0:T(8,128)S(1)} %shard_map.60), channel_id=1, source_target_pairs={{0,3},{1,2},{2,1},{3,0},{4,7},{5,6},{6,5},{7,4},{8,11},{9,10},{10,... | collective-permute-start | bytes 24584 | tf_op jit(solution)/shard_map/ppermute | solution.py:400
  79.9 3.7 %collective-permute-start.10 = (f32[16,128]{1,0:T(8,128)S(1)}, f32[16,128]{1,0:T(8,128)S(1)}, u32[]{:S(2)}, u32[]{:S(2)}) collective-permute-start(f32[16,128]{1,0:T(8,128)S(1)} %shard_map.60), channel_id=1, source_target_pairs={{0,2},{1,3},{2,0},{3,1},{4,6},{5,7},{6,4},{7,5},{8,10},{9,11},{10,... | collective-permute-start | bytes 24584 | tf_op jit(solution)/shard_map/ppermute | solution.py:400
  82.1 3.7 %collective-permute-start.9 = (f32[16,128]{1,0:T(8,128)S(1)}, f32[16,128]{1,0:T(8,128)S(1)}, u32[]{:S(2)}, u32[]{:S(2)}) collective-permute-start(f32[16,128]{1,0:T(8,128)S(1)} %shard_map.60), channel_id=1, source_target_pairs={{0,1},{1,0},{2,3},{3,2},{4,5},{5,4},{6,7},{7,6},{8,9},{9,8},{10,11... | collective-permute-start | bytes 24584 | tf_op jit(solution)/shard_map/ppermute | solution.py:400
  85.8 4.5 %collective-permute-start.12 = (f32[16,128]{1,0:T(8,128)S(1)}, f32[16,128]{1,0:T(8,128)S(1)}, u32[]{:S(2)}, u32[]{:S(2)}) collective-permute-start(f32[16,128]{1,0:T(8,128)S(1)} %add_add_fusion), channel_id=1, source_target_pairs={{0,4},{1,5},{2,6},{3,7},{4,0},{5,1},{6,2},{7,3},{8,12},{9,13},{10,... | collective-permute-start | bytes 24584 | tf_op jit(solution)/shard_map/ppermute | solution.py:400
  90.4 6.5 %collective-permute-start.13 = (f32[16,128]{1,0:T(8,128)S(1)}, f32[16,128]{1,0:T(8,128)S(1)}, u32[]{:S(2)}, u32[]{:S(2)}) collective-permute-start(f32[16,128]{1,0:T(8,128)S(1)} %add.33.sum_ref.mine_ref), channel_id=1, source_target_pairs={{0,16},{16,0},{1,17},{17,1},{2,18},{18,2},{3,19},{19,3},{4,20},{20... | collective-permute-start | bytes 24584 | tf_op jit(solution)/shard_map/ppermute | solution.py:400
